TPU v7x, 256 devices: a whole 4x4x8 slice. The times are simulated.
256 devices in a mesh: proj: 16 (over x, y_lo, core), tile: 16 (over z, y_hi).
Axes of the slice: x: 4, y: 4 (y_hi: 2, y_lo: 2; y = y_hi * 2 + y_lo), z: 8, core: 2. Of those that a mesh axis runs over, the one named last changes fastest.
Arguments:
- raw: bfloat16 [32, 1024, 4096], P(None, 'proj', 'tile'), may hold values from -6 to 6
- row_weights: bfloat16 [32, 16, 128, 256], P('proj', 'tile'), may hold values from 0 to 1
- col_weights: bfloat16 [32, 16, 1024, 2048], P('proj', 'tile'), may hold values from 0 to 1
- band_start: int32 [32, 16], replicated, may hold values from 0 to 768
- band_length: int32 [32, 16], replicated, may hold values from 64 to 256, as said below
- col_offset: int32 [32, 16], P('proj', 'tile'), may hold values from 0 to 24
Outputs:
- slab: float32 [128, 32768], P('proj', 'tile')
Inputs may be any that keep to these rules, and one draw needn't show every extreme that they name: `band_length`: in every projection some tile uses exactly 256 rows.
All inputs are finite; a program needn't handle non-finite values.
Results may differ from a plain program's by a relative error of at most 0.008.
Values may be sent and summed in bfloat16 or wider, within the bound.
No kernel may reach another device: no remote copies, remote signals or barrier semaphores. Data moves between devices by JAX's collectives and lax.ppermute only.
A program may use at most 128 MiB of HBM per device.

v0:
```python
import math

import jax
import jax.numpy as jnp
from jax import lax
from jax.sharding import PartitionSpec as P

LMAX = 256


def with_halo(array, sides, width):
    for axis, dim in sides:
        count, length = (lax.axis_size(axis), array.shape[dim])
        up = [(i, (i + 1) % count) for i in range(count - 1)]
        down = [(j, i) for i, j in up]
        last = lax.slice_in_dim(array, length - width, length, axis=dim)
        leading = lax.slice_in_dim(array, 0, width, axis=dim)
        before = lax.ppermute(last, axis, up)
        after = lax.ppermute(leading, axis, down)
        array = jnp.concatenate([before, array, after], axis=dim)
    return array


def tap_tiles():
    rows_a = jnp.arange(128, dtype=jnp.int32)[:, None]
    cols_c = jnp.arange(128, dtype=jnp.int32)[None, :]
    tiles = []
    for shift in (-1, 0, 1):
        offset = cols_c - rows_a - 128 * shift
        offset_f = offset.astype(jnp.float32)
        odd_mask = offset % 2 != 0
        safe_sq = jnp.where(offset == 0, 1.0, offset_f * offset_f)
        value = jnp.where(
            offset == 0, 0.25, jnp.where(odd_mask, -1.0 / (math.pi * math.pi * safe_sq), 0.0)
        )
        value = jnp.where((offset >= -128) & (offset <= 127), value, 0.0)
        tiles.append(value.astype(jnp.bfloat16))
    return tiles


def mask_rows(rows, length):
    mask = jnp.arange(rows.shape[0], dtype=jnp.int32)[:, None] < length
    return jnp.where(mask, rows, jnp.zeros_like(rows))


def take_band(proj_data, start, length):
    return mask_rows(lax.dynamic_slice_in_dim(proj_data, start, LMAX, 0), length)


def body(raw, row_weights, col_weights, band_start, band_length, col_offset):
    proj_count, rows_dev, cols_dev = raw.shape
    n_proj = lax.axis_size("proj")
    n_tile = lax.axis_size("tile")
    proj_me = lax.axis_index("proj")
    tile_me = lax.axis_index("tile")
    total_rows = rows_dev * n_proj
    total_cols = cols_dev * n_tile
    dist = 2.0 * total_cols
    row_ids = (proj_me * rows_dev + jnp.arange(rows_dev, dtype=jnp.int32)).astype(jnp.float32)
    col_ids = (tile_me * cols_dev + jnp.arange(cols_dev, dtype=jnp.int32)).astype(jnp.float32)
    vcoord = row_ids + 0.5 - total_rows / 2.0
    ucoord = col_ids + 0.5 - total_cols / 2.0
    weight = dist / jnp.sqrt(dist * dist + ucoord[None, :] ** 2 + vcoord[:, None] ** 2)
    weighted = (raw.astype(jnp.float32) * weight[None]).astype(jnp.bfloat16)
    padded = with_halo(weighted, (("tile", 2),), 128)
    tiles = tap_tiles()
    blocks = cols_dev // 128
    total = jnp.zeros((proj_count, rows_dev, blocks, 128), jnp.float32)
    for index in range(3):
        piece = padded[:, :, 128 * index : 128 * index + cols_dev].reshape(
            proj_count, rows_dev, blocks, 128
        )
        total = total + jnp.einsum(
            "prna,ab->prnb", piece, tiles[index], preferred_element_type=jnp.float32
        )
    filtered = total.reshape(proj_count, rows_dev, cols_dev).astype(jnp.bfloat16)
    owned = lax.all_to_all(filtered, "proj", split_axis=0, concat_axis=1, tiled=True)
    local_count = owned.shape[0]
    first_proj = proj_me * local_count
    starts = lax.dynamic_slice_in_dim(band_start, first_proj, local_count, 0)
    lengths = lax.dynamic_slice_in_dim(band_length, first_proj, local_count, 0)
    win_cols = col_weights.shape[2]
    my_offsets = col_offset[:, 0]

    def cut_window(band_rows, offset):
        return lax.dynamic_slice_in_dim(band_rows, offset * 128, win_cols, 1)

    full = lax.all_gather(owned, "tile", axis=2, tiled=True)
    my_starts = lax.dynamic_slice_in_dim(starts, tile_me, 1, 1)[:, 0]
    my_lengths = lax.dynamic_slice_in_dim(lengths, tile_me, 1, 1)[:, 0]
    bands = jax.vmap(take_band)(full, my_starts, my_lengths)
    windows = jax.vmap(cut_window)(bands, my_offsets)
    acc = jnp.zeros((row_weights.shape[2], col_weights.shape[3]), jnp.float32)
    for local in range(local_count):
        spread = jnp.dot(
            windows[local], col_weights[local, 0], preferred_element_type=jnp.float32
        ).astype(jnp.bfloat16)
        acc = acc + jnp.dot(row_weights[local, 0], spread, preferred_element_type=jnp.float32)
    return lax.psum_scatter(acc, "proj", scatter_dimension=0, tiled=True)


def solution(mesh):
    return jax.shard_map(
        body,
        mesh=mesh,
        in_specs=(
            P(None, "proj", "tile"),
            P("proj", "tile", None, None),
            P("proj", "tile", None, None),
            P(),
            P(),
            P("proj", "tile"),
        ),
        out_specs=P("proj", "tile"),
        check_vma=False,
    )
```

profile of v0, /device:TPU:1, one launch (start us, length us, event | category | flops | bytes accessed | tf_op | source)
XLA Modules:
  0.0 395.8 jit_solution(17064370836072021085)
XLA Ops:
  6.6 0.1 rsqrt_multiply_fusion
  6.7 1.6 multiply_convert_fusion
  8.2 0.3 fusion.134
  8.5 5.7 %collective-permute-start = (bf16[32,64,128]{2,1,0:T(8,128)(2,1)S(1)}, bf16[32,64,128]{2,1,0:T(8,128)(2,1)S(1)}, u32[]{:S(2)}, u32[]{:S(2)}) collective-permute-start(bf16[32,64,128]{2,1,0:T(8,128)(2,1)S(1)} %get-tuple-element.44), channel_id=1, source_target_pairs={{0,1},{1,2},{2,3},{3,4},{4,5},{5,6},{6,7},{7,8},{8,9},{9,10},{10,1... | collective-permute-start | bytes 1572872 | tf_op jit(solution)/shard_map/ppermute | solution.py:18
  14.2 1.3 collective-permute-start.1
  15.5 0.5 fusion.21
  16.0 20.0 %collective-permute-done = bf16[32,64,128]{2,1,0:T(8,128)(2,1)S(1)} collective-permute-done((bf16[32,64,128]{2,1,0:T(8,128)(2,1)S(1)}, bf16[32,64,128]{2,1,0:T(8,128)(2,1)S(1)}, u32[]{:S(2)}, u32[]{:S(2)}) %collective-permute-start) | collective-permute-done | bytes 524320 | tf_op jit(solution)/shard_map/ppermute | solution.py:18
  36.0 0.4 fusion.27
  36.4 0.4 fusion.24
  36.8 0.5 fusion.16
  37.4 0.2 copy.57
  37.6 21.0 %all_to_all.18 = bf16[32,64,256]{2,1,0:T(8,128)(2,1)S(1)} all-to-all(bf16[32,64,256]{2,1,0:T(8,128)(2,1)S(1)} %bitcast.91), channel_id=1, replica_groups=mesh['proj'=16,'tile'=16] {'proj'}, dimensions={0} | all-to-all | bytes 2097152 | tf_op jit(solution)/shard_map/all_to_all | solution.py:77
  58.6 1.0 copy.30
  59.7 0.8 dynamic_slice.12
  60.5 0.1 copy.39
  60.6 0.1 copy.32
  60.9 238.0 %all-gather.2.cloned.1.call-done = bf16[2,1024,4096]{2,1,0:T(8,128)(2,1)} async-done(((bf16[2,1024,256]{2,1,0:T(8,128)(2,1)}), bf16[2,1024,4096]{2,1,0:T(8,128)(2,1)}) %all-gather.2.cloned.1.call-update) | async-done | bytes 16777232 | tf_op jit(solution)/shard_map/all_gather | solution.py:88
  299.0 10.6 %while.4 = (s32[]{:T(128)}, bf16[2,1024,4096]{2,1,0:T(8,128)(2,1)}, s32[2,3]{1,0:T(2,128)S(1)}, bf16[2,256,4096]{2,1,0:T(8,128)(2,1)}) while((s32[]{:T(128)}, bf16[2,1024,4096]{2,1,0:T(8,128)(2,1)}, s32[2,3]{1,0:T(2,128)S(1)}, bf16[2,256,4096]{2,1,0:T(8,128)(2,1)}) %tuple.45), condition=%wide.while_cond.clone, body=%wide.while_body.sunk.clone | while | flops 2 | bytes 4195937 | solution.py:47
  299.0 0.6 fusion.142
  299.6 4.7 %dynamic-slice_dynamic-update-slice_fusion.6 = bf16[2,256,4096]{2,1,0:T(8,128)(2,1)} fusion(bf16[2,256,4096]{2,1,0:T(8,128)(2,1)} %get-tuple-element.138, s32[]{:T(128)} %get-tuple-element.135, bf16[2,1024,4096]{2,1,0:T(8,128)(2,1)} %get-tuple-element.140, s32[]{:T(128)} %bitcast.86, s32[]{:T(128)} %bitcast.87), kind=kLoop, calls=%fused_computation.clone.1.clone | loop fusion | bytes 4195840 | tf_op jit(solution)/shard_map/vmap()/gather
  304.3 0.6 fusion.142
  304.9 4.7 %dynamic-slice_dynamic-update-slice_fusion.6 = bf16[2,256,4096]{2,1,0:T(8,128)(2,1)} fusion(bf16[2,256,4096]{2,1,0:T(8,128)(2,1)} %get-tuple-element.138, s32[]{:T(128)} %get-tuple-element.135, bf16[2,1024,4096]{2,1,0:T(8,128)(2,1)} %get-tuple-element.140, s32[]{:T(128)} %bitcast.86, s32[]{:T(128)} %bitcast.87), kind=kLoop, calls=%fused_computation.clone.1.clone | loop fusion | bytes 4195840 | tf_op jit(solution)/shard_map/vmap()/gather
  309.6 4.5 %broadcast_select_fusion = bf16[2,256,4096]{2,1,0:T(8,128)(2,1)} fusion(bf16[2,256,4096]{2,1,0:T(8,128)(2,1)} %get-tuple-element.12, pred[2,256]{1,0:T(4,128)(4,1)S(1)} %iota_compare_fusion), kind=kLoop, calls=%fused_computation.10 | loop fusion | flops 2097152 | bytes 8389120 | tf_op jit(solution)/shard_map/vmap(jit(_where))/select_n | solution.py:43
  314.1 6.4 %while.5 = (s32[]{:T(128)}, bf16[2,256,4096]{2,1,0:T(8,128)(2,1)}, s32[2,3]{1,0:T(2,128)S(1)}, bf16[2,256,1024]{2,1,0:T(8,128)(2,1)S(1)}) while((s32[]{:T(128)}, bf16[2,256,4096]{2,1,0:T(8,128)(2,1)}, s32[2,3]{1,0:T(2,128)S(1)}, bf16[2,256,1024]{2,1,0:T(8,128)(2,1)S(1)}) %tuple.48), condition=%wide.while_cond.1.clone, body=%wide.while_body.1.sunk.clone | while | flops 2 | bytes 1048685 | solution.py:86
  314.1 0.6 fusion.143
  314.7 2.5 dynamic-slice_dynamic-update-slice_fusion.7
  317.3 0.6 fusion.143
  317.9 2.5 dynamic-slice_dynamic-update-slice_fusion.7
  320.5 3.8 fusion.14
  324.2 3.8 fusion.12
  328.0 1.3 copy.37
  329.4 59.6 %reduce-scatter.4.cloned.1.call-done = f32[8,2048]{1,0:T(8,128)} async-done(((f32[128,2048]{1,0:T(8,128)}), f32[8,2048]{1,0:T(8,128)}) %reduce-scatter.4.cloned.1.call-update) | async-done | bytes 65552 | tf_op jit(solution)/shard_map/reduce_scatter | solution.py:99
  (26 shorter events, 0.4 us)
Async XLA Ops:
  6.5 54.2 %copy-start = (s32[32,16]{0,1:T(8,128)S(1)}, s32[32,16]{0,1:T(8,128)}, u32[]{:S(2)}) copy-start(s32[32,16]{0,1:T(8,128)} %param.10) | copy-start | bytes 6148
  6.5 9.0 %copy-start.1 = (bf16[32,64,256]{2,1,0:T(8,128)(2,1)S(1)}, bf16[32,64,256]{2,1,0:T(8,128)(2,1)}, u32[]{:S(2)}) copy-start(bf16[32,64,256]{2,1,0:T(8,128)(2,1)} %param.6) | copy-start | bytes 3145732
  6.5 292.4 %all-gather.2.cloned.1.call-start = ((), (), s32[]{:S(2)}) async-start(), calls=%async_computation.2 | async-start | bytes 17825792 | tf_op jit(solution)/shard_map/all_gather | solution.py:88
  8.5 27.5 %collective-permute-start = (bf16[32,64,128]{2,1,0:T(8,128)(2,1)S(1)}, bf16[32,64,128]{2,1,0:T(8,128)(2,1)S(1)}, u32[]{:S(2)}, u32[]{:S(2)}) collective-permute-start(bf16[32,64,128]{2,1,0:T(8,128)(2,1)S(1)} %get-tuple-element.44), channel_id=1, source_target_pairs={{0,1},{1,2},{2,3},{3,4},{4,5},{5,6},{6,7},{7,8},{8,9},{9,10},{10,1... | collective-permute-start | bytes 1572872 | tf_op jit(solution)/shard_map/ppermute | solution.py:18
  14.2 21.8 %collective-permute-start.1 = (bf16[32,64,128]{2,1,0:T(8,128)(2,1)S(1)}, bf16[32,64,128]{2,1,0:T(8,128)(2,1)S(1)}, u32[]{:S(2)}, u32[]{:S(2)}) collective-permute-start(bf16[32,64,128]{2,1,0:T(8,128)(2,1)S(1)} %get-tuple-element.43), channel_id=1, source_target_pairs={{1,0},{2,1},{3,2},{4,3},{5,4},{6,5},{7,6},{8,7},{9,8},{10,9},{11,1... | collective-permute-start | bytes 1572872 | tf_op jit(solution)/shard_map/ppermute | solution.py:19
  37.4 23.2 %copy-start.3 = (s32[2,1]{0,1:T(1,128)S(1)}, s32[2,1]{0,1:T(1,128)}, u32[]{:S(2)}) copy-start(s32[2,1]{0,1:T(1,128)} %param.11) | copy-start | bytes 28
  59.7 329.3 %reduce-scatter.4.cloned.1.call-start = ((), (), s32[]{:S(2)}) async-start(), calls=%async_computation.3 | async-start | bytes 1114112 | tf_op jit(solution)/shard_map/reduce_scatter | solution.py:99
  314.1 6.4 %copy-start.2 = (bf16[2,1,128,256]{3,2,1,0:T(8,128)(2,1)S(1)}, bf16[2,1,128,256]{3,2,1,0:T(8,128)(2,1)}, u32[]{:S(2)}) copy-start(bf16[2,1,128,256]{3,2,1,0:T(8,128)(2,1)} %param.7) | copy-start | bytes 393220
Sparse Core Ops, SparseCore 0:
  59.8 239.1 all-gather.1
  329.5 59.4 reduce-scatter.3
where the time goes:
time: 399 us; the launch traced here: 396 us
  waiting for transfers between devices  318 us (80%)
  blocking collectives  21 us (5%)
  local copies, waits for them, and re-layouts  20.8 us (5%)
  between operations  13.6 us (3%)
  matrix products  9 us (2%)
  starting transfers between devices  7.02 us (2%)
  other arithmetic  6.68 us (2%)
    all_gather x1, waiting for transfers between devices, body(): full = lax.all_gather(owned, 'tile', axis=2, tiled=True)  238 us
    reduce_scatter x1, waiting for transfers between devices, body(): return lax.psum_scatter(acc, 'proj', scatter_dimension=0, tiled=True)  59.6 us
    all_to_all x1, blocking collectives, body(): lax.all_to_all(filtered, 'proj', split_axis=0, concat_axis=1, tiled=True)  21 us
    ppermute x1, waiting for transfers between devices, with_halo(): before = lax.ppermute(last, axis, up)  20 us
    gather x12, local copies, waits for them, and re-layouts  16.9 us
  transfers between devices with their start and end apart: 4, of which 3 were waited for; matrix products, arithmetic and copies ran while one was open for 0% of the time, Pallas kernels for 0%

commit v1 on v0

v1 whole, which is shorter than its diff:
```python
import math

import jax
import jax.numpy as jnp
from jax import lax
from jax.experimental import pallas as pl
from jax.experimental.pallas import tpu as pltpu
from jax.sharding import PartitionSpec as P

LMAX = 256
TAP_REACH = 128
BF16 = jnp.bfloat16


def tap_matrix(width):
    rows = jnp.arange(width + 2 * TAP_REACH, dtype=jnp.int32)[:, None]
    cols = jnp.arange(width, dtype=jnp.int32)[None, :]
    offset = cols - rows + TAP_REACH
    offset_f = offset.astype(jnp.float32)
    safe_sq = jnp.where(offset == 0, 1.0, offset_f * offset_f)
    value = jnp.where(
        offset == 0, 0.25, jnp.where(offset % 2 != 0, -1.0 / (math.pi * math.pi * safe_sq), 0.0)
    )
    value = jnp.where((offset >= -TAP_REACH) & (offset < TAP_REACH), value, 0.0)
    return value.astype(BF16)


def gather_offsets(offsets, me_count):
    flat = offsets.reshape(-1)
    bit = 1
    while bit < me_count:
        flat = jnp.concatenate(
            [flat, lax.ppermute(flat, "tile", [(i, i ^ bit) for i in range(me_count)])]
        )
        bit *= 2
    return flat


def filter_cut(info_ref, recv_ref, weight_ref, taps_ref, out_ref, padded, filtered):
    groups, n_src, chunk, width = recv_ref.shape
    n_tile, rows_out, win = out_ref.shape
    periods = rows_out // chunk
    rows = groups * chunk
    total = n_src * width
    me = info_ref[2 * n_tile]
    row_class = info_ref[2 * n_tile + 1]
    zero = jnp.zeros((rows, TAP_REACH), BF16)
    padded[:, :TAP_REACH] = zero
    padded[:, TAP_REACH + total :] = zero
    for src in range(n_src):
        piece = recv_ref[:, src].astype(jnp.float32)
        piece = piece * weight_ref[:, :, width * src : width * (src + 1)]
        lo = TAP_REACH + width * src
        padded[:, lo : lo + width] = piece.reshape(rows, width).astype(BF16)
    for src in range(n_src):
        lo = width * src
        block = jnp.dot(
            padded[:, lo : lo + width + 2 * TAP_REACH],
            taps_ref[...],
            preferred_element_type=jnp.float32,
        )
        filtered[:, :, lo : lo + width] = block.reshape(groups, chunk, width)
    row_ids = lax.broadcasted_iota(jnp.int32, (chunk, win), 0)
    span = chunk * 8

    @pl.loop(0, n_tile)
    def _(k):
        start = info_ref[k]
        col = pl.multiple_of(info_ref[n_tile + k] * 128, 128)
        tile = jnp.bitwise_xor(me, k)
        parts = []
        for m in range(periods):
            delta = start - (span * m + chunk * row_class) + LMAX
            low = lax.shift_right_logical(delta, 8)
            rest = jnp.bitwise_and(delta, LMAX - 1)
            first = jnp.clip(low - 1, 0, groups // periods - 1) * periods + m
            second = jnp.clip(low, 0, groups // periods - 1) * periods + m
            parts.append(
                jnp.where(
                    row_ids >= rest,
                    filtered[first, :, pl.ds(col, win)],
                    filtered[second, :, pl.ds(col, win)],
                )
            )
        out_ref[tile] = jnp.concatenate(parts, axis=0).astype(BF16)


def spread_sum(recv_ref, rowm_ref, colw_ref, out_ref):
    n_src, rows, win = recv_ref.shape
    local = rowm_ref.shape[0]
    per = n_src // local
    acc = None
    for q in range(local):
        window = recv_ref[per * q : per * (q + 1)].reshape(per * rows, win)
        spread = jnp.dot(window, colw_ref[q, 0], preferred_element_type=jnp.float32).astype(BF16)
        term = jnp.dot(rowm_ref[q], spread, preferred_element_type=jnp.float32)
        acc = term if acc is None else acc + term
    out_ref[...] = acc.reshape(out_ref.shape).astype(BF16)


def body(raw, row_weights, col_weights, band_start, band_length, col_offset):
    proj_count, rows_dev, cols_dev = raw.shape
    n_proj = lax.axis_size("proj")
    n_tile = lax.axis_size("tile")
    proj_me = lax.axis_index("proj")
    tile_me = lax.axis_index("tile")
    local = proj_count // n_proj
    total_rows = rows_dev * n_proj
    total_cols = cols_dev * n_tile
    classes = n_tile // local
    chunk = rows_dev // classes
    slices, vox = row_weights.shape[2], col_weights.shape[3]
    win = col_weights.shape[2]
    rows_out = LMAX // classes

    recv = lax.all_to_all(
        raw.reshape(n_proj * n_tile, chunk, cols_dev),
        ("proj", "tile"),
        split_axis=0,
        concat_axis=0,
        tiled=True,
    ).reshape(n_proj, n_tile, chunk, cols_dev)

    offsets = gather_offsets(col_offset, n_tile).reshape(n_tile, local)
    which = tile_me // classes
    row_class = tile_me % classes
    first_proj = proj_me * local
    starts_all = lax.dynamic_slice(band_start, (first_proj, 0), (local, n_tile))
    lengths_all = lax.dynamic_slice(band_length, (first_proj, 0), (local, n_tile))
    order = jnp.bitwise_xor(jnp.arange(n_tile, dtype=jnp.int32), tile_me)
    my_starts = jnp.take(lax.dynamic_index_in_dim(starts_all, which, 0, False), order)
    my_offsets = lax.dynamic_index_in_dim(offsets, which, 1, False)
    info = jnp.concatenate(
        [my_starts, my_offsets, tile_me.reshape(1), row_class.reshape(1)]
    ).astype(jnp.int32)

    dist = 2.0 * total_cols
    row_ids = (
        rows_dev * jnp.arange(n_proj, dtype=jnp.int32)[:, None]
        + chunk * row_class
        + jnp.arange(chunk, dtype=jnp.int32)[None, :]
    ).astype(jnp.float32)
    vcoord = row_ids + 0.5 - total_rows / 2.0
    ucoord = jnp.arange(total_cols, dtype=jnp.int32).astype(jnp.float32) + 0.5 - total_cols / 2.0
    weight = dist / jnp.sqrt(dist * dist + ucoord[None, None, :] ** 2 + vcoord[:, :, None] ** 2)

    cut = pl.pallas_call(
        filter_cut,
        out_shape=jax.ShapeDtypeStruct((n_tile, rows_out, win), BF16),
        in_specs=[pl.BlockSpec(memory_space=pltpu.SMEM)]
        + [pl.BlockSpec(memory_space=pltpu.VMEM)] * 3,
        out_specs=pl.BlockSpec(memory_space=pltpu.VMEM),
        scratch_shapes=[
            pltpu.VMEM((n_proj * chunk, total_cols + 2 * TAP_REACH), BF16),
            pltpu.VMEM((n_proj, chunk, total_cols), jnp.float32),
        ],
        compiler_params=pltpu.CompilerParams(vmem_limit_bytes=24 << 20),
    )(info, recv, weight, tap_matrix(cols_dev))

    windows = lax.all_to_all(cut, "tile", split_axis=0, concat_axis=0, tiled=True)

    place = jnp.arange(LMAX, dtype=jnp.int32)
    row_mod = place // rows_out * chunk + place % rows_out // chunk * rows_dev + place % chunk
    my_start = lax.dynamic_slice_in_dim(starts_all, tile_me, 1, 1)
    my_length = lax.dynamic_slice_in_dim(lengths_all, tile_me, 1, 1)
    band_row = jnp.bitwise_and(row_mod[None, :] - my_start, LMAX - 1)
    pick = (place[None, :, None] == band_row[:, None, :]) & (band_row < my_length)[:, None, :]
    row_moved = jnp.einsum(
        "qsi,qik->qsk", row_weights[:, 0], pick.astype(BF16), preferred_element_type=jnp.float32
    ).astype(BF16)

    step = 512
    part = pl.pallas_call(
        spread_sum,
        out_shape=jax.ShapeDtypeStruct((n_proj, slices // n_proj, vox), BF16),
        grid=(vox // step,),
        in_specs=[
            pl.BlockSpec((n_tile, rows_out, win), lambda n: (0, 0, 0)),
            pl.BlockSpec((local, slices, LMAX), lambda n: (0, 0, 0)),
            pl.BlockSpec((local, 1, win, step), lambda n: (0, 0, 0, n)),
        ],
        out_specs=pl.BlockSpec((n_proj, slices // n_proj, step), lambda n: (0, 0, n)),
        compiler_params=pltpu.CompilerParams(vmem_limit_bytes=24 << 20),
    )(windows, row_moved, col_weights)

    terms = lax.all_to_all(part, "proj", split_axis=0, concat_axis=0, tiled=True)
    return jnp.sum(terms.astype(jnp.float32), axis=0)


def solution(mesh):
    return jax.shard_map(
        body,
        mesh=mesh,
        in_specs=(
            P(None, "proj", "tile"),
            P("proj", "tile", None, None),
            P("proj", "tile", None, None),
            P(),
            P(),
            P("proj", "tile"),
        ),
        out_specs=P("proj", "tile"),
        check_vma=False,
    )
```

time: 399 us -> 118 us (0.30)
  waiting for transfers between devices: 318 us -> 46.5 us
  starting transfers between devices: 7.02 us -> 33.5 us
  between operations: 13.6 us -> 0.2 us
  local copies, waits for them, and re-layouts: 20.8 us -> 8.77 us
  matrix products: 9 us -> 0.36 us
  Pallas kernels: 0 us -> 6.2 us
    all_gather x1 -> x0, waiting for transfers between devices: 238 us -> none  [body(): full = lax.all_gather(owned, 'tile', axis=2, tiled=True)]
    reduce_scatter x1 -> x0, waiting for transfers between devices: 59.6 us -> none  [body(): return lax.psum_scatter(acc, 'proj', scatter_dimension=0, tiled=True)]
    all_to_all x0 -> x2, waiting for transfers between devices: none -> 24 us  [the longest x1 24 us: body(): lax.all_to_all(cut, 'tile', split_axis=0, concat_axis=0, tiled=True)]
    all_to_all x0 -> x2, starting transfers between devices: none -> 21.8 us  [the longest x1 13 us: body(): lax.all_to_all(raw.reshape(n_proj * n_tile, chunk, cols_dev), ('proj', 't...]
    gather x12 -> x1, local copies, waits for them, and re-layouts: 16.9 us -> 0.66 us  [body(): jnp.take(lax.dynamic_index_in_dim(starts_all, which, 0, False), order)]
    dot_general x5 -> x1, matrix products: 9 us -> 0.36 us  [body(): jnp.einsum('qsi,qik->qsk', row_weights[:, 0], pick.astype(BF16), preferre...]
    pallas_call x0 -> x2, Pallas kernels: none -> 6.2 us  [the longest x1 4.39 us: body(): pl.pallas_call(spread_sum, out_shape=jax.ShapeDtypeStruct((n_proj, slices...]
    ppermute x2 -> x4, starting transfers between devices: 6.97 us -> 11.7 us  [gather_offsets(): lax.ppermute(flat, 'tile', [(i, i ^ bit) for i in range(me_count)])]
  transfers between devices with their start and end apart: 4 -> 6, of which waited for: 3 -> 4; matrix products, arithmetic and copies ran while one was open for 0% -> 6% of each run, Pallas kernels for 0% -> 0%
where the time goes in v1:
time: 118 us
  waiting for transfers between devices  46.5 us (39%)
  starting transfers between devices  33.5 us (28%)
  blocking collectives  19 us (16%)
  local copies, waits for them, and re-layouts  8.77 us (7%)
  Pallas kernels  6.2 us (5%)
  other arithmetic  3.17 us (3%)
    all_to_all x1, waiting for transfers between devices, body(): lax.all_to_all(cut, 'tile', split_axis=0, concat_axis=0, tiled=True)  24 us
    ppermute x4, waiting for transfers between devices, gather_offsets(): lax.ppermute(flat, 'tile', [(i, i ^ bit) for i in range(me_count)])  22.5 us
    all_to_all x1, blocking collectives, body(): lax.all_to_all(part, 'proj', split_axis=0, concat_axis=0, tiled=True)  19 us
    all_to_all x1, starting transfers between devices, body(): lax.all_to_all(raw.reshape(n_proj * n_tile, chunk, cols_dev), ('proj', 't...  13 us
    ppermute x4, starting transfers between devices, gather_offsets(): lax.ppermute(flat, 'tile', [(i, i ^ bit) for i in range(me_count)])  11.7 us
    all_to_all x1, starting transfers between devices, body(): lax.all_to_all(cut, 'tile', split_axis=0, concat_axis=0, tiled=True)  8.8 us
    unnamed x14, local copies, waits for them, and re-layouts  4.84 us
    pallas_call x1, Pallas kernels, body(): pl.pallas_call(spread_sum, out_shape=jax.ShapeDtypeStruct((n_proj, slices...  4.39 us
  transfers between devices with their start and end apart: 6, of which 4 were waited for; matrix products, arithmetic and copies ran while one was open for 6% of the time, Pallas kernels for 0%

profile of v1, /device:TPU:1, one launch (start us, length us, event | category | flops | bytes accessed | tf_op | source)
XLA Modules:
  0.0 117.8 jit_solution(10279230398605065379)
XLA Ops:
  0.0 3.7 %collective-permute-start = (s32[2]{0:T(128)}, s32[2]{0:T(128)S(1)}, u32[]{:S(2)}, u32[]{:S(2)}) collective-permute-start(s32[2]{0:T(128)} %bitcast.18), channel_id=1, source_target_pairs={{0,1},{1,0},{2,3},{3,2},{4,5},{5,4},{6,7},{7,6},{8,9},{9,8},{10,11... | collective-permute-start | bytes 32 | tf_op jit(solution)/shard_map/ppermute | solution.py:33
  3.8 13.0 %all-to-all-start = ((bf16[256,8,256]{2,1,0:T(8,128)(2,1)}), bf16[256,8,256]{2,1,0:T(8,128)(2,1)S(1)}, u32[]{:S(2)}, u32[]{:S(2)}) async-start(bf16[256,8,256]{2,1,0:T(8,128)(2,1)} %bitcast.17), calls=%async_computation | async-start | bytes 2097152 | tf_op jit(solution)/shard_map/all_to_all | solution.py:116
  16.8 0.2 dynamic-slice_reduce_fusion.1
  17.0 0.7 gather_fusion
  17.7 0.5 and_select_fusion.4
  18.3 0.5 rsqrt_multiply_fusion.weight_ref
  18.8 0.1 pad_add_fusion
  18.9 1.5 %collective-permute-start.1 = (s32[4]{0:T(128)S(1)}, s32[4]{0:T(128)S(1)}, u32[]{:S(2)}, u32[]{:S(2)}) collective-permute-start(s32[4]{0:T(128)S(1)} %pad_add_fusion), channel_id=1, source_target_pairs={{0,2},{1,3},{2,0},{3,1},{4,6},{5,7},{6,4},{7,5},{8,10},{9,11},{10,... | collective-permute-start | bytes 56 | tf_op jit(solution)/shard_map/ppermute | solution.py:33
  20.4 19.0 %collective-permute-done.1 = s32[4]{0:T(128)S(1)} collective-permute-done((s32[4]{0:T(128)S(1)}, s32[4]{0:T(128)S(1)}, u32[]{:S(2)}, u32[]{:S(2)}) %collective-permute-start.1) | collective-permute-done | bytes 48 | tf_op jit(solution)/shard_map/ppermute | solution.py:33
  39.5 0.7 collective-permute-start.2
  40.2 2.9 %collective-permute-done.2 = s32[8]{0:T(128)S(1)} collective-permute-done((s32[8]{0:T(128)S(1)}, s32[8]{0:T(128)S(1)}, u32[]{:S(2)}, u32[]{:S(2)}) %collective-permute-start.2) | collective-permute-done | bytes 64 | tf_op jit(solution)/shard_map/ppermute | solution.py:33
  43.1 0.1 pad_add_fusion.2
  43.2 0.5 copy-done.6
  43.7 5.8 %collective-permute-start.3 = (s32[16]{0:T(128)S(1)}, s32[16]{0:T(128)}, u32[]{:S(2)}, u32[]{:S(2)}) collective-permute-start(s32[16]{0:T(128)S(1)} %pad_add_fusion.2), channel_id=1, source_target_pairs={{0,8},{1,9},{2,10},{3,11},{4,12},{5,13},{6,14},{7,15},{8,0},{9,1},... | collective-permute-start | bytes 200 | tf_op jit(solution)/shard_map/ppermute | solution.py:33
  49.4 0.3 select_convert_fusion.taps_ref
  49.8 0.6 collective-permute-done.3
  50.3 1.3 %concatenate.21 = s32[32]{0:T(128)} concatenate(s32[2]{0:T(128)S(1)} %bitcast.22, s32[2]{0:T(128)S(1)} %collective-permute-done, s32[4]{0:T(128)} %copy-done.5, s32[8]{0:T(128)} %copy-done.6, s32[16]{0:T(128)} %collective-permute-done.3), dimensions={0} | concatenate | bytes 256 | tf_op jit(solution)/shard_map/concatenate | solution.py:32
  51.6 0.7 reshape.187
  52.4 0.2 dynamic-slice_reduce_fusion
  52.6 0.7 pad_add_fusion.3.info_ref
  53.3 1.8 %shard_map.64 = bf16[16,32,1024]{2,1,0:T(8,128)(2,1)S(1)} custom-call(s32[34]{0:T(128)S(1)} %pad_add_fusion.3.info_ref, bf16[16,16,8,256]{3,2,1,0:T(8,128)(2,1)S(1)} %bitcast.16, f32[16,8,4096]{2,1,0:T(8,128)S(1)} %rsqrt_multiply_fusion.weight_ref, bf16[512,256]{1,0:T(8,128)(2,1)S(1)} %select_convert_fusion.taps_ref), custom_call_target="tpu_custom_call" | custom-call | tf_op jit(solution)/shard_map/pallas_call | solution.py:147
  55.1 1.0 copy-done.2
  56.0 8.8 %all-to-all-start.1 = ((bf16[16,32,1024]{2,1,0:T(8,128)(2,1)}), bf16[16,32,1024]{2,1,0:T(8,128)(2,1)S(1)}, u32[]{:S(2)}, u32[]{:S(2)}) async-start(bf16[16,32,1024]{2,1,0:T(8,128)(2,1)} %copy-done.2), calls=%async_computation.1 | async-start | bytes 2097152 | tf_op jit(solution)/shard_map/all_to_all | solution.py:160
  64.9 0.1 dynamic-slice_bitcast_fusion.1
  64.9 0.8 dynamic-slice_bitcast_fusion
  65.7 0.1 broadcast_compare_fusion
  65.9 0.4 fusion.rowm_ref
  66.2 24.0 %all-to-all-done.1.recv_ref = bf16[16,32,1024]{2,1,0:T(8,128)(2,1)S(1)} async-done(((bf16[16,32,1024]{2,1,0:T(8,128)(2,1)}), bf16[16,32,1024]{2,1,0:T(8,128)(2,1)S(1)}, u32[]{:S(2)}, u32[]{:S(2)}) %all-to-all-start.1) | async-done | bytes 1048608 | tf_op jit(solution)/shard_map/all_to_all | solution.py:160
  90.2 3.4 %copy-done.1 = bf16[2,1,1024,2048]{3,2,1,0:T(8,128)(2,1)S(1)} copy-done((bf16[2,1,1024,2048]{3,2,1,0:T(8,128)(2,1)S(1)}, bf16[2,1,1024,2048]{3,2,1,0:T(8,128)(2,1)}, u32[]{:S(2)}) %copy-start.1) | copy-done | bytes 8388632
  93.6 4.4 %shard_map.65 = bf16[16,8,2048]{2,1,0:T(8,128)(2,1)S(1)} custom-call(bf16[16,32,1024]{2,1,0:T(8,128)(2,1)S(1)} %all-to-all-done.1.recv_ref, bf16[2,128,256]{2,1,0:T(8,128)(2,1)S(1)} %fusion.rowm_ref, bf16[2,1,1024,2048]{3,2,1,0:T(8,128)(2,1)S(1)} %copy-done.1), custom_call_target="tpu_custom_call" | custom-call | tf_op jit(solution)/shard_map/pallas_call | solution.py:173
  98.0 19.0 %all_to_all.15 = bf16[16,8,2048]{2,1,0:T(8,128)(2,1)S(1)} all-to-all(bf16[16,8,2048]{2,1,0:T(8,128)(2,1)S(1)} %shard_map.65), channel_id=1, replica_groups=mesh['proj'=16,'tile'=16] {'proj'}, dimensions={0} | all-to-all | bytes 1048576 | tf_op jit(solution)/shard_map/all_to_all | solution.py:186
  117.0 0.7 convert_reduce_fusion
  (21 shorter events, 0.3 us)
Async XLA Ops:
  0.0 65.9 %copy-start = (bf16[2,1,128,256]{3,2,1,0:T(8,128)(2,1)S(1)}, bf16[2,1,128,256]{3,2,1,0:T(8,128)(2,1)}, u32[]{:S(2)}) copy-start(bf16[2,1,128,256]{3,2,1,0:T(8,128)(2,1)} %param.7) | copy-start | bytes 393220
  0.0 16.8 %copy-start.3 = (s32[32,16]{0,1:T(8,128)S(1)}, s32[32,16]{0,1:T(8,128)}, u32[]{:S(2)}) copy-start(s32[32,16]{0,1:T(8,128)} %param.9) | copy-start | bytes 6148
  0.0 18.8 %collective-permute-start = (s32[2]{0:T(128)}, s32[2]{0:T(128)S(1)}, u32[]{:S(2)}, u32[]{:S(2)}) collective-permute-start(s32[2]{0:T(128)} %bitcast.18), channel_id=1, source_target_pairs={{0,1},{1,0},{2,3},{3,2},{4,5},{5,4},{6,7},{7,6},{8,9},{9,8},{10,11... | collective-permute-start | bytes 32 | tf_op jit(solution)/shard_map/ppermute | solution.py:33
  3.7 15.0 %copy-start.4 = (s32[2,1]{0,1:T(1,128)S(1)}, s32[2,1]{0,1:T(1,128)}, u32[]{:S(2)}) copy-start(s32[2,1]{0,1:T(1,128)} %param.11) | copy-start | bytes 28
  3.8 49.5 %all-to-all-start = ((bf16[256,8,256]{2,1,0:T(8,128)(2,1)}), bf16[256,8,256]{2,1,0:T(8,128)(2,1)S(1)}, u32[]{:S(2)}, u32[]{:S(2)}) async-start(bf16[256,8,256]{2,1,0:T(8,128)(2,1)} %bitcast.17), calls=%async_computation | async-start | bytes 2097152 | tf_op jit(solution)/shard_map/all_to_all | solution.py:116
  18.9 20.6 %collective-permute-start.1 = (s32[4]{0:T(128)S(1)}, s32[4]{0:T(128)S(1)}, u32[]{:S(2)}, u32[]{:S(2)}) collective-permute-start(s32[4]{0:T(128)S(1)} %pad_add_fusion), channel_id=1, source_target_pairs={{0,2},{1,3},{2,0},{3,1},{4,6},{5,7},{6,4},{7,5},{8,10},{9,11},{10,... | collective-permute-start | bytes 56 | tf_op jit(solution)/shard_map/ppermute | solution.py:33
  39.4 3.8 %copy-start.5 = (s32[4]{0:T(128)}, s32[4]{0:T(128)S(1)}, u32[]{:S(2)}) copy-start(s32[4]{0:T(128)S(1)} %collective-permute-done.1) | copy-start | bytes 52
  39.5 3.6 %collective-permute-start.2 = (s32[8]{0:T(128)S(1)}, s32[8]{0:T(128)S(1)}, u32[]{:S(2)}, u32[]{:S(2)}) collective-permute-start(s32[8]{0:T(128)S(1)} %pad_add_fusion.1), channel_id=1, source_target_pairs={{0,4},{1,5},{2,6},{3,7},{4,0},{5,1},{6,2},{7,3},{8,12},{9,13},{10,... | collective-permute-start | bytes 104 | tf_op jit(solution)/shard_map/ppermute | solution.py:33
  43.1 0.6 copy-start.6
  43.7 6.6 %collective-permute-start.3 = (s32[16]{0:T(128)S(1)}, s32[16]{0:T(128)}, u32[]{:S(2)}, u32[]{:S(2)}) collective-permute-start(s32[16]{0:T(128)S(1)} %pad_add_fusion.2), channel_id=1, source_target_pairs={{0,8},{1,9},{2,10},{3,11},{4,12},{5,13},{6,14},{7,15},{8,0},{9,1},... | collective-permute-start | bytes 200 | tf_op jit(solution)/shard_map/ppermute | solution.py:33
  55.1 1.0 copy-start.2
  56.0 34.2 %all-to-all-start.1 = ((bf16[16,32,1024]{2,1,0:T(8,128)(2,1)}), bf16[16,32,1024]{2,1,0:T(8,128)(2,1)S(1)}, u32[]{:S(2)}, u32[]{:S(2)}) async-start(bf16[16,32,1024]{2,1,0:T(8,128)(2,1)} %copy-done.2), calls=%async_computation.1 | async-start | bytes 2097152 | tf_op jit(solution)/shard_map/all_to_all | solution.py:160
  90.2 3.4 %copy-start.1 = (bf16[2,1,1024,2048]{3,2,1,0:T(8,128)(2,1)S(1)}, bf16[2,1,1024,2048]{3,2,1,0:T(8,128)(2,1)}, u32[]{:S(2)}) copy-start(bf16[2,1,1024,2048]{3,2,1,0:T(8,128)(2,1)} %colw_ref.1) | copy-start | bytes 25165828

commit v2 on v1

--- a/solution.py
+++ b/solution.py
@@ -1,3 +1,4 @@
+import functools
 import math
 
 import jax
@@ -25,29 +26,59 @@
     return value.astype(BF16)
 
 
-def gather_offsets(offsets, me_count):
+def gather_offsets(offsets, count):
     flat = offsets.reshape(-1)
-    bit = 1
-    while bit < me_count:
-        flat = jnp.concatenate(
-            [flat, lax.ppermute(flat, "tile", [(i, i ^ bit) for i in range(me_count)])]
-        )
-        bit *= 2
-    return flat
-
-
-def filter_cut(info_ref, recv_ref, weight_ref, taps_ref, out_ref, padded, filtered):
+    far = [flat]
+    for k in range(1, count // 4):
+        far.append(lax.ppermute(flat, "tile", [(i, (i - 4 * k) % count) for i in range(count)]))
+    held = jnp.concatenate(far)
+    near = [lax.ppermute(held, "tile", [(i, i ^ m) for i in range(count)]) for m in range(1, 4)]
+    return jnp.concatenate([held] + near)
+
+
+def filter_cut(
+    local,
+    start_ref,
+    off_ref,
+    recv_ref,
+    weight_hbm,
+    taps_ref,
+    out_ref,
+    padded,
+    filtered,
+    cut,
+    sems,
+    weight_ref,
+    weight_sems,
+):
     groups, n_src, chunk, width = recv_ref.shape
     n_tile, rows_out, win = out_ref.shape
     periods = rows_out // chunk
     rows = groups * chunk
     total = n_src * width
-    me = info_ref[2 * n_tile]
-    row_class = info_ref[2 * n_tile + 1]
+    me = lax.axis_index("tile")
+    classes = n_tile // local
+    row_class = lax.rem(me, classes)
+    which = lax.div(me, classes)
+    proj = lax.axis_index("proj") * local + which
+    parts = weight_sems.shape[0]
+    span = total // parts
+    weight_copies = [
+        pltpu.make_async_copy(
+            weight_hbm.at[:, :, pl.ds(span * n, span)],
+            weight_ref.at[:, :, pl.ds(span * n, span)],
+            weight_sems.at[n],
+        )
+        for n in range(parts)
+    ]
+    for copy in weight_copies:
+        copy.start()
     zero = jnp.zeros((rows, TAP_REACH), BF16)
     padded[:, :TAP_REACH] = zero
     padded[:, TAP_REACH + total :] = zero
     for src in range(n_src):
+        if width * src % span == 0:
+            weight_copies[width * src // span].wait()
         piece = recv_ref[:, src].astype(jnp.float32)
         piece = piece * weight_ref[:, :, width * src : width * (src + 1)]
         lo = TAP_REACH + width * src
@@ -61,13 +92,16 @@
         )
         filtered[:, :, lo : lo + width] = block.reshape(groups, chunk, width)
     row_ids = lax.broadcasted_iota(jnp.int32, (chunk, win), 0)
-    span = chunk * 8
+    span = chunk * classes
+
+    def send(tile):
+        return pltpu.make_async_copy(cut.at[tile], out_ref.at[tile], sems.at[tile])
 
     @pl.loop(0, n_tile)
     def _(k):
-        start = info_ref[k]
-        col = pl.multiple_of(info_ref[n_tile + k] * 128, 128)
-        tile = jnp.bitwise_xor(me, k)
+        tile = lax.rem(jnp.bitwise_xor(me, lax.div(k, 4)) + 4 * lax.rem(k, 4), n_tile)
+        start = start_ref[proj, tile]
+        col = pl.multiple_of(off_ref[local * k + which] * 128, 128)
         parts = []
         for m in range(periods):
             delta = start - (span * m + chunk * row_class) + LMAX
@@ -82,20 +116,40 @@
                     filtered[second, :, pl.ds(col, win)],
                 )
             )
-        out_ref[tile] = jnp.concatenate(parts, axis=0).astype(BF16)
-
-
-def spread_sum(recv_ref, rowm_ref, colw_ref, out_ref):
+        cut[tile] = jnp.concatenate(parts, axis=0).astype(BF16)
+        send(tile).start()
+
+    @pl.loop(0, n_tile)
+    def _(k):
+        send(k).wait()
+
+
+def spread_sum(recv_ref, rowm_ref, colw_ref, out_ref, held, sems):
     n_src, rows, win = recv_ref.shape
     local = rowm_ref.shape[0]
+    step = held.shape[-1]
     per = n_src // local
-    acc = None
-    for q in range(local):
-        window = recv_ref[per * q : per * (q + 1)].reshape(per * rows, win)
-        spread = jnp.dot(window, colw_ref[q, 0], preferred_element_type=jnp.float32).astype(BF16)
-        term = jnp.dot(rowm_ref[q], spread, preferred_element_type=jnp.float32)
-        acc = term if acc is None else acc + term
-    out_ref[...] = acc.reshape(out_ref.shape).astype(BF16)
+    n_step = held.shape[1]
+
+    def fetch(q, n):
+        return pltpu.make_async_copy(
+            colw_ref.at[q, 0, :, pl.ds(n * step, step)], held.at[q, n], sems.at[q, n]
+        )
+
+    for n in range(n_step):
+        for q in range(local):
+            fetch(q, n).start()
+    for n in range(n_step):
+        acc = None
+        for q in range(local):
+            window = recv_ref[per * q : per * (q + 1)].reshape(per * rows, win)
+            fetch(q, n).wait()
+            spread = jnp.dot(window, held[q, n], preferred_element_type=jnp.float32).astype(BF16)
+            term = jnp.dot(rowm_ref[q], spread, preferred_element_type=jnp.float32)
+            acc = term if acc is None else acc + term
+        out_ref[:, :, step * n : step * (n + 1)] = acc.reshape(
+            out_ref.shape[0], out_ref.shape[1], step
+        ).astype(BF16)
 
 
 def body(raw, row_weights, col_weights, band_start, band_length, col_offset):
@@ -121,18 +175,11 @@
         tiled=True,
     ).reshape(n_proj, n_tile, chunk, cols_dev)
 
-    offsets = gather_offsets(col_offset, n_tile).reshape(n_tile, local)
-    which = tile_me // classes
+    offsets = gather_offsets(col_offset, n_tile)
     row_class = tile_me % classes
     first_proj = proj_me * local
     starts_all = lax.dynamic_slice(band_start, (first_proj, 0), (local, n_tile))
     lengths_all = lax.dynamic_slice(band_length, (first_proj, 0), (local, n_tile))
-    order = jnp.bitwise_xor(jnp.arange(n_tile, dtype=jnp.int32), tile_me)
-    my_starts = jnp.take(lax.dynamic_index_in_dim(starts_all, which, 0, False), order)
-    my_offsets = lax.dynamic_index_in_dim(offsets, which, 1, False)
-    info = jnp.concatenate(
-        [my_starts, my_offsets, tile_me.reshape(1), row_class.reshape(1)]
-    ).astype(jnp.int32)
 
     dist = 2.0 * total_cols
     row_ids = (
@@ -145,17 +192,25 @@
     weight = dist / jnp.sqrt(dist * dist + ucoord[None, None, :] ** 2 + vcoord[:, :, None] ** 2)
 
     cut = pl.pallas_call(
-        filter_cut,
+        functools.partial(filter_cut, local),
         out_shape=jax.ShapeDtypeStruct((n_tile, rows_out, win), BF16),
-        in_specs=[pl.BlockSpec(memory_space=pltpu.SMEM)]
-        + [pl.BlockSpec(memory_space=pltpu.VMEM)] * 3,
-        out_specs=pl.BlockSpec(memory_space=pltpu.VMEM),
+        in_specs=[pl.BlockSpec(memory_space=pltpu.SMEM)] * 2
+        + [
+            pl.BlockSpec(memory_space=pltpu.VMEM),
+            pl.BlockSpec(memory_space=pltpu.HBM),
+            pl.BlockSpec(memory_space=pltpu.VMEM),
+        ],
+        out_specs=pl.BlockSpec(memory_space=pltpu.HBM),
         scratch_shapes=[
             pltpu.VMEM((n_proj * chunk, total_cols + 2 * TAP_REACH), BF16),
             pltpu.VMEM((n_proj, chunk, total_cols), jnp.float32),
-        ],
-        compiler_params=pltpu.CompilerParams(vmem_limit_bytes=24 << 20),
-    )(info, recv, weight, tap_matrix(cols_dev))
+            pltpu.VMEM((n_tile, rows_out, win), BF16),
+            pltpu.SemaphoreType.DMA((n_tile,)),
+            pltpu.VMEM((n_proj, chunk, total_cols), jnp.float32),
+            pltpu.SemaphoreType.DMA((4,)),
+        ],
+        compiler_params=pltpu.CompilerParams(vmem_limit_bytes=50 << 20),
+    )(band_start, offsets, recv, weight, tap_matrix(cols_dev))
 
     windows = lax.all_to_all(cut, "tile", split_axis=0, concat_axis=0, tiled=True)
 
@@ -173,14 +228,17 @@
     part = pl.pallas_call(
         spread_sum,
         out_shape=jax.ShapeDtypeStruct((n_proj, slices // n_proj, vox), BF16),
-        grid=(vox // step,),
         in_specs=[
-            pl.BlockSpec((n_tile, rows_out, win), lambda n: (0, 0, 0)),
-            pl.BlockSpec((local, slices, LMAX), lambda n: (0, 0, 0)),
-            pl.BlockSpec((local, 1, win, step), lambda n: (0, 0, 0, n)),
-        ],
-        out_specs=pl.BlockSpec((n_proj, slices // n_proj, step), lambda n: (0, 0, n)),
-        compiler_params=pltpu.CompilerParams(vmem_limit_bytes=24 << 20),
+            pl.BlockSpec(memory_space=pltpu.VMEM),
+            pl.BlockSpec(memory_space=pltpu.VMEM),
+            pl.BlockSpec(memory_space=pltpu.HBM),
+        ],
+        out_specs=pl.BlockSpec(memory_space=pltpu.VMEM),
+        scratch_shapes=[
+            pltpu.VMEM((local, vox // step, win, step), BF16),
+            pltpu.SemaphoreType.DMA((local, vox // step)),
+        ],
+        compiler_params=pltpu.CompilerParams(vmem_limit_bytes=48 << 20),
     )(windows, row_moved, col_weights)
 
     terms = lax.all_to_all(part, "proj", split_axis=0, concat_axis=0, tiled=True)

time: 118 us -> 112 us (0.949)
  local copies, waits for them, and re-layouts: 8.77 us -> 1 us
  Pallas kernels: 6.2 us -> 10.5 us
  starting transfers between devices: 33.5 us -> 32.2 us
  waiting for transfers between devices: 46.5 us -> 45.3 us
    all_to_all x1, starting transfers between devices: 8.8 us -> 3.66 us  [body(): lax.all_to_all(cut, 'tile', split_axis=0, concat_axis=0, tiled=True)]
    unnamed x14 -> x7, local copies, waits for them, and re-layouts: 4.84 us -> 0.09 us
    pallas_call x1, Pallas kernels: 1.8 us -> 4.51 us  [body(): pl.pallas_call(functools.partial(filter_cut, local), out_shape=jax.ShapeD...]
    all_to_all x1, starting transfers between devices: 13 us -> 15.7 us  [body(): lax.all_to_all(raw.reshape(n_proj * n_tile, chunk, cols_dev), ('proj', 't...]
    ppermute x4 -> x6, waiting for transfers between devices: 22.5 us -> 20.9 us  [the longest x3 16.8 us: gather_offsets(): lax.ppermute(flat, 'tile', [(i, (i - 4 * k) % count) for i in range(count)])]
    pallas_call x1, Pallas kernels: 4.39 us -> 5.95 us  [body(): pl.pallas_call(spread_sum, out_shape=jax.ShapeDtypeStruct((n_proj, slices...]
    concatenate x1, local copies, waits for them, and re-layouts: 1.32 us -> 0.08 us  [gather_offsets(): return jnp.concatenate([held] + near)]
    div x1, other arithmetic: 0.48 us -> 1.68 us  [body(): dist / jnp.sqrt(dist * dist + ucoord[None, None, :] ** 2 + vcoord[:, :, N...]
  transfers between devices with their start and end apart: 6 -> 8, of which waited for: 4 -> 5; matrix products, arithmetic and copies ran while one was open for 6% -> 3% of each run, Pallas kernels for 0% -> 0%
where the time goes in v2:
time: 112 us
  waiting for transfers between devices  45.3 us (40%)
  starting transfers between devices  32.2 us (29%)
  blocking collectives  19.3 us (17%)
  Pallas kernels  10.5 us (9%)
  other arithmetic  3.02 us (3%)
    all_to_all x1, waiting for transfers between devices, body(): lax.all_to_all(cut, 'tile', split_axis=0, concat_axis=0, tiled=True)  24.4 us
    all_to_all x1, blocking collectives, body(): lax.all_to_all(part, 'proj', split_axis=0, concat_axis=0, tiled=True)  19.3 us
    ppermute x3, waiting for transfers between devices, gather_offsets(): lax.ppermute(flat, 'tile', [(i, (i - 4 * k) % count) for i in range(count)])  16.8 us
    all_to_all x1, starting transfers between devices, body(): lax.all_to_all(raw.reshape(n_proj * n_tile, chunk, cols_dev), ('proj', 't...  15.7 us
    ppermute x3, starting transfers between devices, gather_offsets(): lax.ppermute(flat, 'tile', [(i, (i - 4 * k) % count) for i in range(count)])  8.67 us
    pallas_call x1, Pallas kernels, body(): pl.pallas_call(spread_sum, out_shape=jax.ShapeDtypeStruct((n_proj, slices...  5.95 us
    pallas_call x1, Pallas kernels, body(): pl.pallas_call(functools.partial(filter_cut, local), out_shape=jax.ShapeD...  4.51 us
    ppermute x3, starting transfers between devices, gather_offsets(): lax.ppermute(held, 'tile', [(i, i ^ m) for i in range(count)])  4.2 us
  transfers between devices with their start and end apart: 8, of which 5 were waited for; matrix products, arithmetic and copies ran while one was open for 3% of the time, Pallas kernels for 0%

profile of v2, /device:TPU:1, one launch (start us, length us, event | category | flops | bytes accessed | tf_op | source)
XLA Modules:
  0.0 111.8 jit_solution(11372395602450761574)
XLA Ops:
  0.0 0.0 copy-start
  0.0 15.7 %all-to-all-start = ((bf16[256,8,256]{2,1,0:T(8,128)(2,1)}), bf16[256,8,256]{2,1,0:T(8,128)(2,1)S(1)}, u32[]{:S(2)}, u32[]{:S(2)}) async-start(bf16[256,8,256]{2,1,0:T(8,128)(2,1)} %bitcast.13), calls=%async_computation | async-start | bytes 2097152 | tf_op jit(solution)/shard_map/all_to_all | solution.py:170
  15.7 5.0 %collective-permute-start = (s32[2]{0:T(128)S(1)}, s32[2]{0:T(128)S(1)}, u32[]{:S(2)}, u32[]{:S(2)}) collective-permute-start(s32[2]{0:T(128)S(1)} %bitcast.14), channel_id=1, source_target_pairs={{0,12},{1,13},{2,14},{3,15},{4,0},{5,1},{6,2},{7,3},{8,4},{9,5},{1... | collective-permute-start | bytes 32 | tf_op jit(solution)/shard_map/ppermute | solution.py:33
  20.7 1.4 %collective-permute-start.1 = (s32[2]{0:T(128)S(1)}, s32[2]{0:T(128)S(1)}, u32[]{:S(2)}, u32[]{:S(2)}) collective-permute-start(s32[2]{0:T(128)S(1)} %bitcast.15), channel_id=1, source_target_pairs={{0,8},{1,9},{2,10},{3,11},{4,12},{5,13},{6,14},{7,15},{8,0},{9,1},... | collective-permute-start | bytes 32 | tf_op jit(solution)/shard_map/ppermute | solution.py:33
  22.1 2.3 %collective-permute-start.2 = (s32[2]{0:T(128)S(1)}, s32[2]{0:T(128)S(1)}, u32[]{:S(2)}, u32[]{:S(2)}) collective-permute-start(s32[2]{0:T(128)S(1)} %bitcast.16), channel_id=1, source_target_pairs={{0,4},{1,5},{2,6},{3,7},{4,8},{5,9},{6,10},{7,11},{8,12},{9,13},{1... | collective-permute-start | bytes 32 | tf_op jit(solution)/shard_map/ppermute | solution.py:33
  24.4 0.1 copy.7.start_ref
  24.5 0.3 select_convert_fusion.taps_ref
  24.8 0.1 add_multiply_fusion
  24.8 1.7 %rsqrt_multiply_fusion.weight_hbm = f32[16,8,4096]{2,1,0:T(8,128)} fusion(f32[16,8]{1,0:T(8,128)S(1)} %add_multiply_fusion, f32[4096]{0:T(1024)S(1)} %multiply_add_fusion), kind=kLoop, calls=%fused_computation | loop fusion | flops 1048576 | bytes 2114048 | tf_op jit(solution)/shard_map/div | solution.py:192
  26.5 11.4 %collective-permute-done = s32[2]{0:T(128)S(1)} collective-permute-done((s32[2]{0:T(128)S(1)}, s32[2]{0:T(128)S(1)}, u32[]{:S(2)}, u32[]{:S(2)}) %collective-permute-start) | collective-permute-done | bytes 40 | tf_op jit(solution)/shard_map/ppermute | solution.py:33
  38.0 5.4 %collective-permute-done.1 = s32[2]{0:T(128)S(1)} collective-permute-done((s32[2]{0:T(128)S(1)}, s32[2]{0:T(128)S(1)}, u32[]{:S(2)}, u32[]{:S(2)}) %collective-permute-start.1) | collective-permute-done | bytes 40 | tf_op jit(solution)/shard_map/ppermute | solution.py:33
  43.4 0.0 collective-permute-done.2
  43.4 0.1 pad_add_fusion
  43.5 2.9 %collective-permute-start.3 = (s32[8]{0:T(128)S(1)}, s32[8]{0:T(128)S(1)}, u32[]{:S(2)}, u32[]{:S(2)}) collective-permute-start(s32[8]{0:T(128)S(1)} %pad_add_fusion), channel_id=1, source_target_pairs={{0,1},{1,0},{2,3},{3,2},{4,5},{5,4},{6,7},{7,6},{8,9},{9,8},{10,11... | collective-permute-start | bytes 104 | tf_op jit(solution)/shard_map/ppermute | solution.py:35
  46.4 0.5 collective-permute-start.4
  46.9 0.8 collective-permute-start.5
  47.7 0.0 collective-permute-done.3
  47.7 1.1 collective-permute-done.4
  48.8 2.9 %collective-permute-done.5 = s32[8]{0:T(128)S(1)} collective-permute-done((s32[8]{0:T(128)S(1)}, s32[8]{0:T(128)S(1)}, u32[]{:S(2)}, u32[]{:S(2)}) %collective-permute-start.5) | collective-permute-done | bytes 64 | tf_op jit(solution)/shard_map/ppermute | solution.py:35
  51.7 0.1 concatenate.8.off_ref
  51.7 0.0 all-to-all-done
  51.7 4.5 %shard_map.64 = bf16[16,32,1024]{2,1,0:T(8,128)(2,1)} custom-call(s32[32,16]{1,0:T(8,128)S(1)} %copy.7.start_ref, s32[32]{0:T(128)S(1)} %concatenate.8.off_ref, bf16[16,16,8,256]{3,2,1,0:T(8,128)(2,1)S(1)} %bitcast.12, f32[16,8,4096]{2,1,0:T(8,128)} %rsqrt_multiply_fusion.weight_hbm, bf16[512,256]{1,0:T(8,128)(2,1)S(1)} %select_convert_fusion.taps_ref), custom_call_target="tpu_custom_call" | custom-call | tf_op jit(solution)/shard_map/pallas_call | solution.py:194
  56.3 3.7 %all-to-all-start.1 = ((bf16[16,32,1024]{2,1,0:T(8,128)(2,1)}), bf16[16,32,1024]{2,1,0:T(8,128)(2,1)S(1)}, u32[]{:S(2)}, u32[]{:S(2)}) async-start(bf16[16,32,1024]{2,1,0:T(8,128)(2,1)} %shard_map.64), calls=%async_computation.1 | async-start | bytes 2097152 | tf_op jit(solution)/shard_map/all_to_all | solution.py:215
  60.0 0.1 dynamic-slice_bitcast_fusion.1
  60.0 0.8 dynamic-slice_bitcast_fusion
  60.8 0.1 broadcast_compare_fusion
  60.9 0.1 subtract_and_fusion
  61.0 0.4 fusion.rowm_ref
  61.3 24.4 %all-to-all-done.1.recv_ref = bf16[16,32,1024]{2,1,0:T(8,128)(2,1)S(1)} async-done(((bf16[16,32,1024]{2,1,0:T(8,128)(2,1)}), bf16[16,32,1024]{2,1,0:T(8,128)(2,1)S(1)}, u32[]{:S(2)}, u32[]{:S(2)}) %all-to-all-start.1) | async-done | bytes 1048608 | tf_op jit(solution)/shard_map/all_to_all | solution.py:215
  85.8 6.0 %shard_map.65 = bf16[16,8,2048]{2,1,0:T(8,128)(2,1)S(1)} custom-call(bf16[16,32,1024]{2,1,0:T(8,128)(2,1)S(1)} %all-to-all-done.1.recv_ref, bf16[2,128,256]{2,1,0:T(8,128)(2,1)S(1)} %fusion.rowm_ref, bf16[2,1,1024,2048]{3,2,1,0:T(8,128)(2,1)} %colw_ref.1), custom_call_target="tpu_custom_call" | custom-call | tf_op jit(solution)/shard_map/pallas_call | solution.py:228
  91.7 19.3 %all_to_all.15 = bf16[16,8,2048]{2,1,0:T(8,128)(2,1)S(1)} all-to-all(bf16[16,8,2048]{2,1,0:T(8,128)(2,1)S(1)} %shard_map.65), channel_id=1, replica_groups=mesh['proj'=16,'tile'=16] {'proj'}, dimensions={0} | all-to-all | bytes 1048576 | tf_op jit(solution)/shard_map/all_to_all | solution.py:244
  111.1 0.7 convert_reduce_fusion
  (8 shorter events, 0.0 us)
Async XLA Ops:
  0.0 61.0 %copy-start = (bf16[2,1,128,256]{3,2,1,0:T(8,128)(2,1)S(1)}, bf16[2,1,128,256]{3,2,1,0:T(8,128)(2,1)}, u32[]{:S(2)}) copy-start(bf16[2,1,128,256]{3,2,1,0:T(8,128)(2,1)} %param.7) | copy-start | bytes 393220
  0.0 15.7 %copy-start.2 = (s32[2,1]{0,1:T(1,128)S(1)}, s32[2,1]{0,1:T(1,128)}, u32[]{:S(2)}) copy-start(s32[2,1]{0,1:T(1,128)} %param.11) | copy-start | bytes 28
  0.0 24.4 %copy-start.1 = (s32[32,16]{0,1:T(8,128)S(1)}, s32[32,16]{0,1:T(8,128)}, u32[]{:S(2)}) copy-start(s32[32,16]{0,1:T(8,128)} %param.9) | copy-start | bytes 6148
  0.0 51.7 %all-to-all-start = ((bf16[256,8,256]{2,1,0:T(8,128)(2,1)}), bf16[256,8,256]{2,1,0:T(8,128)(2,1)S(1)}, u32[]{:S(2)}, u32[]{:S(2)}) async-start(bf16[256,8,256]{2,1,0:T(8,128)(2,1)} %bitcast.13), calls=%async_computation | async-start | bytes 2097152 | tf_op jit(solution)/shard_map/all_to_all | solution.py:170
  15.7 22.3 %collective-permute-start = (s32[2]{0:T(128)S(1)}, s32[2]{0:T(128)S(1)}, u32[]{:S(2)}, u32[]{:S(2)}) collective-permute-start(s32[2]{0:T(128)S(1)} %bitcast.14), channel_id=1, source_target_pairs={{0,12},{1,13},{2,14},{3,15},{4,0},{5,1},{6,2},{7,3},{8,4},{9,5},{1... | collective-permute-start | bytes 32 | tf_op jit(solution)/shard_map/ppermute | solution.py:33
  20.7 22.6 %collective-permute-start.1 = (s32[2]{0:T(128)S(1)}, s32[2]{0:T(128)S(1)}, u32[]{:S(2)}, u32[]{:S(2)}) collective-permute-start(s32[2]{0:T(128)S(1)} %bitcast.15), channel_id=1, source_target_pairs={{0,8},{1,9},{2,10},{3,11},{4,12},{5,13},{6,14},{7,15},{8,0},{9,1},... | collective-permute-start | bytes 32 | tf_op jit(solution)/shard_map/ppermute | solution.py:33
  22.1 21.3 %collective-permute-start.2 = (s32[2]{0:T(128)S(1)}, s32[2]{0:T(128)S(1)}, u32[]{:S(2)}, u32[]{:S(2)}) collective-permute-start(s32[2]{0:T(128)S(1)} %bitcast.16), channel_id=1, source_target_pairs={{0,4},{1,5},{2,6},{3,7},{4,8},{5,9},{6,10},{7,11},{8,12},{9,13},{1... | collective-permute-start | bytes 32 | tf_op jit(solution)/shard_map/ppermute | solution.py:33
  43.5 4.2 %collective-permute-start.3 = (s32[8]{0:T(128)S(1)}, s32[8]{0:T(128)S(1)}, u32[]{:S(2)}, u32[]{:S(2)}) collective-permute-start(s32[8]{0:T(128)S(1)} %pad_add_fusion), channel_id=1, source_target_pairs={{0,1},{1,0},{2,3},{3,2},{4,5},{5,4},{6,7},{7,6},{8,9},{9,8},{10,11... | collective-permute-start | bytes 104 | tf_op jit(solution)/shard_map/ppermute | solution.py:35
  46.4 2.4 %collective-permute-start.4 = (s32[8]{0:T(128)S(1)}, s32[8]{0:T(128)S(1)}, u32[]{:S(2)}, u32[]{:S(2)}) collective-permute-start(s32[8]{0:T(128)S(1)} %pad_add_fusion), channel_id=1, source_target_pairs={{0,2},{1,3},{2,0},{3,1},{4,6},{5,7},{6,4},{7,5},{8,10},{9,11},{10,... | collective-permute-start | bytes 104 | tf_op jit(solution)/shard_map/ppermute | solution.py:35
  46.9 4.8 %collective-permute-start.5 = (s32[8]{0:T(128)S(1)}, s32[8]{0:T(128)S(1)}, u32[]{:S(2)}, u32[]{:S(2)}) collective-permute-start(s32[8]{0:T(128)S(1)} %pad_add_fusion), channel_id=1, source_target_pairs={{0,3},{1,2},{2,1},{3,0},{4,7},{5,6},{6,5},{7,4},{8,11},{9,10},{10,... | collective-permute-start | bytes 104 | tf_op jit(solution)/shard_map/ppermute | solution.py:35
  56.3 29.5 %all-to-all-start.1 = ((bf16[16,32,1024]{2,1,0:T(8,128)(2,1)}), bf16[16,32,1024]{2,1,0:T(8,128)(2,1)S(1)}, u32[]{:S(2)}, u32[]{:S(2)}) async-start(bf16[16,32,1024]{2,1,0:T(8,128)(2,1)} %shard_map.64), calls=%async_computation.1 | async-start | bytes 2097152 | tf_op jit(solution)/shard_map/all_to_all | solution.py:215

commit v3 on v2

--- a/solution.py
+++ b/solution.py
@@ -41,15 +41,11 @@
     start_ref,
     off_ref,
     recv_ref,
-    weight_hbm,
+    weight_ref,
     taps_ref,
     out_ref,
     padded,
     filtered,
-    cut,
-    sems,
-    weight_ref,
-    weight_sems,
 ):
     groups, n_src, chunk, width = recv_ref.shape
     n_tile, rows_out, win = out_ref.shape
@@ -61,24 +57,10 @@
     row_class = lax.rem(me, classes)
     which = lax.div(me, classes)
     proj = lax.axis_index("proj") * local + which
-    parts = weight_sems.shape[0]
-    span = total // parts
-    weight_copies = [
-        pltpu.make_async_copy(
-            weight_hbm.at[:, :, pl.ds(span * n, span)],
-            weight_ref.at[:, :, pl.ds(span * n, span)],
-            weight_sems.at[n],
-        )
-        for n in range(parts)
-    ]
-    for copy in weight_copies:
-        copy.start()
     zero = jnp.zeros((rows, TAP_REACH), BF16)
     padded[:, :TAP_REACH] = zero
     padded[:, TAP_REACH + total :] = zero
     for src in range(n_src):
-        if width * src % span == 0:
-            weight_copies[width * src // span].wait()
         piece = recv_ref[:, src].astype(jnp.float32)
         piece = piece * weight_ref[:, :, width * src : width * (src + 1)]
         lo = TAP_REACH + width * src
@@ -93,9 +75,6 @@
         filtered[:, :, lo : lo + width] = block.reshape(groups, chunk, width)
     row_ids = lax.broadcasted_iota(jnp.int32, (chunk, win), 0)
     span = chunk * classes
-
-    def send(tile):
-        return pltpu.make_async_copy(cut.at[tile], out_ref.at[tile], sems.at[tile])
 
     @pl.loop(0, n_tile)
     def _(k):
@@ -116,12 +95,7 @@
                     filtered[second, :, pl.ds(col, win)],
                 )
             )
-        cut[tile] = jnp.concatenate(parts, axis=0).astype(BF16)
-        send(tile).start()
-
-    @pl.loop(0, n_tile)
-    def _(k):
-        send(k).wait()
+        out_ref[tile] = jnp.concatenate(parts, axis=0).astype(BF16)
 
 
 def spread_sum(recv_ref, rowm_ref, colw_ref, out_ref, held, sems):
@@ -191,29 +165,6 @@
     ucoord = jnp.arange(total_cols, dtype=jnp.int32).astype(jnp.float32) + 0.5 - total_cols / 2.0
     weight = dist / jnp.sqrt(dist * dist + ucoord[None, None, :] ** 2 + vcoord[:, :, None] ** 2)
 
-    cut = pl.pallas_call(
-        functools.partial(filter_cut, local),
-        out_shape=jax.ShapeDtypeStruct((n_tile, rows_out, win), BF16),
-        in_specs=[pl.BlockSpec(memory_space=pltpu.SMEM)] * 2
-        + [
-            pl.BlockSpec(memory_space=pltpu.VMEM),
-            pl.BlockSpec(memory_space=pltpu.HBM),
-            pl.BlockSpec(memory_space=pltpu.VMEM),
-        ],
-        out_specs=pl.BlockSpec(memory_space=pltpu.HBM),
-        scratch_shapes=[
-            pltpu.VMEM((n_proj * chunk, total_cols + 2 * TAP_REACH), BF16),
-            pltpu.VMEM((n_proj, chunk, total_cols), jnp.float32),
-            pltpu.VMEM((n_tile, rows_out, win), BF16),
-            pltpu.SemaphoreType.DMA((n_tile,)),
-            pltpu.VMEM((n_proj, chunk, total_cols), jnp.float32),
-            pltpu.SemaphoreType.DMA((4,)),
-        ],
-        compiler_params=pltpu.CompilerParams(vmem_limit_bytes=50 << 20),
-    )(band_start, offsets, recv, weight, tap_matrix(cols_dev))
-
-    windows = lax.all_to_all(cut, "tile", split_axis=0, concat_axis=0, tiled=True)
-
     place = jnp.arange(LMAX, dtype=jnp.int32)
     row_mod = place // rows_out * chunk + place % rows_out // chunk * rows_dev + place % chunk
     my_start = lax.dynamic_slice_in_dim(starts_all, tile_me, 1, 1)
@@ -224,7 +175,23 @@
         "qsi,qik->qsk", row_weights[:, 0], pick.astype(BF16), preferred_element_type=jnp.float32
     ).astype(BF16)
 
-    step = 512
+    offsets, row_moved = lax.optimization_barrier((offsets, row_moved))
+    cut = pl.pallas_call(
+        functools.partial(filter_cut, local),
+        out_shape=jax.ShapeDtypeStruct((n_tile, rows_out, win), BF16),
+        in_specs=[pl.BlockSpec(memory_space=pltpu.SMEM)] * 2
+        + [pl.BlockSpec(memory_space=pltpu.VMEM)] * 3,
+        out_specs=pl.BlockSpec(memory_space=pltpu.VMEM),
+        scratch_shapes=[
+            pltpu.VMEM((n_proj * chunk, total_cols + 2 * TAP_REACH), BF16),
+            pltpu.VMEM((n_proj, chunk, total_cols), jnp.float32),
+        ],
+        compiler_params=pltpu.CompilerParams(vmem_limit_bytes=24 << 20),
+    )(band_start, offsets, recv, weight, tap_matrix(cols_dev))
+
+    windows = lax.all_to_all(cut, "tile", split_axis=0, concat_axis=0, tiled=True)
+
+    step = 256
     part = pl.pallas_call(
         spread_sum,
         out_shape=jax.ShapeDtypeStruct((n_proj, slices // n_proj, vox), BF16),

time: 112 us -> 113 us (level)
  blocking collectives: 19.3 us -> 47.2 us
  waiting for transfers between devices: 45.3 us -> 22.2 us
  starting transfers between devices: 32.2 us -> 25.3 us
  local copies, waits for them, and re-layouts: 1 us -> 2.8 us
  Pallas kernels: 10.5 us -> 12.1 us
    all_to_all x0 -> x1, blocking collectives: none -> 31.8 us  [body(): lax.all_to_all(cut, 'tile', split_axis=0, concat_axis=0, tiled=True)]
    all_to_all x1 -> x0, waiting for transfers between devices: 24.4 us -> none  [body(): lax.all_to_all(cut, 'tile', split_axis=0, concat_axis=0, tiled=True)]
    ppermute x3, waiting for transfers between devices: 16.8 us -> 0.01 us  [gather_offsets(): lax.ppermute(flat, 'tile', [(i, (i - 4 * k) % count) for i in range(count)])]
    ppermute x3, waiting for transfers between devices: 4.01 us -> 16.9 us  [gather_offsets(): lax.ppermute(held, 'tile', [(i, i ^ m) for i in range(count)])]
    all_to_all x1, starting transfers between devices: 15.7 us -> 9.5 us  [body(): lax.all_to_all(raw.reshape(n_proj * n_tile, chunk, cols_dev), ('proj', 't...]
    all_to_all x1, waiting for transfers between devices: 0.01 us -> 5.29 us  [body(): lax.all_to_all(raw.reshape(n_proj * n_tile, chunk, cols_dev), ('proj', 't...]
    pallas_call x1, Pallas kernels: 5.95 us -> 9.94 us  [body(): pl.pallas_call(spread_sum, out_shape=jax.ShapeDtypeStruct((n_proj, slices...]
    all_to_all x1, blocking collectives: 19.3 us -> 15.4 us  [body(): lax.all_to_all(part, 'proj', split_axis=0, concat_axis=0, tiled=True)]
  transfers between devices with their start and end apart: 8 -> 7, of which waited for: 5 -> 2; matrix products, arithmetic and copies ran while one was open for 3% -> 4% of each run, Pallas kernels for 0% -> 0%
where the time goes in v3:
time: 113 us
  blocking collectives  47.2 us (42%)
  starting transfers between devices  25.3 us (22%)
  waiting for transfers between devices  22.2 us (20%)
  Pallas kernels  12.1 us (11%)
  local copies, waits for them, and re-layouts  2.8 us (2%)
  other arithmetic  2.5 us (2%)
    all_to_all x1, blocking collectives, body(): lax.all_to_all(cut, 'tile', split_axis=0, concat_axis=0, tiled=True)  31.8 us
    ppermute x3, waiting for transfers between devices, gather_offsets(): lax.ppermute(held, 'tile', [(i, i ^ m) for i in range(count)])  16.9 us
    all_to_all x1, blocking collectives, body(): lax.all_to_all(part, 'proj', split_axis=0, concat_axis=0, tiled=True)  15.4 us
    ppermute x3, starting transfers between devices, gather_offsets(): lax.ppermute(flat, 'tile', [(i, (i - 4 * k) % count) for i in range(count)])  11.3 us
    pallas_call x1, Pallas kernels, body(): pl.pallas_call(spread_sum, out_shape=jax.ShapeDtypeStruct((n_proj, slices...  9.94 us
    all_to_all x1, starting transfers between devices, body(): lax.all_to_all(raw.reshape(n_proj * n_tile, chunk, cols_dev), ('proj', 't...  9.5 us
    all_to_all x1, waiting for transfers between devices, body(): lax.all_to_all(raw.reshape(n_proj * n_tile, chunk, cols_dev), ('proj', 't...  5.29 us
    ppermute x3, starting transfers between devices, gather_offsets(): lax.ppermute(held, 'tile', [(i, i ^ m) for i in range(count)])  4.45 us
  transfers between devices with their start and end apart: 7, of which 2 were waited for; matrix products, arithmetic and copies ran while one was open for 4% of the time, Pallas kernels for 0%

profile of v3, /device:TPU:1, one launch (start us, length us, event | category | flops | bytes accessed | tf_op | source)
XLA Modules:
  0.0 113.2 jit_solution(10876643517087529704)
XLA Ops:
  0.0 0.0 copy-start
  0.0 3.8 %collective-permute-start.2 = (s32[2]{0:T(128)}, s32[2]{0:T(128)}, u32[]{:S(2)}, u32[]{:S(2)}) collective-permute-start(s32[2]{0:T(128)} %bitcast.14), channel_id=1, source_target_pairs={{0,4},{1,5},{2,6},{3,7},{4,8},{5,9},{6,10},{7,11},{8,12},{9,13},{1... | collective-permute-start | bytes 32 | tf_op jit(solution)/shard_map/ppermute | solution.py:33
  3.8 5.1 %collective-permute-start.1 = (s32[2]{0:T(128)}, s32[2]{0:T(128)}, u32[]{:S(2)}, u32[]{:S(2)}) collective-permute-start(s32[2]{0:T(128)} %bitcast.15), channel_id=1, source_target_pairs={{0,8},{1,9},{2,10},{3,11},{4,12},{5,13},{6,14},{7,15},{8,0},{9,1},... | collective-permute-start | bytes 32 | tf_op jit(solution)/shard_map/ppermute | solution.py:33
  8.9 2.4 %collective-permute-start = (s32[2]{0:T(128)}, s32[2]{0:T(128)}, u32[]{:S(2)}, u32[]{:S(2)}) collective-permute-start(s32[2]{0:T(128)} %bitcast.16), channel_id=1, source_target_pairs={{0,12},{1,13},{2,14},{3,15},{4,0},{5,1},{6,2},{7,3},{8,4},{9,5},{1... | collective-permute-start | bytes 32 | tf_op jit(solution)/shard_map/ppermute | solution.py:33
  11.3 9.5 %all-to-all-start = ((bf16[256,8,256]{2,1,0:T(8,128)(2,1)}), bf16[256,8,256]{2,1,0:T(8,128)(2,1)S(1)}, u32[]{:S(2)}, u32[]{:S(2)}) async-start(bf16[256,8,256]{2,1,0:T(8,128)(2,1)} %bitcast.13), calls=%async_computation | async-start | bytes 2097152 | tf_op jit(solution)/shard_map/all_to_all | solution.py:144
  20.9 0.3 select_convert_fusion.taps_ref
  21.2 0.8 dynamic-slice_bitcast_fusion
  22.0 0.1 copy.8.start_ref
  22.1 0.1 broadcast_compare_fusion
  22.1 0.1 subtract_and_fusion
  22.2 0.1 add_multiply_fusion
  22.3 0.0 copy-done
  22.3 1.0 fusion.rowm_ref
  23.3 0.5 rsqrt_multiply_fusion.weight_ref
  23.8 0.0 collective-permute-done.2
  23.8 0.0 collective-permute-done.1
  23.8 0.0 collective-permute-done
  23.8 0.8 pad_add_fusion
  24.6 4.1 %collective-permute-start.5 = (s32[8]{0:T(128)S(1)}, s32[8]{0:T(128)}, u32[]{:S(2)}, u32[]{:S(2)}) collective-permute-start(s32[8]{0:T(128)S(1)} %pad_add_fusion), channel_id=1, source_target_pairs={{0,3},{1,2},{2,1},{3,0},{4,7},{5,6},{6,5},{7,4},{8,11},{9,10},{10,... | collective-permute-start | bytes 104 | tf_op jit(solution)/shard_map/ppermute | solution.py:35
  28.6 0.0 collective-permute-start.4
  28.7 0.3 collective-permute-start.3
  29.0 16.8 %collective-permute-done.5 = s32[8]{0:T(128)} collective-permute-done((s32[8]{0:T(128)S(1)}, s32[8]{0:T(128)}, u32[]{:S(2)}, u32[]{:S(2)}) %collective-permute-start.5) | collective-permute-done | bytes 64 | tf_op jit(solution)/shard_map/ppermute | solution.py:35
  45.9 0.0 collective-permute-done.4
  45.9 0.0 collective-permute-done.3
  45.9 1.3 %concatenate.8.off_ref = s32[32]{0:T(128)} concatenate(s32[2]{0:T(128)} %bitcast.18, s32[2]{0:T(128)} %collective-permute-done, s32[2]{0:T(128)} %collective-permute-done.1, s32[2]{0:T(128)} %collective-permute-done.2, s32[8]{0:T(128)} %collective-permute-done.3, s32[8]{0:T(128)} %collective-permute-done.4, s32[8]{0:T(128)} %collective-permute-done.5), dimensions={0} | concatenate | bytes 256 | tf_op jit(solution)/shard_map/concatenate | solution.py:36
  47.2 5.3 %all-to-all-done = bf16[256,8,256]{2,1,0:T(8,128)(2,1)S(1)} async-done(((bf16[256,8,256]{2,1,0:T(8,128)(2,1)}), bf16[256,8,256]{2,1,0:T(8,128)(2,1)S(1)}, u32[]{:S(2)}, u32[]{:S(2)}) %all-to-all-start) | async-done | bytes 1048608 | tf_op jit(solution)/shard_map/all_to_all | solution.py:144
  52.5 0.7 copy-done.2
  53.1 2.2 %shard_map.64 = bf16[16,32,1024]{2,1,0:T(8,128)(2,1)S(1)} custom-call(s32[32,16]{1,0:T(8,128)S(1)} %copy.8.start_ref, s32[32]{0:T(128)S(1)} %copy-done.2, bf16[16,16,8,256]{3,2,1,0:T(8,128)(2,1)S(1)} %bitcast.12, f32[16,8,4096]{2,1,0:T(8,128)S(1)} %rsqrt_multiply_fusion.weight_ref, bf16[512,256]{1,0:T(8,128)(2,1)S(1)} %select_convert_fusion.taps_ref), custom_call_target="tpu_custom_call" | custom-call | tf_op jit(solution)/shard_map/pallas_call | solution.py:179
  55.3 31.8 %all_to_all.15.recv_ref = bf16[16,32,1024]{2,1,0:T(8,128)(2,1)S(1)} all-to-all(bf16[16,32,1024]{2,1,0:T(8,128)(2,1)S(1)} %shard_map.64), channel_id=1, replica_groups=mesh['proj'=16,'tile'=16] {'tile'}, dimensions={0} | all-to-all | bytes 2097152 | tf_op jit(solution)/shard_map/all_to_all | solution.py:192
  87.1 9.9 %shard_map.65 = bf16[16,8,2048]{2,1,0:T(8,128)(2,1)S(1)} custom-call(bf16[16,32,1024]{2,1,0:T(8,128)(2,1)S(1)} %all_to_all.15.recv_ref, bf16[2,128,256]{2,1,0:T(8,128)(2,1)S(1)} %copy-done.1, bf16[2,1,1024,2048]{3,2,1,0:T(8,128)(2,1)} %colw_ref.1), custom_call_target="tpu_custom_call" | custom-call | tf_op jit(solution)/shard_map/pallas_call | solution.py:195
  97.1 15.4 %all_to_all.16 = bf16[16,8,2048]{2,1,0:T(8,128)(2,1)S(1)} all-to-all(bf16[16,8,2048]{2,1,0:T(8,128)(2,1)S(1)} %shard_map.65), channel_id=1, replica_groups=mesh['proj'=16,'tile'=16] {'proj'}, dimensions={0} | all-to-all | bytes 1048576 | tf_op jit(solution)/shard_map/all_to_all | solution.py:211
  112.5 0.7 convert_reduce_fusion
  (8 shorter events, 0.0 us)
Async XLA Ops:
  0.0 22.3 %copy-start = (bf16[2,1,128,256]{3,2,1,0:T(8,128)(2,1)S(1)}, bf16[2,1,128,256]{3,2,1,0:T(8,128)(2,1)}, u32[]{:S(2)}) copy-start(bf16[2,1,128,256]{3,2,1,0:T(8,128)(2,1)} %param.7) | copy-start | bytes 393220
  0.0 21.2 %copy-start.3 = (s32[32,16]{0,1:T(8,128)S(1)}, s32[32,16]{0,1:T(8,128)}, u32[]{:S(2)}) copy-start(s32[32,16]{0,1:T(8,128)} %param.9) | copy-start | bytes 6148
  0.0 23.8 %collective-permute-start.2 = (s32[2]{0:T(128)}, s32[2]{0:T(128)}, u32[]{:S(2)}, u32[]{:S(2)}) collective-permute-start(s32[2]{0:T(128)} %bitcast.14), channel_id=1, source_target_pairs={{0,4},{1,5},{2,6},{3,7},{4,8},{5,9},{6,10},{7,11},{8,12},{9,13},{1... | collective-permute-start | bytes 32 | tf_op jit(solution)/shard_map/ppermute | solution.py:33
  3.8 20.0 %collective-permute-start.1 = (s32[2]{0:T(128)}, s32[2]{0:T(128)}, u32[]{:S(2)}, u32[]{:S(2)}) collective-permute-start(s32[2]{0:T(128)} %bitcast.15), channel_id=1, source_target_pairs={{0,8},{1,9},{2,10},{3,11},{4,12},{5,13},{6,14},{7,15},{8,0},{9,1},... | collective-permute-start | bytes 32 | tf_op jit(solution)/shard_map/ppermute | solution.py:33
  8.9 14.9 %collective-permute-start = (s32[2]{0:T(128)}, s32[2]{0:T(128)}, u32[]{:S(2)}, u32[]{:S(2)}) collective-permute-start(s32[2]{0:T(128)} %bitcast.16), channel_id=1, source_target_pairs={{0,12},{1,13},{2,14},{3,15},{4,0},{5,1},{6,2},{7,3},{8,4},{9,5},{1... | collective-permute-start | bytes 32 | tf_op jit(solution)/shard_map/ppermute | solution.py:33
  11.3 41.2 %all-to-all-start = ((bf16[256,8,256]{2,1,0:T(8,128)(2,1)}), bf16[256,8,256]{2,1,0:T(8,128)(2,1)S(1)}, u32[]{:S(2)}, u32[]{:S(2)}) async-start(bf16[256,8,256]{2,1,0:T(8,128)(2,1)} %bitcast.13), calls=%async_computation | async-start | bytes 2097152 | tf_op jit(solution)/shard_map/all_to_all | solution.py:144
  24.6 21.3 %collective-permute-start.5 = (s32[8]{0:T(128)S(1)}, s32[8]{0:T(128)}, u32[]{:S(2)}, u32[]{:S(2)}) collective-permute-start(s32[8]{0:T(128)S(1)} %pad_add_fusion), channel_id=1, source_target_pairs={{0,3},{1,2},{2,1},{3,0},{4,7},{5,6},{6,5},{7,4},{8,11},{9,10},{10,... | collective-permute-start | bytes 104 | tf_op jit(solution)/shard_map/ppermute | solution.py:35
  28.6 17.2 %collective-permute-start.4 = (s32[8]{0:T(128)S(1)}, s32[8]{0:T(128)}, u32[]{:S(2)}, u32[]{:S(2)}) collective-permute-start(s32[8]{0:T(128)S(1)} %pad_add_fusion), channel_id=1, source_target_pairs={{0,2},{1,3},{2,0},{3,1},{4,6},{5,7},{6,4},{7,5},{8,10},{9,11},{10,... | collective-permute-start | bytes 104 | tf_op jit(solution)/shard_map/ppermute | solution.py:35
  28.7 17.2 %collective-permute-start.3 = (s32[8]{0:T(128)S(1)}, s32[8]{0:T(128)}, u32[]{:S(2)}, u32[]{:S(2)}) collective-permute-start(s32[8]{0:T(128)S(1)} %pad_add_fusion), channel_id=1, source_target_pairs={{0,1},{1,0},{2,3},{3,2},{4,5},{5,4},{6,7},{7,6},{8,9},{9,8},{10,11... | collective-permute-start | bytes 104 | tf_op jit(solution)/shard_map/ppermute | solution.py:35
  52.5 0.7 copy-start.2
  55.3 31.8 %copy-start.1 = (bf16[2,128,256]{2,1,0:T(8,128)(2,1)S(1)}, bf16[2,128,256]{2,1,0:T(8,128)(2,1)}, u32[]{:S(2)}) copy-start(bf16[2,128,256]{2,1,0:T(8,128)(2,1)} %fusion.rowm_ref) | copy-start | bytes 393220

commit v4 on v3

--- a/solution.py
+++ b/solution.py
@@ -27,44 +27,30 @@
 
 
 def gather_offsets(offsets, count):
+    half = count // 4
     flat = offsets.reshape(-1)
-    far = [flat]
-    for k in range(1, count // 4):
-        far.append(lax.ppermute(flat, "tile", [(i, (i - 4 * k) % count) for i in range(count)]))
-    held = jnp.concatenate(far)
-    near = [lax.ppermute(held, "tile", [(i, i ^ m) for i in range(count)]) for m in range(1, 4)]
-    return jnp.concatenate([held] + near)
-
-
-def filter_cut(
-    local,
-    start_ref,
-    off_ref,
-    recv_ref,
-    weight_ref,
-    taps_ref,
-    out_ref,
-    padded,
-    filtered,
-):
+    held = jnp.concatenate([flat, lax.ppermute(flat, "tile", [(i, i ^ 1) for i in range(count)])])
+    held = lax.optimization_barrier(held)
+    far = [
+        lax.ppermute(
+            held, "tile", [((i + 2 * (k + half * (i % 2))) % count, i) for i in range(count)]
+        )
+        for k in range(1, half + 1)
+    ]
+    return held, jnp.concatenate(far)
+
+
+def filter_rows(recv_ref, weight_ref, taps_ref, out_ref, padded):
     groups, n_src, chunk, width = recv_ref.shape
-    n_tile, rows_out, win = out_ref.shape
-    periods = rows_out // chunk
     rows = groups * chunk
     total = n_src * width
-    me = lax.axis_index("tile")
-    classes = n_tile // local
-    row_class = lax.rem(me, classes)
-    which = lax.div(me, classes)
-    proj = lax.axis_index("proj") * local + which
     zero = jnp.zeros((rows, TAP_REACH), BF16)
     padded[:, :TAP_REACH] = zero
     padded[:, TAP_REACH + total :] = zero
     for src in range(n_src):
-        piece = recv_ref[:, src].astype(jnp.float32)
-        piece = piece * weight_ref[:, :, width * src : width * (src + 1)]
-        lo = TAP_REACH + width * src
-        padded[:, lo : lo + width] = piece.reshape(rows, width).astype(BF16)
+        lo = width * src
+        piece = recv_ref[:, src].astype(jnp.float32) * weight_ref[:, :, lo : lo + width]
+        padded[:, lo + TAP_REACH : lo + TAP_REACH + width] = piece.reshape(rows, width).astype(BF16)
     for src in range(n_src):
         lo = width * src
         block = jnp.dot(
@@ -72,15 +58,35 @@
             taps_ref[...],
             preferred_element_type=jnp.float32,
         )
-        filtered[:, :, lo : lo + width] = block.reshape(groups, chunk, width)
+        out_ref[:, :, lo : lo + width] = block.reshape(groups, chunk, width)
+
+
+def cut_windows(local, start_ref, own_ref, mine_ref, other_ref, filtered, out_ref):
+    groups, chunk, _ = filtered.shape
+    n_tile, rows_out, win = out_ref.shape
+    periods = rows_out // chunk
+    me = lax.axis_index("tile")
+    classes = n_tile // local
+    row_class = lax.rem(me, classes)
+    which = lax.div(me, classes)
+    proj = lax.axis_index("proj") * local + which
     row_ids = lax.broadcasted_iota(jnp.int32, (chunk, win), 0)
     span = chunk * classes
+    half = n_tile // 4
+    me_y = lax.rem(me, 2)
 
     @pl.loop(0, n_tile)
     def _(k):
-        tile = lax.rem(jnp.bitwise_xor(me, lax.div(k, 4)) + 4 * lax.rem(k, 4), n_tile)
-        start = start_ref[proj, tile]
-        col = pl.multiple_of(off_ref[local * k + which] * 128, 128)
+        turn = lax.div(k, 2)
+        y = lax.rem(k, 2)
+        side = jnp.where(turn > half, 1, 0)
+        near = (jnp.bitwise_xor(y, me_y)) * local + which
+        block = jnp.where(turn > half, turn - half, jnp.maximum(turn, 1)) - 1
+        spot = (2 * block + jnp.bitwise_xor(y, side)) * local + which
+        far = jnp.where(side == me_y, mine_ref[spot], other_ref[spot])
+        col = pl.multiple_of(jnp.where(turn == 0, own_ref[near], far) * 128, 128)
+        tile = lax.rem(me - me_y + 2 * turn, n_tile) + y
+        start = start_ref[tile, proj]
         parts = []
         for m in range(periods):
             delta = start - (span * m + chunk * row_class) + LMAX
@@ -98,32 +104,38 @@
         out_ref[tile] = jnp.concatenate(parts, axis=0).astype(BF16)
 
 
-def spread_sum(recv_ref, rowm_ref, colw_ref, out_ref, held, sems):
+def spread_sum(recv_ref, rowm_ref, colw_ref, out_ref, held, acc, total, sems):
     n_src, rows, win = recv_ref.shape
-    local = rowm_ref.shape[0]
-    step = held.shape[-1]
+    local, parts, depth, _ = held.shape
     per = n_src // local
-    n_step = held.shape[1]
-
-    def fetch(q, n):
+
+    def fetch(q, k):
         return pltpu.make_async_copy(
-            colw_ref.at[q, 0, :, pl.ds(n * step, step)], held.at[q, n], sems.at[q, n]
+            colw_ref.at[q, 0, pl.ds(depth * k, depth)], held.at[q, k], sems.at[q, k]
         )
 
-    for n in range(n_step):
-        for q in range(local):
-            fetch(q, n).start()
-    for n in range(n_step):
-        acc = None
-        for q in range(local):
-            window = recv_ref[per * q : per * (q + 1)].reshape(per * rows, win)
-            fetch(q, n).wait()
-            spread = jnp.dot(window, held[q, n], preferred_element_type=jnp.float32).astype(BF16)
-            term = jnp.dot(rowm_ref[q], spread, preferred_element_type=jnp.float32)
-            acc = term if acc is None else acc + term
-        out_ref[:, :, step * n : step * (n + 1)] = acc.reshape(
-            out_ref.shape[0], out_ref.shape[1], step
-        ).astype(BF16)
+    for q in range(local):
+        for k in range(parts):
+            fetch(q, k).start()
+    for q in range(local):
+        for k in range(parts):
+            fetch(q, k).wait()
+            window = recv_ref[per * q : per * (q + 1), :, depth * k : depth * (k + 1)]
+            piece = jnp.dot(
+                window.reshape(per * rows, depth), held[q, k], preferred_element_type=jnp.float32
+            )
+            if k:
+                piece = acc[...] + piece
+            if k < parts - 1:
+                acc[...] = piece
+                continue
+            term = jnp.dot(rowm_ref[q], piece.astype(BF16), preferred_element_type=jnp.float32)
+            if q:
+                term = total[...] + term
+            if q < local - 1:
+                total[...] = term
+            else:
+                out_ref[...] = term.reshape(out_ref.shape).astype(BF16)
 
 
 def body(raw, row_weights, col_weights, band_start, band_length, col_offset):
@@ -149,7 +161,9 @@
         tiled=True,
     ).reshape(n_proj, n_tile, chunk, cols_dev)
 
-    offsets = gather_offsets(col_offset, n_tile)
+    own, mine = gather_offsets(col_offset, n_tile)
+    mine, recv = lax.optimization_barrier((mine, recv))
+    other = lax.ppermute(mine, "tile", [(i, i ^ 1) for i in range(n_tile)])
     row_class = tile_me % classes
     first_proj = proj_me * local
     starts_all = lax.dynamic_slice(band_start, (first_proj, 0), (local, n_tile))
@@ -175,35 +189,41 @@
         "qsi,qik->qsk", row_weights[:, 0], pick.astype(BF16), preferred_element_type=jnp.float32
     ).astype(BF16)
 
-    offsets, row_moved = lax.optimization_barrier((offsets, row_moved))
+    other, row_moved = lax.optimization_barrier((other, row_moved))
+    filtered = pl.pallas_call(
+        filter_rows,
+        out_shape=jax.ShapeDtypeStruct((n_proj, chunk, total_cols), jnp.float32),
+        in_specs=[pl.BlockSpec(memory_space=pltpu.VMEM)] * 3,
+        out_specs=pl.BlockSpec(memory_space=pltpu.VMEM),
+        scratch_shapes=[pltpu.VMEM((n_proj * chunk, total_cols + 2 * TAP_REACH), BF16)],
+        compiler_params=pltpu.CompilerParams(vmem_limit_bytes=24 << 20),
+    )(recv, weight, tap_matrix(cols_dev))
     cut = pl.pallas_call(
-        functools.partial(filter_cut, local),
+        functools.partial(cut_windows, local),
         out_shape=jax.ShapeDtypeStruct((n_tile, rows_out, win), BF16),
-        in_specs=[pl.BlockSpec(memory_space=pltpu.SMEM)] * 2
-        + [pl.BlockSpec(memory_space=pltpu.VMEM)] * 3,
+        in_specs=[pl.BlockSpec(memory_space=pltpu.SMEM)] * 4
+        + [pl.BlockSpec(memory_space=pltpu.VMEM)],
         out_specs=pl.BlockSpec(memory_space=pltpu.VMEM),
-        scratch_shapes=[
-            pltpu.VMEM((n_proj * chunk, total_cols + 2 * TAP_REACH), BF16),
-            pltpu.VMEM((n_proj, chunk, total_cols), jnp.float32),
-        ],
         compiler_params=pltpu.CompilerParams(vmem_limit_bytes=24 << 20),
-    )(band_start, offsets, recv, weight, tap_matrix(cols_dev))
+    )(band_start.T, own, mine, other, filtered)
 
     windows = lax.all_to_all(cut, "tile", split_axis=0, concat_axis=0, tiled=True)
 
-    step = 256
+    parts = 2
     part = pl.pallas_call(
         spread_sum,
         out_shape=jax.ShapeDtypeStruct((n_proj, slices // n_proj, vox), BF16),
         in_specs=[
             pl.BlockSpec(memory_space=pltpu.VMEM),
             pl.BlockSpec(memory_space=pltpu.VMEM),
-            pl.BlockSpec(memory_space=pltpu.HBM),
+            pl.BlockSpec(memory_space=pl.ANY),
         ],
         out_specs=pl.BlockSpec(memory_space=pltpu.VMEM),
         scratch_shapes=[
-            pltpu.VMEM((local, vox // step, win, step), BF16),
-            pltpu.SemaphoreType.DMA((local, vox // step)),
+            pltpu.VMEM((local, parts, win // parts, vox), BF16),
+            pltpu.VMEM((LMAX, vox), jnp.float32),
+            pltpu.VMEM((slices, vox), jnp.float32),
+            pltpu.SemaphoreType.DMA((local, parts)),
         ],
         compiler_params=pltpu.CompilerParams(vmem_limit_bytes=48 << 20),
     )(windows, row_moved, col_weights)

time: 113 us -> 106 us (0.938)
  waiting for transfers between devices: 22.2 us -> 16.4 us
  Pallas kernels: 12.1 us -> 6.85 us
  starting transfers between devices: 25.3 us -> 30.2 us
  local copies, waits for them, and re-layouts: 2.8 us -> 0.78 us
  other arithmetic: 2.5 us -> 3.75 us
    pallas_call x1, Pallas kernels: 9.94 us -> 4.61 us  [body(): pl.pallas_call(spread_sum, out_shape=jax.ShapeDtypeStruct((n_proj, slices...]
    ppermute x6, waiting for transfers between devices: 16.9 us -> 12.5 us  [the longest x4 10.3 us: gather_offsets(): lax.ppermute(held, 'tile', [((i + 2 * (k + half * (i % 2))) % count, i) f...]
    all_to_all x1, starting transfers between devices: 9.5 us -> 13 us  [body(): lax.all_to_all(raw.reshape(n_proj * n_tile, chunk, cols_dev), ('proj', 't...]
    all_to_all x1, blocking collectives: 31.8 us -> 30 us  [body(): lax.all_to_all(cut, 'tile', split_axis=0, concat_axis=0, tiled=True)]
    ppermute x6, starting transfers between devices: 15.8 us -> 17.2 us  [the longest x4 12.5 us: gather_offsets(): lax.ppermute(held, 'tile', [((i + 2 * (k + half * (i % 2))) % count, i) f...]
    all_to_all x1, waiting for transfers between devices: 5.29 us -> 3.89 us  [body(): lax.all_to_all(raw.reshape(n_proj * n_tile, chunk, cols_dev), ('proj', 't...]
    concatenate x1 -> x0, local copies, waits for them, and re-layouts: 1.3 us -> none  [gather_offsets(): return jnp.concatenate([held] + near)]
  transfers between devices with their start and end apart: 7 -> 7, of which waited for: 2 -> 5; matrix products, arithmetic and copies ran while one was open for 4% -> 5% of each run, Pallas kernels for 0% -> 1%
where the time goes in v4:
time: 106 us
  blocking collectives  46.5 us (44%)
  starting transfers between devices  30.2 us (28%)
  waiting for transfers between devices  16.4 us (15%)
  Pallas kernels  6.85 us (6%)
  other arithmetic  3.75 us (4%)
    all_to_all x1, blocking collectives, body(): lax.all_to_all(cut, 'tile', split_axis=0, concat_axis=0, tiled=True)  30 us
    all_to_all x1, blocking collectives, body(): lax.all_to_all(part, 'proj', split_axis=0, concat_axis=0, tiled=True)  16.5 us
    all_to_all x1, starting transfers between devices, body(): lax.all_to_all(raw.reshape(n_proj * n_tile, chunk, cols_dev), ('proj', 't...  13 us
    ppermute x4, starting transfers between devices, gather_offsets(): lax.ppermute(held, 'tile', [((i + 2 * (k + half * (i % 2))) % count, i) f...  12.5 us
    ppermute x4, waiting for transfers between devices, gather_offsets(): lax.ppermute(held, 'tile', [((i + 2 * (k + half * (i % 2))) % count, i) f...  10.3 us
    pallas_call x1, Pallas kernels, body(): pl.pallas_call(spread_sum, out_shape=jax.ShapeDtypeStruct((n_proj, slices...  4.61 us
    all_to_all x1, waiting for transfers between devices, body(): lax.all_to_all(raw.reshape(n_proj * n_tile, chunk, cols_dev), ('proj', 't...  3.89 us
    ppermute x1, starting transfers between devices, gather_offsets(): lax.ppermute(flat, 'tile', [(i, i ^ 1) for i in range(count)])  3.74 us
  transfers between devices with their start and end apart: 7, of which 5 were waited for; matrix products, arithmetic and copies ran while one was open for 5% of the time, Pallas kernels for 1%

profile of v4, /device:TPU:1, one launch (start us, length us, event | category | flops | bytes accessed | tf_op | source)
XLA Modules:
  0.0 105.5 jit_solution(5853126765560474584)
XLA Ops:
  0.0 0.0 copy-start
  0.0 3.7 %collective-permute-start = (s32[2]{0:T(128)}, s32[2]{0:T(128)}, u32[]{:S(2)}, u32[]{:S(2)}) collective-permute-start(s32[2]{0:T(128)} %bitcast.16), channel_id=1, source_target_pairs={{0,1},{1,0},{2,3},{3,2},{4,5},{5,4},{6,7},{7,6},{8,9},{9,8},{10,11... | collective-permute-start | bytes 32 | tf_op jit(solution)/shard_map/ppermute | solution.py:32
  3.8 13.0 %all-to-all-start = ((bf16[256,8,256]{2,1,0:T(8,128)(2,1)}), bf16[256,8,256]{2,1,0:T(8,128)(2,1)S(1)}, u32[]{:S(2)}, u32[]{:S(2)}) async-start(bf16[256,8,256]{2,1,0:T(8,128)(2,1)} %bitcast.15), calls=%async_computation | async-start | bytes 2097152 | tf_op jit(solution)/shard_map/all_to_all | solution.py:156
  16.7 0.6 multiply_add_fusion
  17.4 0.3 select_convert_fusion.taps_ref
  17.7 0.8 dynamic-slice_bitcast_fusion
  18.5 0.1 broadcast_compare_fusion
  18.6 0.1 subtract_and_fusion
  18.6 0.1 add_multiply_fusion
  18.7 0.0 copy-done
  18.7 1.0 fusion.rowm_ref
  19.7 1.1 %rsqrt_multiply_fusion.weight_ref = f32[16,8,4096]{2,1,0:T(8,128)S(1)} fusion(f32[16,8]{1,0:T(8,128)S(1)} %add_multiply_fusion, f32[4096]{0:T(1024)} %multiply_add_fusion), kind=kLoop, calls=%fused_computation | loop fusion | flops 1048576 | bytes 2114048 | tf_op jit(solution)/shard_map/div | solution.py:180
  20.8 0.0 collective-permute-done
  20.8 0.8 pad_add_fusion.own_ref
  21.6 4.3 %collective-permute-start.1 = (s32[4]{0:T(128)S(1)}, s32[4]{0:T(128)S(1)}, u32[]{:S(2)}, u32[]{:S(2)}) collective-permute-start(s32[4]{0:T(128)S(1)} %pad_add_fusion.own_ref), channel_id=1, source_target_pairs={{2,0},{11,1},{4,2},{13,3},{6,4},{15,5},{8,6},{1,7},{10,8},{3,9},{1... | collective-permute-start | bytes 56 | tf_op jit(solution)/shard_map/ppermute | solution.py:35
  25.9 1.5 %collective-permute-start.2 = (s32[4]{0:T(128)S(1)}, s32[4]{0:T(128)S(1)}, u32[]{:S(2)}, u32[]{:S(2)}) collective-permute-start(s32[4]{0:T(128)S(1)} %pad_add_fusion.own_ref), channel_id=1, source_target_pairs={{4,0},{13,1},{6,2},{15,3},{8,4},{1,5},{10,6},{3,7},{12,8},{5,9},{1... | collective-permute-start | bytes 56 | tf_op jit(solution)/shard_map/ppermute | solution.py:35
  27.4 0.6 collective-permute-start.3
  28.1 6.0 %collective-permute-start.4 = (s32[4]{0:T(128)S(1)}, s32[4]{0:T(128)S(1)}, u32[]{:S(2)}, u32[]{:S(2)}) collective-permute-start(s32[4]{0:T(128)S(1)} %pad_add_fusion.own_ref), channel_id=1, source_target_pairs={{8,0},{1,1},{10,2},{3,3},{12,4},{5,5},{14,6},{7,7},{0,8},{9,9},{2,... | collective-permute-start | bytes 56 | tf_op jit(solution)/shard_map/ppermute | solution.py:35
  34.1 5.3 %collective-permute-done.1 = s32[4]{0:T(128)S(1)} collective-permute-done((s32[4]{0:T(128)S(1)}, s32[4]{0:T(128)S(1)}, u32[]{:S(2)}, u32[]{:S(2)}) %collective-permute-start.1) | collective-permute-done | bytes 48 | tf_op jit(solution)/shard_map/ppermute | solution.py:35
  39.4 0.0 collective-permute-done.2
  39.4 0.1 collective-permute-done.3
  39.5 4.9 %collective-permute-done.4 = s32[4]{0:T(128)S(1)} collective-permute-done((s32[4]{0:T(128)S(1)}, s32[4]{0:T(128)S(1)}, u32[]{:S(2)}, u32[]{:S(2)}) %collective-permute-start.4) | collective-permute-done | bytes 48 | tf_op jit(solution)/shard_map/ppermute | solution.py:35
  44.4 0.1 pad_add_fusion.1.mine_ref
  44.5 3.9 %all-to-all-done = bf16[256,8,256]{2,1,0:T(8,128)(2,1)S(1)} async-done(((bf16[256,8,256]{2,1,0:T(8,128)(2,1)}), bf16[256,8,256]{2,1,0:T(8,128)(2,1)S(1)}, u32[]{:S(2)}, u32[]{:S(2)}) %all-to-all-start) | async-done | bytes 1048608 | tf_op jit(solution)/shard_map/all_to_all | solution.py:156
  48.4 0.9 collective-permute-start.5
  49.3 0.8 shard_map.64.filtered
  50.1 2.2 %collective-permute-done.5.other_ref = s32[16]{0:T(128)S(1)} collective-permute-done((s32[16]{0:T(128)S(1)}, s32[16]{0:T(128)S(1)}, u32[]{:S(2)}, u32[]{:S(2)}) %collective-permute-start.5) | collective-permute-done | bytes 96 | tf_op jit(solution)/shard_map/ppermute | solution.py:166
  52.3 1.4 %shard_map.65 = bf16[16,32,1024]{2,1,0:T(8,128)(2,1)S(1)} custom-call(s32[16,32]{1,0:T(8,128)S(1)} %bitcast.14, s32[4]{0:T(128)S(1)} %pad_add_fusion.own_ref, s32[16]{0:T(128)S(1)} %pad_add_fusion.1.mine_ref, s32[16]{0:T(128)S(1)} %collective-permute-done.5.other_ref, f32[16,8,4096]{2,1,0:T(8,128)S(1)} %shard_map.64.filtered), custom_call_target="tpu_custom_call" | custom-call | tf_op jit(solution)/shard_map/pallas_call | solution.py:201
  53.7 30.0 %all_to_all.15.recv_ref = bf16[16,32,1024]{2,1,0:T(8,128)(2,1)S(1)} all-to-all(bf16[16,32,1024]{2,1,0:T(8,128)(2,1)S(1)} %shard_map.65), channel_id=1, replica_groups=mesh['proj'=16,'tile'=16] {'tile'}, dimensions={0} | all-to-all | bytes 2097152 | tf_op jit(solution)/shard_map/all_to_all | solution.py:210
  83.7 4.6 %shard_map.66 = bf16[16,8,2048]{2,1,0:T(8,128)(2,1)S(1)} custom-call(bf16[16,32,1024]{2,1,0:T(8,128)(2,1)S(1)} %all_to_all.15.recv_ref, bf16[2,128,256]{2,1,0:T(8,128)(2,1)S(1)} %copy-done.1, bf16[2,1,1024,2048]{3,2,1,0:T(8,128)(2,1)} %colw_ref.1), custom_call_target="tpu_custom_call" | custom-call | tf_op jit(solution)/shard_map/pallas_call | solution.py:213
  88.3 16.5 %all_to_all.16 = bf16[16,8,2048]{2,1,0:T(8,128)(2,1)S(1)} all-to-all(bf16[16,8,2048]{2,1,0:T(8,128)(2,1)S(1)} %shard_map.66), channel_id=1, replica_groups=mesh['proj'=16,'tile'=16] {'proj'}, dimensions={0} | all-to-all | bytes 1048576 | tf_op jit(solution)/shard_map/all_to_all | solution.py:231
  104.8 0.7 convert_reduce_fusion
  (8 shorter events, 0.0 us)
Async XLA Ops:
  0.0 18.7 %copy-start = (bf16[2,1,128,256]{3,2,1,0:T(8,128)(2,1)S(1)}, bf16[2,1,128,256]{3,2,1,0:T(8,128)(2,1)}, u32[]{:S(2)}) copy-start(bf16[2,1,128,256]{3,2,1,0:T(8,128)(2,1)} %param.7) | copy-start | bytes 393220
  0.0 17.7 %copy-start.2 = (s32[32,16]{0,1:T(8,128)S(1)}, s32[32,16]{0,1:T(8,128)}, u32[]{:S(2)}) copy-start(s32[32,16]{0,1:T(8,128)} %param.9) | copy-start | bytes 6148
  0.0 20.8 %collective-permute-start = (s32[2]{0:T(128)}, s32[2]{0:T(128)}, u32[]{:S(2)}, u32[]{:S(2)}) collective-permute-start(s32[2]{0:T(128)} %bitcast.16), channel_id=1, source_target_pairs={{0,1},{1,0},{2,3},{3,2},{4,5},{5,4},{6,7},{7,6},{8,9},{9,8},{10,11... | collective-permute-start | bytes 32 | tf_op jit(solution)/shard_map/ppermute | solution.py:32
  3.7 17.1 %copy-start.3 = (s32[2,1]{0,1:T(1,128)S(1)}, s32[2,1]{0,1:T(1,128)}, u32[]{:S(2)}) copy-start(s32[2,1]{0,1:T(1,128)} %param.11) | copy-start | bytes 28
  3.8 44.6 %all-to-all-start = ((bf16[256,8,256]{2,1,0:T(8,128)(2,1)}), bf16[256,8,256]{2,1,0:T(8,128)(2,1)S(1)}, u32[]{:S(2)}, u32[]{:S(2)}) async-start(bf16[256,8,256]{2,1,0:T(8,128)(2,1)} %bitcast.15), calls=%async_computation | async-start | bytes 2097152 | tf_op jit(solution)/shard_map/all_to_all | solution.py:156
  21.6 17.9 %collective-permute-start.1 = (s32[4]{0:T(128)S(1)}, s32[4]{0:T(128)S(1)}, u32[]{:S(2)}, u32[]{:S(2)}) collective-permute-start(s32[4]{0:T(128)S(1)} %pad_add_fusion.own_ref), channel_id=1, source_target_pairs={{2,0},{11,1},{4,2},{13,3},{6,4},{15,5},{8,6},{1,7},{10,8},{3,9},{1... | collective-permute-start | bytes 56 | tf_op jit(solution)/shard_map/ppermute | solution.py:35
  25.9 13.5 %collective-permute-start.2 = (s32[4]{0:T(128)S(1)}, s32[4]{0:T(128)S(1)}, u32[]{:S(2)}, u32[]{:S(2)}) collective-permute-start(s32[4]{0:T(128)S(1)} %pad_add_fusion.own_ref), channel_id=1, source_target_pairs={{4,0},{13,1},{6,2},{15,3},{8,4},{1,5},{10,6},{3,7},{12,8},{5,9},{1... | collective-permute-start | bytes 56 | tf_op jit(solution)/shard_map/ppermute | solution.py:35
  27.4 12.1 %collective-permute-start.3 = (s32[4]{0:T(128)S(1)}, s32[4]{0:T(128)S(1)}, u32[]{:S(2)}, u32[]{:S(2)}) collective-permute-start(s32[4]{0:T(128)S(1)} %pad_add_fusion.own_ref), channel_id=1, source_target_pairs={{6,0},{15,1},{8,2},{1,3},{10,4},{3,5},{12,6},{5,7},{14,8},{7,9},{0... | collective-permute-start | bytes 56 | tf_op jit(solution)/shard_map/ppermute | solution.py:35
  28.1 16.3 %collective-permute-start.4 = (s32[4]{0:T(128)S(1)}, s32[4]{0:T(128)S(1)}, u32[]{:S(2)}, u32[]{:S(2)}) collective-permute-start(s32[4]{0:T(128)S(1)} %pad_add_fusion.own_ref), channel_id=1, source_target_pairs={{8,0},{1,1},{10,2},{3,3},{12,4},{5,5},{14,6},{7,7},{0,8},{9,9},{2,... | collective-permute-start | bytes 56 | tf_op jit(solution)/shard_map/ppermute | solution.py:35
  48.4 3.9 %collective-permute-start.5 = (s32[16]{0:T(128)S(1)}, s32[16]{0:T(128)S(1)}, u32[]{:S(2)}, u32[]{:S(2)}) collective-permute-start(s32[16]{0:T(128)S(1)} %pad_add_fusion.1.mine_ref), channel_id=1, source_target_pairs={{0,1},{1,0},{2,3},{3,2},{4,5},{5,4},{6,7},{7,6},{8,9},{9,8},{10,11... | collective-permute-start | bytes 200 | tf_op jit(solution)/shard_map/ppermute | solution.py:166
  52.3 31.5 %copy-start.1 = (bf16[2,128,256]{2,1,0:T(8,128)(2,1)S(1)}, bf16[2,128,256]{2,1,0:T(8,128)(2,1)}, u32[]{:S(2)}) copy-start(bf16[2,128,256]{2,1,0:T(8,128)(2,1)} %fusion.rowm_ref) | copy-start | bytes 393220

commit v5 on v4

--- a/solution.py
+++ b/solution.py
@@ -37,7 +37,8 @@
         )
         for k in range(1, half + 1)
     ]
-    return held, jnp.concatenate(far)
+    mine = lax.optimization_barrier(jnp.concatenate(far))
+    return held, mine, lax.ppermute(mine, "tile", [(i, i ^ 1) for i in range(count)])
 
 
 def filter_rows(recv_ref, weight_ref, taps_ref, out_ref, padded):
@@ -104,7 +105,7 @@
         out_ref[tile] = jnp.concatenate(parts, axis=0).astype(BF16)
 
 
-def spread_sum(recv_ref, rowm_ref, colw_ref, out_ref, held, acc, total, sems):
+def spread_sum(recv_ref, rowm_ref, first_ref, colw_ref, out_ref, held, acc, total, sems):
     n_src, rows, win = recv_ref.shape
     local, parts, depth, _ = held.shape
     per = n_src // local
@@ -116,13 +117,16 @@
 
     for q in range(local):
         for k in range(parts):
-            fetch(q, k).start()
+            if q:
+                fetch(q, k).start()
     for q in range(local):
         for k in range(parts):
-            fetch(q, k).wait()
+            if q:
+                fetch(q, k).wait()
+            block = held[q, k] if q else first_ref[depth * k : depth * (k + 1)]
             window = recv_ref[per * q : per * (q + 1), :, depth * k : depth * (k + 1)]
             piece = jnp.dot(
-                window.reshape(per * rows, depth), held[q, k], preferred_element_type=jnp.float32
+                window.reshape(per * rows, depth), block, preferred_element_type=jnp.float32
             )
             if k:
                 piece = acc[...] + piece
@@ -161,9 +165,7 @@
         tiled=True,
     ).reshape(n_proj, n_tile, chunk, cols_dev)
 
-    own, mine = gather_offsets(col_offset, n_tile)
-    mine, recv = lax.optimization_barrier((mine, recv))
-    other = lax.ppermute(mine, "tile", [(i, i ^ 1) for i in range(n_tile)])
+    own, mine, other = gather_offsets(col_offset, n_tile)
     row_class = tile_me % classes
     first_proj = proj_me * local
     starts_all = lax.dynamic_slice(band_start, (first_proj, 0), (local, n_tile))
@@ -189,7 +191,9 @@
         "qsi,qik->qsk", row_weights[:, 0], pick.astype(BF16), preferred_element_type=jnp.float32
     ).astype(BF16)
 
-    other, row_moved = lax.optimization_barrier((other, row_moved))
+    parts = 2
+    first = col_weights[0, 0]
+    other, row_moved, first = lax.optimization_barrier((other, row_moved, first))
     filtered = pl.pallas_call(
         filter_rows,
         out_shape=jax.ShapeDtypeStruct((n_proj, chunk, total_cols), jnp.float32),
@@ -209,11 +213,11 @@
 
     windows = lax.all_to_all(cut, "tile", split_axis=0, concat_axis=0, tiled=True)
 
-    parts = 2
     part = pl.pallas_call(
         spread_sum,
         out_shape=jax.ShapeDtypeStruct((n_proj, slices // n_proj, vox), BF16),
         in_specs=[
+            pl.BlockSpec(memory_space=pltpu.VMEM),
             pl.BlockSpec(memory_space=pltpu.VMEM),
             pl.BlockSpec(memory_space=pltpu.VMEM),
             pl.BlockSpec(memory_space=pl.ANY),
@@ -226,7 +230,7 @@
             pltpu.SemaphoreType.DMA((local, parts)),
         ],
         compiler_params=pltpu.CompilerParams(vmem_limit_bytes=48 << 20),
-    )(windows, row_moved, col_weights)
+    )(windows, row_moved, first, col_weights)
 
     terms = lax.all_to_all(part, "proj", split_axis=0, concat_axis=0, tiled=True)
     return jnp.sum(terms.astype(jnp.float32), axis=0)

time: 106 us -> 104 us (0.981)
  waiting for transfers between devices: 16.4 us -> 7.56 us
  local copies, waits for them, and re-layouts: 0.78 us -> 6.02 us
  blocking collectives: 46.5 us -> 48.9 us
  starting transfers between devices: 30.2 us -> 32.3 us
  other arithmetic: 3.75 us -> 1.89 us
  Pallas kernels: 6.85 us -> 5.39 us
    ppermute x4, waiting for transfers between devices: 10.3 us -> 4.83 us  [gather_offsets(): lax.ppermute(held, 'tile', [((i + 2 * (k + half * (i % 2))) % count, i) f...]
    squeeze x0 -> x1, local copies, waits for them, and re-layouts: none -> 4.72 us  [body(): first = col_weights[0, 0]]
    all_to_all x1, waiting for transfers between devices: 3.89 us -> 0.01 us  [body(): lax.all_to_all(raw.reshape(n_proj * n_tile, chunk, cols_dev), ('proj', 't...]
    all_to_all x1, starting transfers between devices: 13 us -> 15.7 us  [body(): lax.all_to_all(raw.reshape(n_proj * n_tile, chunk, cols_dev), ('proj', 't...]
    all_to_all x1, blocking collectives: 16.5 us -> 18 us  [body(): lax.all_to_all(part, 'proj', split_axis=0, concat_axis=0, tiled=True)]
    pallas_call x1, Pallas kernels: 4.61 us -> 3.14 us  [body(): pl.pallas_call(spread_sum, out_shape=jax.ShapeDtypeStruct((n_proj, slices...]
  transfers between devices with their start and end apart: 7 -> 7, of which waited for: 5 -> 2; matrix products, arithmetic and copies ran while one was open for 5% -> 7% of each run, Pallas kernels for 1% -> 0%
where the time goes in v5:
time: 104 us; the launch traced here: 103 us
  blocking collectives  48.9 us (47%)
  starting transfers between devices  32.3 us (31%)
  waiting for transfers between devices  7.56 us (7%)
  local copies, waits for them, and re-layouts  6.02 us (6%)
  Pallas kernels  5.39 us (5%)
  other arithmetic  1.89 us (2%)
    all_to_all x1, blocking collectives, body(): lax.all_to_all(cut, 'tile', split_axis=0, concat_axis=0, tiled=True)  30.9 us
    all_to_all x1, blocking collectives, body(): lax.all_to_all(part, 'proj', split_axis=0, concat_axis=0, tiled=True)  18 us
    all_to_all x1, starting transfers between devices, body(): lax.all_to_all(raw.reshape(n_proj * n_tile, chunk, cols_dev), ('proj', 't...  15.7 us
    ppermute x4, starting transfers between devices, gather_offsets(): lax.ppermute(held, 'tile', [((i + 2 * (k + half * (i % 2))) % count, i) f...  12.5 us
    ppermute x4, waiting for transfers between devices, gather_offsets(): lax.ppermute(held, 'tile', [((i + 2 * (k + half * (i % 2))) % count, i) f...  4.83 us
    squeeze x1, local copies, waits for them, and re-layouts, body(): first = col_weights[0, 0]  4.72 us
    pallas_call x1, Pallas kernels, body(): pl.pallas_call(spread_sum, out_shape=jax.ShapeDtypeStruct((n_proj, slices...  3.14 us
    ppermute x1, starting transfers between devices, gather_offsets(): lax.ppermute(flat, 'tile', [(i, i ^ 1) for i in range(count)])  2.98 us
  transfers between devices with their start and end apart: 7, of which 2 were waited for; matrix products, arithmetic and copies ran while one was open for 7% of the time, Pallas kernels for 0%

profile of v5, /device:TPU:1, one launch (start us, length us, event | category | flops | bytes accessed | tf_op | source)
XLA Modules:
  0.0 103.2 jit_solution(2876534423249224697)
XLA Ops:
  0.0 0.0 copy-start
  0.0 15.7 %all-to-all-start = ((bf16[256,8,256]{2,1,0:T(8,128)(2,1)}), bf16[256,8,256]{2,1,0:T(8,128)(2,1)S(1)}, u32[]{:S(2)}, u32[]{:S(2)}) async-start(bf16[256,8,256]{2,1,0:T(8,128)(2,1)} %bitcast.17), calls=%async_computation | async-start | bytes 2097152 | tf_op jit(solution)/shard_map/all_to_all | solution.py:160
  15.7 3.0 %collective-permute-start = (s32[2]{0:T(128)S(1)}, s32[2]{0:T(128)S(1)}, u32[]{:S(2)}, u32[]{:S(2)}) collective-permute-start(s32[2]{0:T(128)S(1)} %bitcast.18), channel_id=1, source_target_pairs={{0,1},{1,0},{2,3},{3,2},{4,5},{5,4},{6,7},{7,6},{8,9},{9,8},{10,11... | collective-permute-start | bytes 32 | tf_op jit(solution)/shard_map/ppermute | solution.py:32
  18.7 0.8 dynamic-slice_bitcast_fusion
  19.5 0.1 subtract_and_fusion
  19.6 0.1 broadcast_compare_fusion
  19.6 0.1 add_multiply_fusion
  19.7 1.0 fusion.rowm_ref
  20.7 4.7 %slice_bitcast_fusion.first_ref = bf16[1024,2048]{1,0:T(8,128)(2,1)} fusion(bf16[2,1,1024,2048]{3,2,1,0:T(8,128)(2,1)} %colw_ref.1), kind=kLoop, calls=%fused_computation | loop fusion | bytes 8388608 | tf_op jit(solution)/shard_map/squeeze | solution.py:195
  25.4 0.5 rsqrt_multiply_fusion.weight_ref
  25.9 0.0 collective-permute-done
  25.9 0.1 pad_add_fusion.own_ref
  26.0 8.0 %collective-permute-start.4 = (s32[4]{0:T(128)S(1)}, s32[4]{0:T(128)S(1)}, u32[]{:S(2)}, u32[]{:S(2)}) collective-permute-start(s32[4]{0:T(128)S(1)} %pad_add_fusion.own_ref), channel_id=1, source_target_pairs={{8,0},{1,1},{10,2},{3,3},{12,4},{5,5},{14,6},{7,7},{0,8},{9,9},{2,... | collective-permute-start | bytes 56 | tf_op jit(solution)/shard_map/ppermute | solution.py:35
  34.1 0.1 collective-permute-start.3
  34.2 3.5 %collective-permute-start.2 = (s32[4]{0:T(128)S(1)}, s32[4]{0:T(128)S(1)}, u32[]{:S(2)}, u32[]{:S(2)}) collective-permute-start(s32[4]{0:T(128)S(1)} %pad_add_fusion.own_ref), channel_id=1, source_target_pairs={{4,0},{13,1},{6,2},{15,3},{8,4},{1,5},{10,6},{3,7},{12,8},{5,9},{1... | collective-permute-start | bytes 56 | tf_op jit(solution)/shard_map/ppermute | solution.py:35
  37.6 0.9 collective-permute-start.1
  38.5 4.8 %collective-permute-done.4 = s32[4]{0:T(128)S(1)} collective-permute-done((s32[4]{0:T(128)S(1)}, s32[4]{0:T(128)S(1)}, u32[]{:S(2)}, u32[]{:S(2)}) %collective-permute-start.4) | collective-permute-done | bytes 48 | tf_op jit(solution)/shard_map/ppermute | solution.py:35
  43.4 0.0 collective-permute-done.3
  43.4 0.0 collective-permute-done.2
  43.4 0.0 collective-permute-done.1
  43.4 0.1 pad_add_fusion.1.mine_ref
  43.5 1.2 %collective-permute-start.5 = (s32[16]{0:T(128)S(1)}, s32[16]{0:T(128)S(1)}, u32[]{:S(2)}, u32[]{:S(2)}) collective-permute-start(s32[16]{0:T(128)S(1)} %pad_add_fusion.1.mine_ref), channel_id=1, source_target_pairs={{0,1},{1,0},{2,3},{3,2},{4,5},{5,4},{6,7},{7,6},{8,9},{9,8},{10,11... | collective-permute-start | bytes 200 | tf_op jit(solution)/shard_map/ppermute | solution.py:41
  44.6 0.3 select_convert_fusion.taps_ref
  44.9 2.7 %collective-permute-done.5.other_ref = s32[16]{0:T(128)S(1)} collective-permute-done((s32[16]{0:T(128)S(1)}, s32[16]{0:T(128)S(1)}, u32[]{:S(2)}, u32[]{:S(2)}) %collective-permute-start.5) | collective-permute-done | bytes 96 | tf_op jit(solution)/shard_map/ppermute | solution.py:41
  47.7 0.5 copy-done.4
  48.2 0.0 all-to-all-done
  48.2 0.8 shard_map.64.filtered
  49.1 1.4 %shard_map.65 = bf16[16,32,1024]{2,1,0:T(8,128)(2,1)S(1)} custom-call(s32[16,32]{1,0:T(8,128)S(1)} %bitcast.16, s32[4]{0:T(128)S(1)} %pad_add_fusion.own_ref, s32[16]{0:T(128)S(1)} %pad_add_fusion.1.mine_ref, s32[16]{0:T(128)S(1)} %copy-done.5, f32[16,8,4096]{2,1,0:T(8,128)S(1)} %shard_map.64.filtered), custom_call_target="tpu_custom_call" | custom-call | tf_op jit(solution)/shard_map/pallas_call | solution.py:205
  50.5 30.9 %all_to_all.15.recv_ref = bf16[16,32,1024]{2,1,0:T(8,128)(2,1)S(1)} all-to-all(bf16[16,32,1024]{2,1,0:T(8,128)(2,1)S(1)} %shard_map.65), channel_id=1, replica_groups=mesh['proj'=16,'tile'=16] {'tile'}, dimensions={0} | all-to-all | bytes 2097152 | tf_op jit(solution)/shard_map/all_to_all | solution.py:214
  81.4 3.1 %shard_map.66 = bf16[16,8,2048]{2,1,0:T(8,128)(2,1)S(1)} custom-call(bf16[16,32,1024]{2,1,0:T(8,128)(2,1)S(1)} %all_to_all.15.recv_ref, bf16[2,128,256]{2,1,0:T(8,128)(2,1)S(1)} %copy-done.2, bf16[1024,2048]{1,0:T(8,128)(2,1)S(1)} %copy-done.1, bf16[2,1,1024,2048]{3,2,1,0:T(8,128)(2,1)} %colw_ref.1), custom_call_target="tpu_custom_call" | custom-call | tf_op jit(solution)/shard_map/pallas_call | solution.py:216
  84.5 18.0 %all_to_all.16 = bf16[16,8,2048]{2,1,0:T(8,128)(2,1)S(1)} all-to-all(bf16[16,8,2048]{2,1,0:T(8,128)(2,1)S(1)} %shard_map.66), channel_id=1, replica_groups=mesh['proj'=16,'tile'=16] {'proj'}, dimensions={0} | all-to-all | bytes 1048576 | tf_op jit(solution)/shard_map/all_to_all | solution.py:235
  102.5 0.7 convert_reduce_fusion
  (15 shorter events, 0.0 us)
Async XLA Ops:
  0.0 19.7 %copy-start = (bf16[2,1,128,256]{3,2,1,0:T(8,128)(2,1)S(1)}, bf16[2,1,128,256]{3,2,1,0:T(8,128)(2,1)}, u32[]{:S(2)}) copy-start(bf16[2,1,128,256]{3,2,1,0:T(8,128)(2,1)} %param.7) | copy-start | bytes 393220
  0.0 15.7 %copy-start.6 = (s32[2,1]{0,1:T(1,128)S(1)}, s32[2,1]{0,1:T(1,128)}, u32[]{:S(2)}) copy-start(s32[2,1]{0,1:T(1,128)} %param.11) | copy-start | bytes 28
  0.0 18.7 %copy-start.3 = (s32[32,16]{0,1:T(8,128)S(1)}, s32[32,16]{0,1:T(8,128)}, u32[]{:S(2)}) copy-start(s32[32,16]{0,1:T(8,128)} %param.9) | copy-start | bytes 6148
  0.0 48.2 %all-to-all-start = ((bf16[256,8,256]{2,1,0:T(8,128)(2,1)}), bf16[256,8,256]{2,1,0:T(8,128)(2,1)S(1)}, u32[]{:S(2)}, u32[]{:S(2)}) async-start(bf16[256,8,256]{2,1,0:T(8,128)(2,1)} %bitcast.17), calls=%async_computation | async-start | bytes 2097152 | tf_op jit(solution)/shard_map/all_to_all | solution.py:160
  15.7 10.2 %collective-permute-start = (s32[2]{0:T(128)S(1)}, s32[2]{0:T(128)S(1)}, u32[]{:S(2)}, u32[]{:S(2)}) collective-permute-start(s32[2]{0:T(128)S(1)} %bitcast.18), channel_id=1, source_target_pairs={{0,1},{1,0},{2,3},{3,2},{4,5},{5,4},{6,7},{7,6},{8,9},{9,8},{10,11... | collective-permute-start | bytes 32 | tf_op jit(solution)/shard_map/ppermute | solution.py:32
  26.0 17.4 %collective-permute-start.4 = (s32[4]{0:T(128)S(1)}, s32[4]{0:T(128)S(1)}, u32[]{:S(2)}, u32[]{:S(2)}) collective-permute-start(s32[4]{0:T(128)S(1)} %pad_add_fusion.own_ref), channel_id=1, source_target_pairs={{8,0},{1,1},{10,2},{3,3},{12,4},{5,5},{14,6},{7,7},{0,8},{9,9},{2,... | collective-permute-start | bytes 56 | tf_op jit(solution)/shard_map/ppermute | solution.py:35
  34.1 9.3 %collective-permute-start.3 = (s32[4]{0:T(128)S(1)}, s32[4]{0:T(128)S(1)}, u32[]{:S(2)}, u32[]{:S(2)}) collective-permute-start(s32[4]{0:T(128)S(1)} %pad_add_fusion.own_ref), channel_id=1, source_target_pairs={{6,0},{15,1},{8,2},{1,3},{10,4},{3,5},{12,6},{5,7},{14,8},{7,9},{0... | collective-permute-start | bytes 56 | tf_op jit(solution)/shard_map/ppermute | solution.py:35
  34.2 9.2 %collective-permute-start.2 = (s32[4]{0:T(128)S(1)}, s32[4]{0:T(128)S(1)}, u32[]{:S(2)}, u32[]{:S(2)}) collective-permute-start(s32[4]{0:T(128)S(1)} %pad_add_fusion.own_ref), channel_id=1, source_target_pairs={{4,0},{13,1},{6,2},{15,3},{8,4},{1,5},{10,6},{3,7},{12,8},{5,9},{1... | collective-permute-start | bytes 56 | tf_op jit(solution)/shard_map/ppermute | solution.py:35
  37.6 5.7 %collective-permute-start.1 = (s32[4]{0:T(128)S(1)}, s32[4]{0:T(128)S(1)}, u32[]{:S(2)}, u32[]{:S(2)}) collective-permute-start(s32[4]{0:T(128)S(1)} %pad_add_fusion.own_ref), channel_id=1, source_target_pairs={{2,0},{11,1},{4,2},{13,3},{6,4},{15,5},{8,6},{1,7},{10,8},{3,9},{1... | collective-permute-start | bytes 56 | tf_op jit(solution)/shard_map/ppermute | solution.py:35
  43.5 4.2 %collective-permute-start.5 = (s32[16]{0:T(128)S(1)}, s32[16]{0:T(128)S(1)}, u32[]{:S(2)}, u32[]{:S(2)}) collective-permute-start(s32[16]{0:T(128)S(1)} %pad_add_fusion.1.mine_ref), channel_id=1, source_target_pairs={{0,1},{1,0},{2,3},{3,2},{4,5},{5,4},{6,7},{7,6},{8,9},{9,8},{10,11... | collective-permute-start | bytes 200 | tf_op jit(solution)/shard_map/ppermute | solution.py:41
  47.7 0.5 copy-start.4
  48.2 0.8 copy-start.5
  49.0 32.3 %copy-start.1 = (bf16[1024,2048]{1,0:T(8,128)(2,1)S(1)}, bf16[1024,2048]{1,0:T(8,128)(2,1)}, u32[]{:S(2)}) copy-start(bf16[1024,2048]{1,0:T(8,128)(2,1)} %slice_bitcast_fusion.first_ref) | copy-start | bytes 12582916
  49.0 32.3 %copy-start.2 = (bf16[2,128,256]{2,1,0:T(8,128)(2,1)S(1)}, bf16[2,128,256]{2,1,0:T(8,128)(2,1)}, u32[]{:S(2)}) copy-start(bf16[2,128,256]{2,1,0:T(8,128)(2,1)} %fusion.rowm_ref) | copy-start | bytes 393220

commit v6 on v5

--- a/solution.py
+++ b/solution.py
@@ -27,18 +27,18 @@
 
 
 def gather_offsets(offsets, count):
-    half = count // 4
     flat = offsets.reshape(-1)
     held = jnp.concatenate([flat, lax.ppermute(flat, "tile", [(i, i ^ 1) for i in range(count)])])
     held = lax.optimization_barrier(held)
-    far = [
-        lax.ppermute(
-            held, "tile", [((i + 2 * (k + half * (i % 2))) % count, i) for i in range(count)]
-        )
-        for k in range(1, half + 1)
-    ]
-    mine = lax.optimization_barrier(jnp.concatenate(far))
-    return held, mine, lax.ppermute(mine, "tile", [(i, i ^ 1) for i in range(count)])
+
+    def fetch(values, turn):
+        return lax.ppermute(values, "tile", [((i + 2 * turn) % count, i) for i in range(count)])
+
+    turns = count // 2
+    early = [fetch(held, k) for k in range(1, 6)]
+    again, early[0] = lax.optimization_barrier((held, early[0]))
+    late = [fetch(again, k) for k in range(6, turns)]
+    return held, jnp.concatenate(early[:4]), early[4:] + late
 
 
 def filter_rows(recv_ref, weight_ref, taps_ref, out_ref, padded):
@@ -59,50 +59,45 @@
             taps_ref[...],
             preferred_element_type=jnp.float32,
         )
-        out_ref[:, :, lo : lo + width] = block.reshape(groups, chunk, width)
-
-
-def cut_windows(local, start_ref, own_ref, mine_ref, other_ref, filtered, out_ref):
-    groups, chunk, _ = filtered.shape
+        turns, high, _ = out_ref.shape
+        out_ref[:, :, lo : lo + width] = block.reshape(turns, high, width).astype(BF16)
+
+
+def cut_windows(local, chunk, start_ref, own_ref, next_ref, *refs):
+    *late_refs, filtered, out_ref = refs
+    turns = filtered.shape[0]
     n_tile, rows_out, win = out_ref.shape
-    periods = rows_out // chunk
     me = lax.axis_index("tile")
     classes = n_tile // local
     row_class = lax.rem(me, classes)
     which = lax.div(me, classes)
     proj = lax.axis_index("proj") * local + which
-    row_ids = lax.broadcasted_iota(jnp.int32, (chunk, win), 0)
-    span = chunk * classes
-    half = n_tile // 4
+    row_ids = lax.broadcasted_iota(jnp.int32, (rows_out, win), 0)
+    row_mod = (row_ids // chunk * classes + row_class) * chunk + row_ids % chunk
     me_y = lax.rem(me, 2)
 
     @pl.loop(0, n_tile)
     def _(k):
         turn = lax.div(k, 2)
         y = lax.rem(k, 2)
-        side = jnp.where(turn > half, 1, 0)
-        near = (jnp.bitwise_xor(y, me_y)) * local + which
-        block = jnp.where(turn > half, turn - half, jnp.maximum(turn, 1)) - 1
-        spot = (2 * block + jnp.bitwise_xor(y, side)) * local + which
-        far = jnp.where(side == me_y, mine_ref[spot], other_ref[spot])
-        col = pl.multiple_of(jnp.where(turn == 0, own_ref[near], far) * 128, 128)
+        spot = jnp.bitwise_xor(y, me_y) * local + which
+        block = own_ref[spot]
+        step = 2 * local
+        near = n_tile // 2 - 1 - len(late_refs)
+        ahead = jnp.clip(turn - 1, 0, near - 1)
+        block = jnp.where(turn > 0, next_ref[step * ahead + spot], block)
+        for at, late_ref in enumerate(late_refs):
+            block = jnp.where(turn == near + 1 + at, late_ref[spot], block)
+        col = pl.multiple_of(block * 128, 128)
         tile = lax.rem(me - me_y + 2 * turn, n_tile) + y
         start = start_ref[tile, proj]
-        parts = []
-        for m in range(periods):
-            delta = start - (span * m + chunk * row_class) + LMAX
-            low = lax.shift_right_logical(delta, 8)
-            rest = jnp.bitwise_and(delta, LMAX - 1)
-            first = jnp.clip(low - 1, 0, groups // periods - 1) * periods + m
-            second = jnp.clip(low, 0, groups // periods - 1) * periods + m
-            parts.append(
-                jnp.where(
-                    row_ids >= rest,
-                    filtered[first, :, pl.ds(col, win)],
-                    filtered[second, :, pl.ds(col, win)],
-                )
-            )
-        out_ref[tile] = jnp.concatenate(parts, axis=0).astype(BF16)
+        turn_at = lax.shift_right_logical(start, 8)
+        later = jnp.minimum(turn_at + 1, turns - 1)
+        out_ref[tile] = jnp.where(
+            row_mod >= jnp.bitwise_and(start, LMAX - 1),
+            filtered[turn_at, :, pl.ds(col, win)],
+            filtered[later, :, pl.ds(col, win)],
+        )
 
 
 def spread_sum(recv_ref, rowm_ref, first_ref, colw_ref, out_ref, held, acc, total, sems):
@@ -165,7 +160,7 @@
         tiled=True,
     ).reshape(n_proj, n_tile, chunk, cols_dev)
 
-    own, mine, other = gather_offsets(col_offset, n_tile)
+    own, ahead, late = gather_offsets(col_offset, n_tile)
     row_class = tile_me % classes
     first_proj = proj_me * local
     starts_all = lax.dynamic_slice(band_start, (first_proj, 0), (local, n_tile))
@@ -193,23 +188,23 @@
 
     parts = 2
     first = col_weights[0, 0]
-    other, row_moved, first = lax.optimization_barrier((other, row_moved, first))
+    own, row_moved, first = lax.optimization_barrier((own, row_moved, first))
     filtered = pl.pallas_call(
         filter_rows,
-        out_shape=jax.ShapeDtypeStruct((n_proj, chunk, total_cols), jnp.float32),
+        out_shape=jax.ShapeDtypeStruct((total_rows // LMAX, rows_out, total_cols), BF16),
         in_specs=[pl.BlockSpec(memory_space=pltpu.VMEM)] * 3,
         out_specs=pl.BlockSpec(memory_space=pltpu.VMEM),
         scratch_shapes=[pltpu.VMEM((n_proj * chunk, total_cols + 2 * TAP_REACH), BF16)],
         compiler_params=pltpu.CompilerParams(vmem_limit_bytes=24 << 20),
     )(recv, weight, tap_matrix(cols_dev))
     cut = pl.pallas_call(
-        functools.partial(cut_windows, local),
+        functools.partial(cut_windows, local, chunk),
         out_shape=jax.ShapeDtypeStruct((n_tile, rows_out, win), BF16),
-        in_specs=[pl.BlockSpec(memory_space=pltpu.SMEM)] * 4
+        in_specs=[pl.BlockSpec(memory_space=pltpu.SMEM)] * (3 + len(late))
         + [pl.BlockSpec(memory_space=pltpu.VMEM)],
         out_specs=pl.BlockSpec(memory_space=pltpu.VMEM),
         compiler_params=pltpu.CompilerParams(vmem_limit_bytes=24 << 20),
-    )(band_start.T, own, mine, other, filtered)
+    )(band_start.T, own, ahead, *late, filtered)
 
     windows = lax.all_to_all(cut, "tile", split_axis=0, concat_axis=0, tiled=True)
 

time: 104 us -> 103 us (level)
    ppermute x5 -> x7, waiting for transfers between devices: 7.55 us -> 4.3 us  [fetch(): lax.ppermute(values, 'tile', [((i + 2 * turn) % count, i) for i in range(...]
    all_to_all x1, waiting for transfers between devices: 0.01 us -> 2.77 us  [body(): lax.all_to_all(raw.reshape(n_proj * n_tile, chunk, cols_dev), ('proj', 't...]
    ppermute x5 -> x7, starting transfers between devices: 13.7 us -> 13.2 us  [fetch(): lax.ppermute(values, 'tile', [((i + 2 * turn) % count, i) for i in range(...]
  transfers between devices with their start and end apart: 7 -> 9, of which waited for: 2 -> 3; matrix products, arithmetic and copies ran while one was open for 7% -> 8% of each run, Pallas kernels for 0% -> 1%
where the time goes in v6:
time: 103 us
  blocking collectives  49.3 us (48%)
  starting transfers between devices  31.8 us (31%)
  waiting for transfers between devices  7.07 us (7%)
  local copies, waits for them, and re-layouts  5.51 us (5%)
  Pallas kernels  5.36 us (5%)
  other arithmetic  2.55 us (2%)
    all_to_all x1, blocking collectives, body(): lax.all_to_all(cut, 'tile', split_axis=0, concat_axis=0, tiled=True)  31.2 us
    all_to_all x1, blocking collectives, body(): lax.all_to_all(part, 'proj', split_axis=0, concat_axis=0, tiled=True)  18 us
    all_to_all x1, starting transfers between devices, body(): lax.all_to_all(raw.reshape(n_proj * n_tile, chunk, cols_dev), ('proj', 't...  15.7 us
    ppermute x7, starting transfers between devices, fetch(): lax.ppermute(values, 'tile', [((i + 2 * turn) % count, i) for i in range(...  13.2 us
    squeeze x1, local copies, waits for them, and re-layouts, body(): first = col_weights[0, 0]  4.72 us
    ppermute x7, waiting for transfers between devices, fetch(): lax.ppermute(values, 'tile', [((i + 2 * turn) % count, i) for i in range(...  4.3 us
    pallas_call x1, Pallas kernels, body(): pl.pallas_call(spread_sum, out_shape=jax.ShapeDtypeStruct((n_proj, slices...  3.14 us
    ppermute x1, starting transfers between devices, gather_offsets(): lax.ppermute(flat, 'tile', [(i, i ^ 1) for i in range(count)])  2.98 us
  transfers between devices with their start and end apart: 9, of which 3 were waited for; matrix products, arithmetic and copies ran while one was open for 8% of the time, Pallas kernels for 1%

profile of v6, /device:TPU:1, one launch (start us, length us, event | category | flops | bytes accessed | tf_op | source)
XLA Modules:
  0.0 102.7 jit_solution(2937342374671866438)
XLA Ops:
  0.0 15.7 %all-to-all-start = ((bf16[256,8,256]{2,1,0:T(8,128)(2,1)}), bf16[256,8,256]{2,1,0:T(8,128)(2,1)S(1)}, u32[]{:S(2)}, u32[]{:S(2)}) async-start(bf16[256,8,256]{2,1,0:T(8,128)(2,1)} %bitcast.17), calls=%async_computation | async-start | bytes 2097152 | tf_op jit(solution)/shard_map/all_to_all | solution.py:155
  15.7 3.0 %collective-permute-start = (s32[2]{0:T(128)S(1)}, s32[2]{0:T(128)}, u32[]{:S(2)}, u32[]{:S(2)}) collective-permute-start(s32[2]{0:T(128)S(1)} %bitcast.18), channel_id=1, source_target_pairs={{0,1},{1,0},{2,3},{3,2},{4,5},{5,4},{6,7},{7,6},{8,9},{9,8},{10,11... | collective-permute-start | bytes 32 | tf_op jit(solution)/shard_map/ppermute | solution.py:31
  18.7 0.3 select_convert_fusion.taps_ref
  19.1 0.8 dynamic-slice_bitcast_fusion
  19.8 0.1 subtract_and_fusion
  19.9 0.1 broadcast_compare_fusion
  20.0 0.1 add_multiply_fusion
  20.1 1.0 fusion.rowm_ref
  21.1 4.7 %slice_bitcast_fusion.first_ref = bf16[1024,2048]{1,0:T(8,128)(2,1)} fusion(bf16[2,1,1024,2048]{3,2,1,0:T(8,128)(2,1)} %colw_ref.1), kind=kLoop, calls=%fused_computation | loop fusion | bytes 8388608 | tf_op jit(solution)/shard_map/squeeze | solution.py:190
  25.8 0.5 rsqrt_multiply_fusion.weight_ref
  26.3 0.7 pad_add_fusion.own_ref
  27.0 3.8 %collective-permute-start.5 = (s32[4]{0:T(128)S(1)}, s32[4]{0:T(128)}, u32[]{:S(2)}, u32[]{:S(2)}) collective-permute-start(s32[4]{0:T(128)S(1)} %pad_add_fusion.own_ref), channel_id=1, source_target_pairs={{10,0},{11,1},{12,2},{13,3},{14,4},{15,5},{0,6},{1,7},{2,8},{3,9},... | collective-permute-start | bytes 56 | tf_op jit(solution)/shard_map/ppermute | solution.py:35
  30.8 3.5 %collective-permute-start.4 = (s32[4]{0:T(128)S(1)}, s32[4]{0:T(128)S(1)}, u32[]{:S(2)}, u32[]{:S(2)}) collective-permute-start(s32[4]{0:T(128)S(1)} %pad_add_fusion.own_ref), channel_id=1, source_target_pairs={{8,0},{9,1},{10,2},{11,3},{12,4},{13,5},{14,6},{15,7},{0,8},{1,9},... | collective-permute-start | bytes 56 | tf_op jit(solution)/shard_map/ppermute | solution.py:35
  34.3 3.4 %collective-permute-start.3 = (s32[4]{0:T(128)S(1)}, s32[4]{0:T(128)S(1)}, u32[]{:S(2)}, u32[]{:S(2)}) collective-permute-start(s32[4]{0:T(128)S(1)} %pad_add_fusion.own_ref), channel_id=1, source_target_pairs={{6,0},{7,1},{8,2},{9,3},{10,4},{11,5},{12,6},{13,7},{14,8},{15,9},... | collective-permute-start | bytes 56 | tf_op jit(solution)/shard_map/ppermute | solution.py:35
  37.7 0.0 collective-permute-start.2
  37.7 0.3 collective-permute-start.1
  37.9 2.4 %collective-permute-done.1 = s32[4]{0:T(128)S(1)} collective-permute-done((s32[4]{0:T(128)S(1)}, s32[4]{0:T(128)S(1)}, u32[]{:S(2)}, u32[]{:S(2)}) %collective-permute-start.1) | collective-permute-done | bytes 48 | tf_op jit(solution)/shard_map/ppermute | solution.py:35
  40.3 1.2 %collective-permute-start.7 = (s32[4]{0:T(128)S(1)}, s32[4]{0:T(128)}, u32[]{:S(2)}, u32[]{:S(2)}) collective-permute-start(s32[4]{0:T(128)S(1)} %pad_add_fusion.own_ref), channel_id=1, source_target_pairs={{14,0},{15,1},{0,2},{1,3},{2,4},{3,5},{4,6},{5,7},{6,8},{7,9},{8,1... | collective-permute-start | bytes 56 | tf_op jit(solution)/shard_map/ppermute | solution.py:35
  41.5 1.9 %collective-permute-done.4 = s32[4]{0:T(128)S(1)} collective-permute-done((s32[4]{0:T(128)S(1)}, s32[4]{0:T(128)S(1)}, u32[]{:S(2)}, u32[]{:S(2)}) %collective-permute-start.4) | collective-permute-done | bytes 48 | tf_op jit(solution)/shard_map/ppermute | solution.py:35
  43.4 1.1 %collective-permute-start.6 = (s32[4]{0:T(128)S(1)}, s32[4]{0:T(128)}, u32[]{:S(2)}, u32[]{:S(2)}) collective-permute-start(s32[4]{0:T(128)S(1)} %pad_add_fusion.own_ref), channel_id=1, source_target_pairs={{12,0},{13,1},{14,2},{15,3},{0,4},{1,5},{2,6},{3,7},{4,8},{5,9},{6... | collective-permute-start | bytes 56 | tf_op jit(solution)/shard_map/ppermute | solution.py:35
  44.5 0.0 collective-permute-done.3
  44.5 0.0 collective-permute-done.2
  44.5 0.1 pad_add_fusion.1.next_ref
  44.6 2.8 %all-to-all-done = bf16[256,8,256]{2,1,0:T(8,128)(2,1)S(1)} async-done(((bf16[256,8,256]{2,1,0:T(8,128)(2,1)}), bf16[256,8,256]{2,1,0:T(8,128)(2,1)S(1)}, u32[]{:S(2)}, u32[]{:S(2)}) %all-to-all-start) | async-done | bytes 1048608 | tf_op jit(solution)/shard_map/all_to_all | solution.py:155
  47.3 0.8 shard_map.64.refs_3_
  48.2 0.0 collective-permute-done.5.refs_0_
  48.2 0.0 collective-permute-done.6.refs_1_
  48.2 1.4 %shard_map.65 = bf16[16,32,1024]{2,1,0:T(8,128)(2,1)S(1)} custom-call(s32[16,32]{1,0:T(8,128)S(1)} %bitcast.16, s32[4]{0:T(128)S(1)} %pad_add_fusion.own_ref, s32[16]{0:T(128)S(1)} %pad_add_fusion.1.next_ref, s32[4]{0:T(128)} %collective-permute-done.5.refs_0_, s32[4]{0:T(128)} %collective-permute-done.6.refs_1_, s32[4]{0:T(128)} %collective-permute-done.7.refs_2_, ...), custom_call_target="tpu_custom_call" | custom-call | tf_op jit(solution)/shard_map/pallas_call | solution.py:200
  49.6 31.2 %all_to_all.15.recv_ref = bf16[16,32,1024]{2,1,0:T(8,128)(2,1)S(1)} all-to-all(bf16[16,32,1024]{2,1,0:T(8,128)(2,1)S(1)} %shard_map.65), channel_id=1, replica_groups=mesh['proj'=16,'tile'=16] {'tile'}, dimensions={0} | all-to-all | bytes 2097152 | tf_op jit(solution)/shard_map/all_to_all | solution.py:209
  80.9 3.1 %shard_map.66 = bf16[16,8,2048]{2,1,0:T(8,128)(2,1)S(1)} custom-call(bf16[16,32,1024]{2,1,0:T(8,128)(2,1)S(1)} %all_to_all.15.recv_ref, bf16[2,128,256]{2,1,0:T(8,128)(2,1)S(1)} %copy-done.2, bf16[1024,2048]{1,0:T(8,128)(2,1)S(1)} %copy-done.1, bf16[2,1,1024,2048]{3,2,1,0:T(8,128)(2,1)} %colw_ref.1), custom_call_target="tpu_custom_call" | custom-call | tf_op jit(solution)/shard_map/pallas_call | solution.py:211
  84.0 18.0 %all_to_all.16 = bf16[16,8,2048]{2,1,0:T(8,128)(2,1)S(1)} all-to-all(bf16[16,8,2048]{2,1,0:T(8,128)(2,1)S(1)} %shard_map.66), channel_id=1, replica_groups=mesh['proj'=16,'tile'=16] {'proj'}, dimensions={0} | all-to-all | bytes 1048576 | tf_op jit(solution)/shard_map/all_to_all | solution.py:230
  102.0 0.7 convert_reduce_fusion
  (15 shorter events, 0.0 us)
Async XLA Ops:
  0.0 20.1 %copy-start = (bf16[2,1,128,256]{3,2,1,0:T(8,128)(2,1)S(1)}, bf16[2,1,128,256]{3,2,1,0:T(8,128)(2,1)}, u32[]{:S(2)}) copy-start(bf16[2,1,128,256]{3,2,1,0:T(8,128)(2,1)} %param.7) | copy-start | bytes 393220
  0.0 15.7 %copy-start.4 = (s32[2,1]{0,1:T(1,128)S(1)}, s32[2,1]{0,1:T(1,128)}, u32[]{:S(2)}) copy-start(s32[2,1]{0,1:T(1,128)} %param.11) | copy-start | bytes 28
  0.0 19.0 %copy-start.3 = (s32[32,16]{0,1:T(8,128)S(1)}, s32[32,16]{0,1:T(8,128)}, u32[]{:S(2)}) copy-start(s32[32,16]{0,1:T(8,128)} %param.9) | copy-start | bytes 6148
  0.0 47.3 %all-to-all-start = ((bf16[256,8,256]{2,1,0:T(8,128)(2,1)}), bf16[256,8,256]{2,1,0:T(8,128)(2,1)S(1)}, u32[]{:S(2)}, u32[]{:S(2)}) async-start(bf16[256,8,256]{2,1,0:T(8,128)(2,1)} %bitcast.17), calls=%async_computation | async-start | bytes 2097152 | tf_op jit(solution)/shard_map/all_to_all | solution.py:155
  15.7 10.6 %collective-permute-start = (s32[2]{0:T(128)S(1)}, s32[2]{0:T(128)}, u32[]{:S(2)}, u32[]{:S(2)}) collective-permute-start(s32[2]{0:T(128)S(1)} %bitcast.18), channel_id=1, source_target_pairs={{0,1},{1,0},{2,3},{3,2},{4,5},{5,4},{6,7},{7,6},{8,9},{9,8},{10,11... | collective-permute-start | bytes 32 | tf_op jit(solution)/shard_map/ppermute | solution.py:31
  27.0 21.1 %collective-permute-start.5 = (s32[4]{0:T(128)S(1)}, s32[4]{0:T(128)}, u32[]{:S(2)}, u32[]{:S(2)}) collective-permute-start(s32[4]{0:T(128)S(1)} %pad_add_fusion.own_ref), channel_id=1, source_target_pairs={{10,0},{11,1},{12,2},{13,3},{14,4},{15,5},{0,6},{1,7},{2,8},{3,9},... | collective-permute-start | bytes 56 | tf_op jit(solution)/shard_map/ppermute | solution.py:35
  30.8 12.6 %collective-permute-start.4 = (s32[4]{0:T(128)S(1)}, s32[4]{0:T(128)S(1)}, u32[]{:S(2)}, u32[]{:S(2)}) collective-permute-start(s32[4]{0:T(128)S(1)} %pad_add_fusion.own_ref), channel_id=1, source_target_pairs={{8,0},{9,1},{10,2},{11,3},{12,4},{13,5},{14,6},{15,7},{0,8},{1,9},... | collective-permute-start | bytes 56 | tf_op jit(solution)/shard_map/ppermute | solution.py:35
  34.3 10.2 %collective-permute-start.3 = (s32[4]{0:T(128)S(1)}, s32[4]{0:T(128)S(1)}, u32[]{:S(2)}, u32[]{:S(2)}) collective-permute-start(s32[4]{0:T(128)S(1)} %pad_add_fusion.own_ref), channel_id=1, source_target_pairs={{6,0},{7,1},{8,2},{9,3},{10,4},{11,5},{12,6},{13,7},{14,8},{15,9},... | collective-permute-start | bytes 56 | tf_op jit(solution)/shard_map/ppermute | solution.py:35
  37.7 6.8 %collective-permute-start.2 = (s32[4]{0:T(128)S(1)}, s32[4]{0:T(128)S(1)}, u32[]{:S(2)}, u32[]{:S(2)}) collective-permute-start(s32[4]{0:T(128)S(1)} %pad_add_fusion.own_ref), channel_id=1, source_target_pairs={{4,0},{5,1},{6,2},{7,3},{8,4},{9,5},{10,6},{11,7},{12,8},{13,9},{1... | collective-permute-start | bytes 56 | tf_op jit(solution)/shard_map/ppermute | solution.py:35
  37.7 2.7 %collective-permute-start.1 = (s32[4]{0:T(128)S(1)}, s32[4]{0:T(128)S(1)}, u32[]{:S(2)}, u32[]{:S(2)}) collective-permute-start(s32[4]{0:T(128)S(1)} %pad_add_fusion.own_ref), channel_id=1, source_target_pairs={{2,0},{3,1},{4,2},{5,3},{6,4},{7,5},{8,6},{9,7},{10,8},{11,9},{12,... | collective-permute-start | bytes 56 | tf_op jit(solution)/shard_map/ppermute | solution.py:35
  40.3 7.8 %collective-permute-start.7 = (s32[4]{0:T(128)S(1)}, s32[4]{0:T(128)}, u32[]{:S(2)}, u32[]{:S(2)}) collective-permute-start(s32[4]{0:T(128)S(1)} %pad_add_fusion.own_ref), channel_id=1, source_target_pairs={{14,0},{15,1},{0,2},{1,3},{2,4},{3,5},{4,6},{5,7},{6,8},{7,9},{8,1... | collective-permute-start | bytes 56 | tf_op jit(solution)/shard_map/ppermute | solution.py:35
  43.4 4.8 %collective-permute-start.6 = (s32[4]{0:T(128)S(1)}, s32[4]{0:T(128)}, u32[]{:S(2)}, u32[]{:S(2)}) collective-permute-start(s32[4]{0:T(128)S(1)} %pad_add_fusion.own_ref), channel_id=1, source_target_pairs={{12,0},{13,1},{14,2},{15,3},{0,4},{1,5},{2,6},{3,7},{4,8},{5,9},{6... | collective-permute-start | bytes 56 | tf_op jit(solution)/shard_map/ppermute | solution.py:35
  47.3 33.5 %copy-start.2 = (bf16[2,128,256]{2,1,0:T(8,128)(2,1)S(1)}, bf16[2,128,256]{2,1,0:T(8,128)(2,1)}, u32[]{:S(2)}) copy-start(bf16[2,128,256]{2,1,0:T(8,128)(2,1)} %fusion.rowm_ref) | copy-start | bytes 393220
  48.2 32.7 %copy-start.1 = (bf16[1024,2048]{1,0:T(8,128)(2,1)S(1)}, bf16[1024,2048]{1,0:T(8,128)(2,1)}, u32[]{:S(2)}) copy-start(bf16[1024,2048]{1,0:T(8,128)(2,1)} %slice_bitcast_fusion.first_ref) | copy-start | bytes 12582916

commit v7 on v6

--- a/solution.py
+++ b/solution.py
@@ -64,7 +64,7 @@
 
 
 def cut_windows(local, chunk, start_ref, own_ref, next_ref, *refs):
-    *late_refs, filtered, out_ref = refs
+    *late_refs, filtered, out_ref, table = refs
     turns = filtered.shape[0]
     n_tile, rows_out, win = out_ref.shape
     me = lax.axis_index("tile")
@@ -76,19 +76,24 @@
     row_mod = (row_ids // chunk * classes + row_class) * chunk + row_ids % chunk
     me_y = lax.rem(me, 2)
 
-    @pl.loop(0, n_tile)
+    step = 2 * local
+    near = n_tile // 2 - 1 - len(late_refs)
+    for turn in range(n_tile // 2):
+        for y in range(2):
+            spot = jnp.bitwise_xor(y, me_y) * local + which
+            if turn == 0:
+                block = own_ref[spot]
+            elif turn <= near:
+                block = next_ref[step * (turn - 1) + spot]
+            else:
+                block = late_refs[turn - near - 1][spot]
+            table[2 * turn + y] = block
+
+    @pl.loop(0, n_tile, unroll=2)
     def _(k):
-        turn = lax.div(k, 2)
-        y = lax.rem(k, 2)
-        spot = jnp.bitwise_xor(y, me_y) * local + which
-        block = own_ref[spot]
-        step = 2 * local
-        near = n_tile // 2 - 1 - len(late_refs)
-        ahead = jnp.clip(turn - 1, 0, near - 1)
-        block = jnp.where(turn > 0, next_ref[step * ahead + spot], block)
-        for at, late_ref in enumerate(late_refs):
-            block = jnp.where(turn == near + 1 + at, late_ref[spot], block)
-        col = pl.multiple_of(block * 128, 128)
+        turn = lax.shift_right_logical(k, 1)
+        y = jnp.bitwise_and(k, 1)
+        col = pl.multiple_of(table[k] * 128, 128)
         tile = lax.rem(me - me_y + 2 * turn, n_tile) + y
         start = start_ref[tile, proj]
         turn_at = lax.shift_right_logical(start, 8)
@@ -203,6 +208,7 @@
         in_specs=[pl.BlockSpec(memory_space=pltpu.SMEM)] * (3 + len(late))
         + [pl.BlockSpec(memory_space=pltpu.VMEM)],
         out_specs=pl.BlockSpec(memory_space=pltpu.VMEM),
+        scratch_shapes=[pltpu.SMEM((n_tile,), jnp.int32)],
         compiler_params=pltpu.CompilerParams(vmem_limit_bytes=24 << 20),
     )(band_start.T, own, ahead, *late, filtered)
 

time: 103 us -> 103 us (level)
  no operation moved by 1% of the time
where the time goes in v7:
time: 103 us
  blocking collectives  49.4 us (48%)
  starting transfers between devices  31.8 us (31%)
  waiting for transfers between devices  7.07 us (7%)
  local copies, waits for them, and re-layouts  5.51 us (5%)
  Pallas kernels  5.18 us (5%)
  other arithmetic  2.55 us (2%)
    all_to_all x1, blocking collectives, body(): lax.all_to_all(cut, 'tile', split_axis=0, concat_axis=0, tiled=True)  31.4 us
    all_to_all x1, blocking collectives, body(): lax.all_to_all(part, 'proj', split_axis=0, concat_axis=0, tiled=True)  18 us
    all_to_all x1, starting transfers between devices, body(): lax.all_to_all(raw.reshape(n_proj * n_tile, chunk, cols_dev), ('proj', 't...  15.7 us
    ppermute x7, starting transfers between devices, fetch(): lax.ppermute(values, 'tile', [((i + 2 * turn) % count, i) for i in range(...  13.2 us
    squeeze x1, local copies, waits for them, and re-layouts, body(): first = col_weights[0, 0]  4.72 us
    ppermute x7, waiting for transfers between devices, fetch(): lax.ppermute(values, 'tile', [((i + 2 * turn) % count, i) for i in range(...  4.3 us
    pallas_call x1, Pallas kernels, body(): pl.pallas_call(spread_sum, out_shape=jax.ShapeDtypeStruct((n_proj, slices...  3.13 us
    ppermute x1, starting transfers between devices, gather_offsets(): lax.ppermute(flat, 'tile', [(i, i ^ 1) for i in range(count)])  2.98 us
  transfers between devices with their start and end apart: 9, of which 3 were waited for; matrix products, arithmetic and copies ran while one was open for 8% of the time, Pallas kernels for 1%

profile of v7, /device:TPU:1, one launch (start us, length us, event | category | flops | bytes accessed | tf_op | source)
XLA Modules:
  0.0 102.7 jit_solution(7844286647881016561)
XLA Ops:
  0.0 15.7 %all-to-all-start = ((bf16[256,8,256]{2,1,0:T(8,128)(2,1)}), bf16[256,8,256]{2,1,0:T(8,128)(2,1)S(1)}, u32[]{:S(2)}, u32[]{:S(2)}) async-start(bf16[256,8,256]{2,1,0:T(8,128)(2,1)} %bitcast.17), calls=%async_computation | async-start | bytes 2097152 | tf_op jit(solution)/shard_map/all_to_all | solution.py:160
  15.7 3.0 %collective-permute-start = (s32[2]{0:T(128)S(1)}, s32[2]{0:T(128)}, u32[]{:S(2)}, u32[]{:S(2)}) collective-permute-start(s32[2]{0:T(128)S(1)} %bitcast.18), channel_id=1, source_target_pairs={{0,1},{1,0},{2,3},{3,2},{4,5},{5,4},{6,7},{7,6},{8,9},{9,8},{10,11... | collective-permute-start | bytes 32 | tf_op jit(solution)/shard_map/ppermute | solution.py:31
  18.7 0.3 select_convert_fusion.taps_ref
  19.1 0.8 dynamic-slice_bitcast_fusion
  19.8 0.1 subtract_and_fusion
  19.9 0.1 broadcast_compare_fusion
  20.0 0.1 add_multiply_fusion
  20.1 1.0 fusion.rowm_ref
  21.1 4.7 %slice_bitcast_fusion.first_ref = bf16[1024,2048]{1,0:T(8,128)(2,1)} fusion(bf16[2,1,1024,2048]{3,2,1,0:T(8,128)(2,1)} %colw_ref.1), kind=kLoop, calls=%fused_computation | loop fusion | bytes 8388608 | tf_op jit(solution)/shard_map/squeeze | solution.py:195
  25.8 0.5 rsqrt_multiply_fusion.weight_ref
  26.3 0.7 pad_add_fusion.own_ref
  27.0 3.8 %collective-permute-start.5 = (s32[4]{0:T(128)S(1)}, s32[4]{0:T(128)}, u32[]{:S(2)}, u32[]{:S(2)}) collective-permute-start(s32[4]{0:T(128)S(1)} %pad_add_fusion.own_ref), channel_id=1, source_target_pairs={{10,0},{11,1},{12,2},{13,3},{14,4},{15,5},{0,6},{1,7},{2,8},{3,9},... | collective-permute-start | bytes 56 | tf_op jit(solution)/shard_map/ppermute | solution.py:35
  30.8 3.5 %collective-permute-start.4 = (s32[4]{0:T(128)S(1)}, s32[4]{0:T(128)S(1)}, u32[]{:S(2)}, u32[]{:S(2)}) collective-permute-start(s32[4]{0:T(128)S(1)} %pad_add_fusion.own_ref), channel_id=1, source_target_pairs={{8,0},{9,1},{10,2},{11,3},{12,4},{13,5},{14,6},{15,7},{0,8},{1,9},... | collective-permute-start | bytes 56 | tf_op jit(solution)/shard_map/ppermute | solution.py:35
  34.3 3.4 %collective-permute-start.3 = (s32[4]{0:T(128)S(1)}, s32[4]{0:T(128)S(1)}, u32[]{:S(2)}, u32[]{:S(2)}) collective-permute-start(s32[4]{0:T(128)S(1)} %pad_add_fusion.own_ref), channel_id=1, source_target_pairs={{6,0},{7,1},{8,2},{9,3},{10,4},{11,5},{12,6},{13,7},{14,8},{15,9},... | collective-permute-start | bytes 56 | tf_op jit(solution)/shard_map/ppermute | solution.py:35
  37.7 0.0 collective-permute-start.2
  37.7 0.3 collective-permute-start.1
  37.9 2.4 %collective-permute-done.1 = s32[4]{0:T(128)S(1)} collective-permute-done((s32[4]{0:T(128)S(1)}, s32[4]{0:T(128)S(1)}, u32[]{:S(2)}, u32[]{:S(2)}) %collective-permute-start.1) | collective-permute-done | bytes 48 | tf_op jit(solution)/shard_map/ppermute | solution.py:35
  40.3 1.2 %collective-permute-start.7 = (s32[4]{0:T(128)S(1)}, s32[4]{0:T(128)}, u32[]{:S(2)}, u32[]{:S(2)}) collective-permute-start(s32[4]{0:T(128)S(1)} %pad_add_fusion.own_ref), channel_id=1, source_target_pairs={{14,0},{15,1},{0,2},{1,3},{2,4},{3,5},{4,6},{5,7},{6,8},{7,9},{8,1... | collective-permute-start | bytes 56 | tf_op jit(solution)/shard_map/ppermute | solution.py:35
  41.5 1.9 %collective-permute-done.4 = s32[4]{0:T(128)S(1)} collective-permute-done((s32[4]{0:T(128)S(1)}, s32[4]{0:T(128)S(1)}, u32[]{:S(2)}, u32[]{:S(2)}) %collective-permute-start.4) | collective-permute-done | bytes 48 | tf_op jit(solution)/shard_map/ppermute | solution.py:35
  43.4 1.1 %collective-permute-start.6 = (s32[4]{0:T(128)S(1)}, s32[4]{0:T(128)}, u32[]{:S(2)}, u32[]{:S(2)}) collective-permute-start(s32[4]{0:T(128)S(1)} %pad_add_fusion.own_ref), channel_id=1, source_target_pairs={{12,0},{13,1},{14,2},{15,3},{0,4},{1,5},{2,6},{3,7},{4,8},{5,9},{6... | collective-permute-start | bytes 56 | tf_op jit(solution)/shard_map/ppermute | solution.py:35
  44.5 0.0 collective-permute-done.3
  44.5 0.0 collective-permute-done.2
  44.5 0.1 pad_add_fusion.1.next_ref
  44.6 2.8 %all-to-all-done = bf16[256,8,256]{2,1,0:T(8,128)(2,1)S(1)} async-done(((bf16[256,8,256]{2,1,0:T(8,128)(2,1)}), bf16[256,8,256]{2,1,0:T(8,128)(2,1)S(1)}, u32[]{:S(2)}, u32[]{:S(2)}) %all-to-all-start) | async-done | bytes 1048608 | tf_op jit(solution)/shard_map/all_to_all | solution.py:160
  47.3 0.8 shard_map.64.refs_3_
  48.2 0.0 collective-permute-done.5.refs_0_
  48.2 0.0 collective-permute-done.6.refs_1_
  48.2 1.2 %shard_map.65 = bf16[16,32,1024]{2,1,0:T(8,128)(2,1)S(1)} custom-call(s32[16,32]{1,0:T(8,128)S(1)} %bitcast.16, s32[4]{0:T(128)S(1)} %pad_add_fusion.own_ref, s32[16]{0:T(128)S(1)} %pad_add_fusion.1.next_ref, s32[4]{0:T(128)} %collective-permute-done.5.refs_0_, s32[4]{0:T(128)} %collective-permute-done.6.refs_1_, s32[4]{0:T(128)} %collective-permute-done.7.refs_2_, ...), custom_call_target="tpu_custom_call" | custom-call | tf_op jit(solution)/shard_map/pallas_call | solution.py:205
  49.4 31.4 %all_to_all.15.recv_ref = bf16[16,32,1024]{2,1,0:T(8,128)(2,1)S(1)} all-to-all(bf16[16,32,1024]{2,1,0:T(8,128)(2,1)S(1)} %shard_map.65), channel_id=1, replica_groups=mesh['proj'=16,'tile'=16] {'tile'}, dimensions={0} | all-to-all | bytes 2097152 | tf_op jit(solution)/shard_map/all_to_all | solution.py:215
  80.8 3.1 %shard_map.66 = bf16[16,8,2048]{2,1,0:T(8,128)(2,1)S(1)} custom-call(bf16[16,32,1024]{2,1,0:T(8,128)(2,1)S(1)} %all_to_all.15.recv_ref, bf16[2,128,256]{2,1,0:T(8,128)(2,1)S(1)} %copy-done.2, bf16[1024,2048]{1,0:T(8,128)(2,1)S(1)} %copy-done.1, bf16[2,1,1024,2048]{3,2,1,0:T(8,128)(2,1)} %colw_ref.1), custom_call_target="tpu_custom_call" | custom-call | tf_op jit(solution)/shard_map/pallas_call | solution.py:217
  84.0 18.0 %all_to_all.16 = bf16[16,8,2048]{2,1,0:T(8,128)(2,1)S(1)} all-to-all(bf16[16,8,2048]{2,1,0:T(8,128)(2,1)S(1)} %shard_map.66), channel_id=1, replica_groups=mesh['proj'=16,'tile'=16] {'proj'}, dimensions={0} | all-to-all | bytes 1048576 | tf_op jit(solution)/shard_map/all_to_all | solution.py:236
  102.0 0.7 convert_reduce_fusion
  (15 shorter events, 0.0 us)
Async XLA Ops:
  0.0 20.1 %copy-start = (bf16[2,1,128,256]{3,2,1,0:T(8,128)(2,1)S(1)}, bf16[2,1,128,256]{3,2,1,0:T(8,128)(2,1)}, u32[]{:S(2)}) copy-start(bf16[2,1,128,256]{3,2,1,0:T(8,128)(2,1)} %param.7) | copy-start | bytes 393220
  0.0 15.7 %copy-start.4 = (s32[2,1]{0,1:T(1,128)S(1)}, s32[2,1]{0,1:T(1,128)}, u32[]{:S(2)}) copy-start(s32[2,1]{0,1:T(1,128)} %param.11) | copy-start | bytes 28
  0.0 19.0 %copy-start.3 = (s32[32,16]{0,1:T(8,128)S(1)}, s32[32,16]{0,1:T(8,128)}, u32[]{:S(2)}) copy-start(s32[32,16]{0,1:T(8,128)} %param.9) | copy-start | bytes 6148
  0.0 47.3 %all-to-all-start = ((bf16[256,8,256]{2,1,0:T(8,128)(2,1)}), bf16[256,8,256]{2,1,0:T(8,128)(2,1)S(1)}, u32[]{:S(2)}, u32[]{:S(2)}) async-start(bf16[256,8,256]{2,1,0:T(8,128)(2,1)} %bitcast.17), calls=%async_computation | async-start | bytes 2097152 | tf_op jit(solution)/shard_map/all_to_all | solution.py:160
  15.7 10.6 %collective-permute-start = (s32[2]{0:T(128)S(1)}, s32[2]{0:T(128)}, u32[]{:S(2)}, u32[]{:S(2)}) collective-permute-start(s32[2]{0:T(128)S(1)} %bitcast.18), channel_id=1, source_target_pairs={{0,1},{1,0},{2,3},{3,2},{4,5},{5,4},{6,7},{7,6},{8,9},{9,8},{10,11... | collective-permute-start | bytes 32 | tf_op jit(solution)/shard_map/ppermute | solution.py:31
  27.0 21.1 %collective-permute-start.5 = (s32[4]{0:T(128)S(1)}, s32[4]{0:T(128)}, u32[]{:S(2)}, u32[]{:S(2)}) collective-permute-start(s32[4]{0:T(128)S(1)} %pad_add_fusion.own_ref), channel_id=1, source_target_pairs={{10,0},{11,1},{12,2},{13,3},{14,4},{15,5},{0,6},{1,7},{2,8},{3,9},... | collective-permute-start | bytes 56 | tf_op jit(solution)/shard_map/ppermute | solution.py:35
  30.8 12.6 %collective-permute-start.4 = (s32[4]{0:T(128)S(1)}, s32[4]{0:T(128)S(1)}, u32[]{:S(2)}, u32[]{:S(2)}) collective-permute-start(s32[4]{0:T(128)S(1)} %pad_add_fusion.own_ref), channel_id=1, source_target_pairs={{8,0},{9,1},{10,2},{11,3},{12,4},{13,5},{14,6},{15,7},{0,8},{1,9},... | collective-permute-start | bytes 56 | tf_op jit(solution)/shard_map/ppermute | solution.py:35
  34.3 10.2 %collective-permute-start.3 = (s32[4]{0:T(128)S(1)}, s32[4]{0:T(128)S(1)}, u32[]{:S(2)}, u32[]{:S(2)}) collective-permute-start(s32[4]{0:T(128)S(1)} %pad_add_fusion.own_ref), channel_id=1, source_target_pairs={{6,0},{7,1},{8,2},{9,3},{10,4},{11,5},{12,6},{13,7},{14,8},{15,9},... | collective-permute-start | bytes 56 | tf_op jit(solution)/shard_map/ppermute | solution.py:35
  37.7 6.8 %collective-permute-start.2 = (s32[4]{0:T(128)S(1)}, s32[4]{0:T(128)S(1)}, u32[]{:S(2)}, u32[]{:S(2)}) collective-permute-start(s32[4]{0:T(128)S(1)} %pad_add_fusion.own_ref), channel_id=1, source_target_pairs={{4,0},{5,1},{6,2},{7,3},{8,4},{9,5},{10,6},{11,7},{12,8},{13,9},{1... | collective-permute-start | bytes 56 | tf_op jit(solution)/shard_map/ppermute | solution.py:35
  37.7 2.7 %collective-permute-start.1 = (s32[4]{0:T(128)S(1)}, s32[4]{0:T(128)S(1)}, u32[]{:S(2)}, u32[]{:S(2)}) collective-permute-start(s32[4]{0:T(128)S(1)} %pad_add_fusion.own_ref), channel_id=1, source_target_pairs={{2,0},{3,1},{4,2},{5,3},{6,4},{7,5},{8,6},{9,7},{10,8},{11,9},{12,... | collective-permute-start | bytes 56 | tf_op jit(solution)/shard_map/ppermute | solution.py:35
  40.3 7.8 %collective-permute-start.7 = (s32[4]{0:T(128)S(1)}, s32[4]{0:T(128)}, u32[]{:S(2)}, u32[]{:S(2)}) collective-permute-start(s32[4]{0:T(128)S(1)} %pad_add_fusion.own_ref), channel_id=1, source_target_pairs={{14,0},{15,1},{0,2},{1,3},{2,4},{3,5},{4,6},{5,7},{6,8},{7,9},{8,1... | collective-permute-start | bytes 56 | tf_op jit(solution)/shard_map/ppermute | solution.py:35
  43.4 4.8 %collective-permute-start.6 = (s32[4]{0:T(128)S(1)}, s32[4]{0:T(128)}, u32[]{:S(2)}, u32[]{:S(2)}) collective-permute-start(s32[4]{0:T(128)S(1)} %pad_add_fusion.own_ref), channel_id=1, source_target_pairs={{12,0},{13,1},{14,2},{15,3},{0,4},{1,5},{2,6},{3,7},{4,8},{5,9},{6... | collective-permute-start | bytes 56 | tf_op jit(solution)/shard_map/ppermute | solution.py:35
  47.3 33.5 %copy-start.2 = (bf16[2,128,256]{2,1,0:T(8,128)(2,1)S(1)}, bf16[2,128,256]{2,1,0:T(8,128)(2,1)}, u32[]{:S(2)}) copy-start(bf16[2,128,256]{2,1,0:T(8,128)(2,1)} %fusion.rowm_ref) | copy-start | bytes 393220
  48.2 32.6 %copy-start.1 = (bf16[1024,2048]{1,0:T(8,128)(2,1)S(1)}, bf16[1024,2048]{1,0:T(8,128)(2,1)}, u32[]{:S(2)}) copy-start(bf16[1024,2048]{1,0:T(8,128)(2,1)} %slice_bitcast_fusion.first_ref) | copy-start | bytes 12582916

commit v8 on v5

--- a/solution.py
+++ b/solution.py
@@ -59,20 +59,20 @@
             taps_ref[...],
             preferred_element_type=jnp.float32,
         )
-        out_ref[:, :, lo : lo + width] = block.reshape(groups, chunk, width)
-
-
-def cut_windows(local, start_ref, own_ref, mine_ref, other_ref, filtered, out_ref):
-    groups, chunk, _ = filtered.shape
+        turns, high, _ = out_ref.shape
+        out_ref[:, :, lo : lo + width] = block.reshape(turns, high, width).astype(BF16)
+
+
+def cut_windows(local, chunk, start_ref, own_ref, mine_ref, other_ref, filtered, out_ref):
+    turns = filtered.shape[0]
     n_tile, rows_out, win = out_ref.shape
-    periods = rows_out // chunk
     me = lax.axis_index("tile")
     classes = n_tile // local
     row_class = lax.rem(me, classes)
     which = lax.div(me, classes)
     proj = lax.axis_index("proj") * local + which
-    row_ids = lax.broadcasted_iota(jnp.int32, (chunk, win), 0)
-    span = chunk * classes
+    row_ids = lax.broadcasted_iota(jnp.int32, (rows_out, win), 0)
+    row_mod = (row_ids // chunk * classes + row_class) * chunk + row_ids % chunk
     half = n_tile // 4
     me_y = lax.rem(me, 2)
 
@@ -88,21 +88,13 @@
         col = pl.multiple_of(jnp.where(turn == 0, own_ref[near], far) * 128, 128)
         tile = lax.rem(me - me_y + 2 * turn, n_tile) + y
         start = start_ref[tile, proj]
-        parts = []
-        for m in range(periods):
-            delta = start - (span * m + chunk * row_class) + LMAX
-            low = lax.shift_right_logical(delta, 8)
-            rest = jnp.bitwise_and(delta, LMAX - 1)
-            first = jnp.clip(low - 1, 0, groups // periods - 1) * periods + m
-            second = jnp.clip(low, 0, groups // periods - 1) * periods + m
-            parts.append(
-                jnp.where(
-                    row_ids >= rest,
-                    filtered[first, :, pl.ds(col, win)],
-                    filtered[second, :, pl.ds(col, win)],
-                )
-            )
-        out_ref[tile] = jnp.concatenate(parts, axis=0).astype(BF16)
+        turn_at = lax.shift_right_logical(start, 8)
+        later = jnp.minimum(turn_at + 1, turns - 1)
+        out_ref[tile] = jnp.where(
+            row_mod >= jnp.bitwise_and(start, LMAX - 1),
+            filtered[turn_at, :, pl.ds(col, win)],
+            filtered[later, :, pl.ds(col, win)],
+        )
 
 
 def spread_sum(recv_ref, rowm_ref, first_ref, colw_ref, out_ref, held, acc, total, sems):
@@ -196,14 +188,14 @@
     other, row_moved, first = lax.optimization_barrier((other, row_moved, first))
     filtered = pl.pallas_call(
         filter_rows,
-        out_shape=jax.ShapeDtypeStruct((n_proj, chunk, total_cols), jnp.float32),
+        out_shape=jax.ShapeDtypeStruct((total_rows // LMAX, rows_out, total_cols), BF16),
         in_specs=[pl.BlockSpec(memory_space=pltpu.VMEM)] * 3,
         out_specs=pl.BlockSpec(memory_space=pltpu.VMEM),
         scratch_shapes=[pltpu.VMEM((n_proj * chunk, total_cols + 2 * TAP_REACH), BF16)],
         compiler_params=pltpu.CompilerParams(vmem_limit_bytes=24 << 20),
     )(recv, weight, tap_matrix(cols_dev))
     cut = pl.pallas_call(
-        functools.partial(cut_windows, local),
+        functools.partial(cut_windows, local, chunk),
         out_shape=jax.ShapeDtypeStruct((n_tile, rows_out, win), BF16),
         in_specs=[pl.BlockSpec(memory_space=pltpu.SMEM)] * 4
         + [pl.BlockSpec(memory_space=pltpu.VMEM)],

time: 104 us -> 103 us (level)
  no operation moved by 1% of the time
where the time goes in v8:
time: 103 us
  blocking collectives  49 us (48%)
  starting transfers between devices  32.3 us (31%)
  waiting for transfers between devices  7.56 us (7%)
  local copies, waits for them, and re-layouts  6.02 us (6%)
  Pallas kernels  5.1 us (5%)
  other arithmetic  1.89 us (2%)
    all_to_all x1, blocking collectives, body(): lax.all_to_all(cut, 'tile', split_axis=0, concat_axis=0, tiled=True)  31 us
    all_to_all x1, blocking collectives, body(): lax.all_to_all(part, 'proj', split_axis=0, concat_axis=0, tiled=True)  18 us
    all_to_all x1, starting transfers between devices, body(): lax.all_to_all(raw.reshape(n_proj * n_tile, chunk, cols_dev), ('proj', 't...  15.7 us
    ppermute x4, starting transfers between devices, gather_offsets(): lax.ppermute(held, 'tile', [((i + 2 * (k + half * (i % 2))) % count, i) f...  12.5 us
    ppermute x4, waiting for transfers between devices, gather_offsets(): lax.ppermute(held, 'tile', [((i + 2 * (k + half * (i % 2))) % count, i) f...  4.83 us
    squeeze x1, local copies, waits for them, and re-layouts, body(): first = col_weights[0, 0]  4.72 us
    pallas_call x1, Pallas kernels, body(): pl.pallas_call(spread_sum, out_shape=jax.ShapeDtypeStruct((n_proj, slices...  3.13 us
    ppermute x1, starting transfers between devices, gather_offsets(): lax.ppermute(flat, 'tile', [(i, i ^ 1) for i in range(count)])  2.98 us
  transfers between devices with their start and end apart: 7, of which 2 were waited for; matrix products, arithmetic and copies ran while one was open for 7% of the time, Pallas kernels for 0%

profile of v8, /device:TPU:1, one launch (start us, length us, event | category | flops | bytes accessed | tf_op | source)
XLA Modules:
  0.0 103.1 jit_solution(14466837234087098571)
XLA Ops:
  0.0 0.0 copy-start
  0.0 15.7 %all-to-all-start = ((bf16[256,8,256]{2,1,0:T(8,128)(2,1)}), bf16[256,8,256]{2,1,0:T(8,128)(2,1)S(1)}, u32[]{:S(2)}, u32[]{:S(2)}) async-start(bf16[256,8,256]{2,1,0:T(8,128)(2,1)} %bitcast.17), calls=%async_computation | async-start | bytes 2097152 | tf_op jit(solution)/shard_map/all_to_all | solution.py:152
  15.7 3.0 %collective-permute-start = (s32[2]{0:T(128)S(1)}, s32[2]{0:T(128)S(1)}, u32[]{:S(2)}, u32[]{:S(2)}) collective-permute-start(s32[2]{0:T(128)S(1)} %bitcast.18), channel_id=1, source_target_pairs={{0,1},{1,0},{2,3},{3,2},{4,5},{5,4},{6,7},{7,6},{8,9},{9,8},{10,11... | collective-permute-start | bytes 32 | tf_op jit(solution)/shard_map/ppermute | solution.py:32
  18.7 0.8 dynamic-slice_bitcast_fusion
  19.5 0.1 subtract_and_fusion
  19.6 0.1 broadcast_compare_fusion
  19.6 0.1 add_multiply_fusion
  19.7 1.0 fusion.rowm_ref
  20.7 4.7 %slice_bitcast_fusion.first_ref = bf16[1024,2048]{1,0:T(8,128)(2,1)} fusion(bf16[2,1,1024,2048]{3,2,1,0:T(8,128)(2,1)} %colw_ref.1), kind=kLoop, calls=%fused_computation | loop fusion | bytes 8388608 | tf_op jit(solution)/shard_map/squeeze | solution.py:187
  25.4 0.5 rsqrt_multiply_fusion.weight_ref
  25.9 0.0 collective-permute-done
  25.9 0.1 pad_add_fusion.own_ref
  26.0 8.0 %collective-permute-start.4 = (s32[4]{0:T(128)S(1)}, s32[4]{0:T(128)S(1)}, u32[]{:S(2)}, u32[]{:S(2)}) collective-permute-start(s32[4]{0:T(128)S(1)} %pad_add_fusion.own_ref), channel_id=1, source_target_pairs={{8,0},{1,1},{10,2},{3,3},{12,4},{5,5},{14,6},{7,7},{0,8},{9,9},{2,... | collective-permute-start | bytes 56 | tf_op jit(solution)/shard_map/ppermute | solution.py:35
  34.1 0.1 collective-permute-start.3
  34.2 3.5 %collective-permute-start.2 = (s32[4]{0:T(128)S(1)}, s32[4]{0:T(128)S(1)}, u32[]{:S(2)}, u32[]{:S(2)}) collective-permute-start(s32[4]{0:T(128)S(1)} %pad_add_fusion.own_ref), channel_id=1, source_target_pairs={{4,0},{13,1},{6,2},{15,3},{8,4},{1,5},{10,6},{3,7},{12,8},{5,9},{1... | collective-permute-start | bytes 56 | tf_op jit(solution)/shard_map/ppermute | solution.py:35
  37.6 0.9 collective-permute-start.1
  38.5 4.8 %collective-permute-done.4 = s32[4]{0:T(128)S(1)} collective-permute-done((s32[4]{0:T(128)S(1)}, s32[4]{0:T(128)S(1)}, u32[]{:S(2)}, u32[]{:S(2)}) %collective-permute-start.4) | collective-permute-done | bytes 48 | tf_op jit(solution)/shard_map/ppermute | solution.py:35
  43.4 0.0 collective-permute-done.3
  43.4 0.0 collective-permute-done.2
  43.4 0.0 collective-permute-done.1
  43.4 0.1 pad_add_fusion.1.mine_ref
  43.5 1.2 %collective-permute-start.5 = (s32[16]{0:T(128)S(1)}, s32[16]{0:T(128)S(1)}, u32[]{:S(2)}, u32[]{:S(2)}) collective-permute-start(s32[16]{0:T(128)S(1)} %pad_add_fusion.1.mine_ref), channel_id=1, source_target_pairs={{0,1},{1,0},{2,3},{3,2},{4,5},{5,4},{6,7},{7,6},{8,9},{9,8},{10,11... | collective-permute-start | bytes 200 | tf_op jit(solution)/shard_map/ppermute | solution.py:41
  44.6 0.3 select_convert_fusion.taps_ref
  44.9 2.7 %collective-permute-done.5.other_ref = s32[16]{0:T(128)S(1)} collective-permute-done((s32[16]{0:T(128)S(1)}, s32[16]{0:T(128)S(1)}, u32[]{:S(2)}, u32[]{:S(2)}) %collective-permute-start.5) | collective-permute-done | bytes 96 | tf_op jit(solution)/shard_map/ppermute | solution.py:41
  47.7 0.5 copy-done.4
  48.2 0.0 all-to-all-done
  48.2 0.8 shard_map.64.filtered
  49.1 1.1 %shard_map.65 = bf16[16,32,1024]{2,1,0:T(8,128)(2,1)S(1)} custom-call(s32[16,32]{1,0:T(8,128)S(1)} %bitcast.16, s32[4]{0:T(128)S(1)} %pad_add_fusion.own_ref, s32[16]{0:T(128)S(1)} %pad_add_fusion.1.mine_ref, s32[16]{0:T(128)S(1)} %copy-done.5, bf16[4,32,4096]{2,1,0:T(8,128)(2,1)S(1)} %shard_map.64.filtered), custom_call_target="tpu_custom_call" | custom-call | tf_op jit(solution)/shard_map/pallas_call | solution.py:197
  50.2 31.0 %all_to_all.15.recv_ref = bf16[16,32,1024]{2,1,0:T(8,128)(2,1)S(1)} all-to-all(bf16[16,32,1024]{2,1,0:T(8,128)(2,1)S(1)} %shard_map.65), channel_id=1, replica_groups=mesh['proj'=16,'tile'=16] {'tile'}, dimensions={0} | all-to-all | bytes 2097152 | tf_op jit(solution)/shard_map/all_to_all | solution.py:206
  81.2 3.1 %shard_map.66 = bf16[16,8,2048]{2,1,0:T(8,128)(2,1)S(1)} custom-call(bf16[16,32,1024]{2,1,0:T(8,128)(2,1)S(1)} %all_to_all.15.recv_ref, bf16[2,128,256]{2,1,0:T(8,128)(2,1)S(1)} %copy-done.2, bf16[1024,2048]{1,0:T(8,128)(2,1)S(1)} %copy-done.1, bf16[2,1,1024,2048]{3,2,1,0:T(8,128)(2,1)} %colw_ref.1), custom_call_target="tpu_custom_call" | custom-call | tf_op jit(solution)/shard_map/pallas_call | solution.py:208
  84.3 18.0 %all_to_all.16 = bf16[16,8,2048]{2,1,0:T(8,128)(2,1)S(1)} all-to-all(bf16[16,8,2048]{2,1,0:T(8,128)(2,1)S(1)} %shard_map.66), channel_id=1, replica_groups=mesh['proj'=16,'tile'=16] {'proj'}, dimensions={0} | all-to-all | bytes 1048576 | tf_op jit(solution)/shard_map/all_to_all | solution.py:227
  102.4 0.7 convert_reduce_fusion
  (15 shorter events, 0.0 us)
Async XLA Ops:
  0.0 19.7 %copy-start = (bf16[2,1,128,256]{3,2,1,0:T(8,128)(2,1)S(1)}, bf16[2,1,128,256]{3,2,1,0:T(8,128)(2,1)}, u32[]{:S(2)}) copy-start(bf16[2,1,128,256]{3,2,1,0:T(8,128)(2,1)} %param.7) | copy-start | bytes 393220
  0.0 15.7 %copy-start.6 = (s32[2,1]{0,1:T(1,128)S(1)}, s32[2,1]{0,1:T(1,128)}, u32[]{:S(2)}) copy-start(s32[2,1]{0,1:T(1,128)} %param.11) | copy-start | bytes 28
  0.0 18.7 %copy-start.3 = (s32[32,16]{0,1:T(8,128)S(1)}, s32[32,16]{0,1:T(8,128)}, u32[]{:S(2)}) copy-start(s32[32,16]{0,1:T(8,128)} %param.9) | copy-start | bytes 6148
  0.0 48.2 %all-to-all-start = ((bf16[256,8,256]{2,1,0:T(8,128)(2,1)}), bf16[256,8,256]{2,1,0:T(8,128)(2,1)S(1)}, u32[]{:S(2)}, u32[]{:S(2)}) async-start(bf16[256,8,256]{2,1,0:T(8,128)(2,1)} %bitcast.17), calls=%async_computation | async-start | bytes 2097152 | tf_op jit(solution)/shard_map/all_to_all | solution.py:152
  15.7 10.2 %collective-permute-start = (s32[2]{0:T(128)S(1)}, s32[2]{0:T(128)S(1)}, u32[]{:S(2)}, u32[]{:S(2)}) collective-permute-start(s32[2]{0:T(128)S(1)} %bitcast.18), channel_id=1, source_target_pairs={{0,1},{1,0},{2,3},{3,2},{4,5},{5,4},{6,7},{7,6},{8,9},{9,8},{10,11... | collective-permute-start | bytes 32 | tf_op jit(solution)/shard_map/ppermute | solution.py:32
  26.0 17.4 %collective-permute-start.4 = (s32[4]{0:T(128)S(1)}, s32[4]{0:T(128)S(1)}, u32[]{:S(2)}, u32[]{:S(2)}) collective-permute-start(s32[4]{0:T(128)S(1)} %pad_add_fusion.own_ref), channel_id=1, source_target_pairs={{8,0},{1,1},{10,2},{3,3},{12,4},{5,5},{14,6},{7,7},{0,8},{9,9},{2,... | collective-permute-start | bytes 56 | tf_op jit(solution)/shard_map/ppermute | solution.py:35
  34.1 9.3 %collective-permute-start.3 = (s32[4]{0:T(128)S(1)}, s32[4]{0:T(128)S(1)}, u32[]{:S(2)}, u32[]{:S(2)}) collective-permute-start(s32[4]{0:T(128)S(1)} %pad_add_fusion.own_ref), channel_id=1, source_target_pairs={{6,0},{15,1},{8,2},{1,3},{10,4},{3,5},{12,6},{5,7},{14,8},{7,9},{0... | collective-permute-start | bytes 56 | tf_op jit(solution)/shard_map/ppermute | solution.py:35
  34.2 9.2 %collective-permute-start.2 = (s32[4]{0:T(128)S(1)}, s32[4]{0:T(128)S(1)}, u32[]{:S(2)}, u32[]{:S(2)}) collective-permute-start(s32[4]{0:T(128)S(1)} %pad_add_fusion.own_ref), channel_id=1, source_target_pairs={{4,0},{13,1},{6,2},{15,3},{8,4},{1,5},{10,6},{3,7},{12,8},{5,9},{1... | collective-permute-start | bytes 56 | tf_op jit(solution)/shard_map/ppermute | solution.py:35
  37.6 5.7 %collective-permute-start.1 = (s32[4]{0:T(128)S(1)}, s32[4]{0:T(128)S(1)}, u32[]{:S(2)}, u32[]{:S(2)}) collective-permute-start(s32[4]{0:T(128)S(1)} %pad_add_fusion.own_ref), channel_id=1, source_target_pairs={{2,0},{11,1},{4,2},{13,3},{6,4},{15,5},{8,6},{1,7},{10,8},{3,9},{1... | collective-permute-start | bytes 56 | tf_op jit(solution)/shard_map/ppermute | solution.py:35
  43.5 4.2 %collective-permute-start.5 = (s32[16]{0:T(128)S(1)}, s32[16]{0:T(128)S(1)}, u32[]{:S(2)}, u32[]{:S(2)}) collective-permute-start(s32[16]{0:T(128)S(1)} %pad_add_fusion.1.mine_ref), channel_id=1, source_target_pairs={{0,1},{1,0},{2,3},{3,2},{4,5},{5,4},{6,7},{7,6},{8,9},{9,8},{10,11... | collective-permute-start | bytes 200 | tf_op jit(solution)/shard_map/ppermute | solution.py:41
  47.7 0.5 copy-start.4
  48.2 0.8 copy-start.5
  48.2 33.0 %copy-start.2 = (bf16[2,128,256]{2,1,0:T(8,128)(2,1)S(1)}, bf16[2,128,256]{2,1,0:T(8,128)(2,1)}, u32[]{:S(2)}) copy-start(bf16[2,128,256]{2,1,0:T(8,128)(2,1)} %fusion.rowm_ref) | copy-start | bytes 393220
  49.0 32.1 %copy-start.1 = (bf16[1024,2048]{1,0:T(8,128)(2,1)S(1)}, bf16[1024,2048]{1,0:T(8,128)(2,1)}, u32[]{:S(2)}) copy-start(bf16[1024,2048]{1,0:T(8,128)(2,1)} %slice_bitcast_fusion.first_ref) | copy-start | bytes 12582916
